TPU v7x, 512 devices: a whole 4x4x16 slice. The times are simulated.
512 devices in a mesh: req: 32 (over z, core), head: 4 (over y), row: 4 (over x).
Axes of the slice: x: 4, y: 4, z: 16, core: 2. Of those that a mesh axis runs over, the one named last changes fastest.
Arguments:
- incoming_activations: bfloat16 [512, 4, 2048], P(('req', 'head'), None, 'row'), may hold values from -6 to 6
- genuine_symbol_number: int32 [512], replicated, may hold values from 1 to 4, as said below
- caller_sheet_slot: int32 [512], replicated, may hold values from 0 to 511, as said below
- memory_sheets: float32 [512, 32, 4096], P('req', 'head', 'row'), may hold values from -4 to 4
- prior_activation_sheets: float32 [512, 2048], P('req', 'row'), may hold values from -6 to 6
- blend_fractions: float32 [5, 2048], P(None, 'row'), may hold values from 0 to 1
- first_projectors: bfloat16 [3, 2048, 2048], P(None, 'row', 'head'), may hold values from -0.125 to 0.125
- fading_narrow_projector: bfloat16 [2048, 96], P('row'), may hold values from -0.125 to 0.125
- fading_widen_projector: bfloat16 [96, 2048], P(None, 'head'), may hold values from -0.625 to 0.625
- fading_offset: float32 [2048], P('head'), may hold values from -5 to 1
- context_step_narrowing: bfloat16 [2048, 96], P('row'), may hold values from -0.125 to 0.125
- context_step_widening: bfloat16 [96, 2048], P(None, 'head'), may hold values from -0.625 to 0.625
- context_step_offset: float32 [2048], P('head'), may hold values from -2 to 2
- erasure_address_gain: float32 [2048], P('head'), may hold values from 0.25 to 2
- address_correction: float32 [2048], P('head'), may hold values from 0 to 1.5
- reward_coefficients: float32 [32, 64], P('head'), may hold values from -0.6 to 0.6
- groupwise_gain: float32 [32, 64], P('head', 'row'), may hold values from 0.5 to 1.5
- final_projector: bfloat16 [32, 64, 2048], P('head', 'row'), may hold values from -0.125 to 0.125
Outputs:
- mixed: bfloat16 [512, 4, 2048], P(('req', 'head'), None, 'row')
- new_state: float32 [512, 32, 4096], P('req', 'head', 'row')
- new_shift: float32 [512, 2048], P('req', 'row')
Inputs may be any that keep to these rules, and one draw needn't show every extreme that they name: `genuine_symbol_number`: every request has 1 or 4 valid tokens; the share with 4 differs between indices of req. `caller_sheet_slot`: a permutation; the pages of index i of req are i * 16 to (i + 1) * 16 - 1; for any two indices of req, between 0 and 1 of the first one's requests have their pages on the second.
All inputs are finite; a program needn't handle non-finite values.
Results may differ from a plain program's by a relative error of at most 0.02.
Values may be sent and summed in bfloat16 or wider, within the bound.
No kernel may reach another device: no remote copies, remote signals or barrier semaphores. Data moves between devices by JAX's collectives and lax.ppermute only.
A program may use at most 64 MiB of HBM per device.

v0:
```python
import jax
import jax.numpy as jnp
from jax import lax
from jax.sharding import PartitionSpec as P

CHANNEL_SPAN = 64
TS = 4
REQ_DEV = 16


def project(token_rows, weight):
    return jnp.einsum("rtd,de->rte", token_rows, weight, preferred_element_type=jnp.float32)


def invert_slots(slots, total_slots):
    width_now = slots.shape[0]
    matches = slots[None, :] == jnp.arange(total_slots, dtype=jnp.int32)[:, None]
    anchor = jnp.sum(jnp.where(matches, jnp.arange(width_now, dtype=jnp.int32)[None, :], 0), axis=1)
    return anchor + jnp.where(jnp.any(matches, axis=1), 0, width_now)


def pick_rows(values, positions):
    padded = jnp.concatenate([values, jnp.zeros_like(values[:1])], axis=0)
    return jnp.take(padded, positions, axis=0)


def slot_tables(genuine_symbol_number, caller_sheet_slot, device, groups, capacity):
    owners = caller_sheet_slot // REQ_DEV
    blocks = owners.reshape(groups, REQ_DEV)
    same_owner = (blocks[:, :, None] == blocks[:, None, :]).astype(jnp.int32)
    positions = jnp.arange(REQ_DEV, dtype=jnp.int32)
    earlier = (positions[None, :] < positions[:, None]).astype(jnp.int32)
    rank_all = jnp.sum(same_owner * earlier[None], axis=2).reshape(-1)
    start_row = device * REQ_DEV
    my_owner = lax.dynamic_slice_in_dim(owners, start_row, REQ_DEV)
    my_rank = lax.dynamic_slice_in_dim(rank_all, start_row, REQ_DEV)
    request_slots = my_owner * capacity + my_rank
    request_valid = lax.dynamic_slice_in_dim(genuine_symbol_number, start_row, REQ_DEV)
    all_requests = jnp.arange(caller_sheet_slot.shape[0], dtype=jnp.int32)
    holder = caller_sheet_slot[None, :] == (start_row + positions)[:, None]
    requester = jnp.sum(jnp.where(holder, all_requests[None, :], 0), axis=1)
    page_slots = requester // REQ_DEV * capacity + jnp.take(rank_all, requester)
    page_valid = jnp.take(genuine_symbol_number, requester)
    return (request_slots, request_valid, page_slots, page_valid)


def time_mix(
    token_rows,
    live_count,
    state_now,
    shift_row,
    blend_fractions,
    first_projectors,
    fading_narrow_projector,
    fading_widen_projector,
    fading_offset,
    context_step_narrowing,
    context_step_widening,
    context_step_offset,
    erasure_address_gain,
    address_correction,
    reward_coefficients,
    groupwise_gain,
):
    requests = token_rows.shape[0]
    local_heads = groupwise_gain.shape[0]
    value_rows = groupwise_gain.shape[1]
    row_count = lax.axis_size("row")
    current = token_rows.astype(jnp.float32)
    before = jnp.concatenate([shift_row[:, None, :], current[:, :-1, :]], axis=1)
    towards = before - current
    mixed_in = [
        (current + towards * blend_fractions[branch]).astype(jnp.bfloat16) for branch in range(5)
    ]
    recept_part = project(mixed_in[0], first_projectors[0])
    key_part = project(mixed_in[2], first_projectors[1])
    value_part = project(mixed_in[3], first_projectors[2])
    decay_part = project(mixed_in[1], fading_narrow_projector)
    learn_part = project(mixed_in[4], context_step_narrowing)
    acceptance_query, key_vec, decay_sum, learn_sum = lax.psum(
        (recept_part, key_part, decay_part, learn_part), "row"
    )
    split_values = value_part.reshape(requests, TS, local_heads, row_count, value_rows)
    payload_entries = lax.psum_scatter(
        split_values, "row", scatter_dimension=3, tiled=True
    ).reshape(requests, TS, local_heads, value_rows)
    heads_shape = (requests, TS, local_heads, CHANNEL_SPAN)
    decay_low = jnp.tanh(decay_sum).astype(jnp.bfloat16)
    log_rate = -jax.nn.softplus(-(fading_offset + project(decay_low, fading_widen_projector))) - 0.5
    decay_rate = jnp.exp(-jnp.exp(log_rate)).reshape(heads_shape)
    learn_flat = jax.nn.sigmoid(
        context_step_offset + project(learn_sum.astype(jnp.bfloat16), context_step_widening)
    )
    learn_rate = learn_flat.reshape(heads_shape)
    scaled = (key_vec * erasure_address_gain).reshape(heads_shape)
    key_dir = scaled / jnp.sqrt(jnp.sum(scaled * scaled, axis=-1, keepdims=True) + 1e-06)
    address_corrected = (key_vec * (1.0 + (learn_flat - 1.0) * address_correction)).reshape(
        heads_shape
    )
    acceptance_query = acceptance_query.reshape(heads_shape)
    outputs = []
    for position in range(TS):
        live_now = (position < live_count)[:, None, None, None]
        removed = jnp.sum(state_now * (-key_dir[:, position])[:, :, None, :], axis=-1)
        update = state_now * decay_rate[:, position][:, :, None, :]
        update = (
            update
            + removed[..., None] * (key_dir[:, position] * learn_rate[:, position])[:, :, None, :]
        )
        update = (
            update
            + payload_entries[:, position][..., None]
            * address_corrected[:, position][:, :, None, :]
        )
        state_now = jnp.where(live_now, update, state_now)
        reading = jnp.sum(state_now * acceptance_query[:, position][:, :, None, :], axis=-1)
        outputs.append(jnp.where(live_now[..., 0], reading, jnp.zeros_like(reading)))
    groupwise_results = jnp.stack(outputs, axis=1)
    genuine_symbol_filter = (jnp.arange(TS)[None, :] < live_count[:, None])[:, :, None, None]
    reward_multiplier = jnp.sum(
        acceptance_query * address_corrected * reward_coefficients, axis=-1, keepdims=True
    )
    reward_summand = jnp.where(
        genuine_symbol_filter, reward_multiplier * payload_entries, jnp.zeros_like(payload_entries)
    )
    head_sum = lax.psum(jnp.sum(groupwise_results, axis=-1), "row")
    demeaned_entries = head_sum / CHANNEL_SPAN
    offset = groupwise_results - demeaned_entries[..., None]
    groupwise_spread = lax.psum(jnp.sum(offset * offset, axis=-1), "row") / CHANNEL_SPAN
    standardised_groups = (
        (groupwise_results - demeaned_entries[..., None])
        / jnp.sqrt(groupwise_spread[..., None] + 0.00064)
        * groupwise_gain
        + reward_summand
    ).astype(jnp.bfloat16)
    last_token = jnp.take_along_axis(current, (live_count - 1)[:, None, None], axis=1)[:, 0]
    return (state_now, last_token, standardised_groups)


def per_device(
    incoming_activations,
    genuine_symbol_number,
    caller_sheet_slot,
    memory_sheets,
    prior_activation_sheets,
    blend_fractions,
    first_projectors,
    fading_narrow_projector,
    fading_widen_projector,
    fading_offset,
    context_step_narrowing,
    context_step_widening,
    context_step_offset,
    erasure_address_gain,
    address_correction,
    reward_coefficients,
    groupwise_gain,
    final_projector,
):
    req_count = lax.axis_size("req")
    head_count = lax.axis_size("head")
    row_count = lax.axis_size("row")
    capacity = (REQ_DEV + req_count - 1) // req_count
    slot_count = req_count * capacity
    device = lax.axis_index("req")
    request_slots, request_valid, page_slots, page_valid = slot_tables(
        genuine_symbol_number, caller_sheet_slot, device, req_count, capacity
    )
    gathered = lax.all_gather(incoming_activations, "head", axis=0, tiled=True)
    local_heads = memory_sheets.shape[1]
    value_rows = groupwise_gain.shape[1]
    leaving = invert_slots(page_slots, slot_count)
    state_got, shift_got = (
        lax.all_to_all(
            pick_rows(memory_sheets, leaving), "req", split_axis=0, concat_axis=0, tiled=True
        ),
        lax.all_to_all(
            pick_rows(prior_activation_sheets, leaving),
            "req",
            split_axis=0,
            concat_axis=0,
            tiled=True,
        ),
    )
    state_now = jnp.take(state_got, request_slots, axis=0).reshape(
        REQ_DEV, local_heads, value_rows, CHANNEL_SPAN
    )
    shift_now = jnp.take(shift_got, request_slots, axis=0)
    state_new, last_token, standardised_groups = time_mix(
        gathered,
        request_valid,
        state_now,
        shift_now,
        blend_fractions,
        first_projectors,
        fading_narrow_projector,
        fading_widen_projector,
        fading_offset,
        context_step_narrowing,
        context_step_widening,
        context_step_offset,
        erasure_address_gain,
        address_correction,
        reward_coefficients,
        groupwise_gain,
    )
    homeward = invert_slots(request_slots, slot_count)
    flat_state = state_new.reshape(REQ_DEV, local_heads, value_rows * CHANNEL_SPAN)
    state_back, shift_back = (
        lax.all_to_all(
            pick_rows(flat_state, homeward).astype(jnp.bfloat16),
            "req",
            split_axis=0,
            concat_axis=0,
            tiled=True,
        ).astype(jnp.float32),
        lax.all_to_all(
            pick_rows(last_token, homeward).astype(jnp.bfloat16),
            "req",
            split_axis=0,
            concat_axis=0,
            tiled=True,
        ).astype(jnp.float32),
    )
    new_state = jnp.take(state_back, page_slots, axis=0)
    new_shift = jnp.take(shift_back, page_slots, axis=0)
    grouped = standardised_groups.reshape(
        head_count, REQ_DEV // head_count, TS, local_heads * value_rows
    )
    columns = final_projector.reshape(
        local_heads * value_rows, row_count, final_projector.shape[2] // row_count
    )
    terms = jnp.einsum("hqtf,fcd->hcqtd", grouped, columns, preferred_element_type=jnp.float32)
    terms = terms.reshape(head_count * row_count * (REQ_DEV // head_count), TS, columns.shape[2])
    mixed = lax.psum_scatter(
        terms.astype(jnp.bfloat16), ("head", "row"), scatter_dimension=0, tiled=True
    )
    return (mixed, new_state, new_shift)


def solution(mesh):
    placed = (
        P(("req", "head"), None, "row"),
        P(),
        P(),
        P("req", "head", "row"),
        P("req", "row"),
        P(None, "row"),
        P(None, "row", "head"),
        P("row", None),
        P(None, "head"),
        P("head"),
        P("row", None),
        P(None, "head"),
        P("head"),
        P("head"),
        P("head"),
        P("head", None),
        P("head", "row"),
        P("head", "row", None),
    )
    return jax.shard_map(
        per_device,
        mesh=mesh,
        in_specs=placed,
        out_specs=(P(("req", "head"), None, "row"), P("req", "head", "row"), P("req", "row")),
        check_vma=False,
    )
```

profile of v0, /device:TPU:1, one launch (start us, length us, event | category | flops | bytes accessed | tf_op | source)
XLA Modules:
  0.0 374.1 jit_solution(15861583957403726147)
XLA Ops:
  7.2 0.8 add_select_fusion.4
  8.7 0.8 compare_and_fusion.4
  9.5 10.5 %all_gather.3 = bf16[16,4,512]{2,1,0:T(4,128)(2,1)S(1)} all-gather(bf16[4,4,512]{2,1,0:T(4,128)(2,1)} %param.26), channel_id=1, replica_groups=mesh['req'=32,'head'=4,'row'=4] {'head'}, dimensions={0}, use_global_device_ids=true | all-gather | bytes 81920 | tf_op jit(solution)/shard_map/all_gather | solution.py:169
  20.2 0.6 gather_fusion.1
  20.9 0.6 gather_fusion.8
  22.1 0.7 reduce
  22.8 0.6 reshape.568
  23.4 18.8 %all-to-all-start.3 = ((bf16[32,2,256]{2,1,0:T(2,128)(2,1)}), bf16[32,2,256]{2,1,0:T(2,128)(2,1)S(1)}, u32[]{:S(2)}, u32[]{:S(2)}) async-start(bf16[32,2,256]{2,1,0:T(2,128)(2,1)} %reshape.568), calls=%async_computation.3 | async-start | bytes 65536 | tf_op jit(solution)/shard_map/all_to_all | solution.py:217
  43.4 0.9 select_reduce_fusion.1
  44.2 0.7 gather_fusion
  47.0 0.7 copy.78
  47.7 0.6 gather_fusion.2
  48.4 1.1 broadcast_select_fusion
  49.5 4.9 %all-to-all-done.3 = bf16[32,2,256]{2,1,0:T(2,128)(2,1)S(1)} async-done(((bf16[32,2,256]{2,1,0:T(2,128)(2,1)}), bf16[32,2,256]{2,1,0:T(2,128)(2,1)S(1)}, u32[]{:S(2)}, u32[]{:S(2)}) %all-to-all-start.3) | async-done | bytes 32800 | tf_op jit(solution)/shard_map/all_to_all | solution.py:217
  54.3 7.3 %all-to-all-start.1 = ((f32[32,1,512]{2,1,0:T(1,128)}), f32[32,1,512]{2,1,0:T(1,128)S(1)}, u32[]{:S(2)}, u32[]{:S(2)}) async-start(f32[32,1,512]{2,1,0:T(1,128)} %copy.78), calls=%async_computation.1 | async-start | bytes 131072 | tf_op jit(solution)/shard_map/all_to_all | solution.py:177
  61.7 1.1 slice_bitcast_fusion
  62.8 11.9 %all-to-all-done.1 = f32[32,1,512]{2,1,0:T(1,128)S(1)} async-done(((f32[32,1,512]{2,1,0:T(1,128)}), f32[32,1,512]{2,1,0:T(1,128)S(1)}, u32[]{:S(2)}, u32[]{:S(2)}) %all-to-all-start.1) | async-done | bytes 65568 | tf_op jit(solution)/shard_map/all_to_all | solution.py:177
  74.7 5.2 %all-to-all-start = ((f32[32,8,1024]{2,1,0:T(8,128)}), f32[32,8,1024]{2,1,0:T(8,128)S(1)}, u32[]{:S(2)}, u32[]{:S(2)}) async-start(f32[32,8,1024]{2,1,0:T(8,128)} %broadcast_select_fusion), calls=%async_computation | async-start | bytes 2097152 | tf_op jit(solution)/shard_map/all_to_all | solution.py:174
  80.0 1.3 dynamic-slice.2
  81.3 1.3 dynamic-slice
  84.4 0.7 reshape.569
  85.7 1.3 fusion.19
  87.0 0.8 reshape.445
  87.8 1.9 fusion.21
  89.8 1.9 fusion.47
  92.0 15.2 %all-reduce.6 = (bf16[16,4,96]{2,0,1:T(8,128)(2,1)S(1)}, f32[16,4,96]{2,0,1:T(8,128)S(1)}) all-reduce(f32[16,4,96]{2,0,1:T(8,128)S(1)} %fusion.40, f32[16,4,96]{2,0,1:T(8,128)S(1)} %fusion.43), channel_id=1, replica_groups=mesh['req'=32,'head'=4,'row'=4] {'row'}, use_global_device_ids=true, to_apply=%region_8.13 | all-reduce | flops 12288 | bytes 86016 | tf_op jit(solution)/shard_map/psum | solution.py:80
  107.7 1.1 mul.569
  108.9 1.1 mul.565
  110.1 1.1 mul.561
  111.4 1.1 mul.557
  112.5 43.9 %all-reduce.13.cloned.1.call-done = (f32[16,4,8,64]{3,2,0,1:T(8,128)}, f32[16,4,512]{2,0,1:T(8,128)}, f32[16,4,8,4,16]{4,0,3,2,1:T(8,128)}) async-done(((f32[16,4,8,64]{3,2,0,1:T(8,128)}, f32[16,4,512]{2,0,1:T(8,128)}, f32[16,4,8,4,16]{4,0,3,2,1:T(8,128)}), (f32[16,4,8,64]{3,2,0,1:T(8,128)}, f32[16,4,512]{2,0,1:T(8,128)}, f32[16,4,8,4,16]{4,0,3,2,1:T(8,128)})) %all-reduce.13.cloned.1.call-update) | async-done | bytes 393232 | tf_op jit(solution)/shard_map/psum | solution.py:80
  156.4 1.1 broadcast_multiply_fusion.4
  157.8 1.6 constant_dynamic-slice_fusion.1
  159.9 0.7 slice_bitcast_fusion.2
  160.6 0.7 slice_bitcast_fusion.1
  161.4 0.7 slice_bitcast_fusion.3
  162.2 0.8 fusion.52
  163.0 0.7 gather_fusion.3
  163.9 1.3 reshape.439
  165.2 5.7 %multiply_reduce_fusion.3 = (f32[16,8,16]{2,1,0:T(8,128)}, f32[16,8,16,64]{3,2,1,0:T(8,128)S(1)}, f32[16,8,16,64]{3,2,1,0:T(8,128)}, f32[16,8,16,64]{3,2,1,0:T(8,128)S(1)}) fusion(f32[16,8,64]{2,1,0:T(8,128)} %get-tuple-element.51, f32[16,8,16,64]{3,2,1,0:T(8,128)} %reshape.439, f32[16,8,64]{2,1,0:T(8,128)} %get-tuple-element.47, ...), kind=kOutput, calls=%fused_computation.33 | output fusion | flops 1179711 | bytes 2277392 | tf_op jit(solution)/shard_map/mul | solution.py:108
  170.8 2.3 mul.560
  173.1 1.1 mul.559
  174.3 5.1 %multiply_reduce_fusion.2 = (f32[16,8,16]{2,1,0:T(8,128)}, f32[16,8,16,64]{3,2,1,0:T(8,128)S(1)}, f32[16,8,16,64]{3,2,1,0:T(8,128)}, f32[16,8,16,64]{3,2,1,0:T(8,128)}) fusion(f32[16,8,64]{2,1,0:T(8,128)} %get-tuple-element.50, f32[16,8,16,64]{3,2,1,0:T(8,128)S(1)} %get-tuple-element.21, f32[16,8,64]{2,1,0:T(8,128)} %get-tuple-element.46, ...), kind=kOutput, calls=%fused_computation.31 | output fusion | flops 1179711 | bytes 2277392 | tf_op jit(solution)/shard_map/mul | solution.py:108
  179.4 2.4 mul.564
  181.8 1.1 mul.563
  182.9 4.5 %broadcast_multiply_fusion.1 = (f32[16,8,16,64]{3,2,1,0:T(8,128)}, f32[16,8,16,64]{3,2,1,0:T(8,128)}, f32[16,8,16,64]{3,2,1,0:T(8,128)S(1)}) fusion(f32[16,8,64]{2,1,0:T(8,128)} %get-tuple-element.45, f32[16,8,16]{2,1,0:T(8,128)} %get-tuple-element.41, f32[16,8,16,64]{3,2,1,0:T(8,128)S(1)} %get-tuple-element.23, f32[16,8,64]{2,1,0:T(8,128)} %copy-done.7, ...), kind=kOutput, calls=%fused_computation.52 | output fusion | flops 919615 | bytes 2236432 | tf_op jit(solution)/shard_map/mul | solution.py:108
  187.4 2.4 mul.568
  189.8 1.1 mul.567
  190.9 5.0 %multiply_reduce_fusion.1 = (f32[16,8,16]{2,1,0:T(8,128)}, f32[16,8,16]{2,1,0:T(8,128)}, f32[16,8,16,64]{3,2,1,0:T(8,128)}, f32[16,8,16,64]{3,2,1,0:T(8,128)S(1)}) fusion(f32[16,8,16,64]{3,2,1,0:T(8,128)S(1)} %copy-done.2, f32[16,8,64]{2,1,0:T(8,128)} %get-tuple-element.49, f32[16,8,64]{2,1,0:T(8,128)} %get-tuple-element.48, ...), kind=kOutput, calls=%fused_computation.29 | output fusion | flops 1439807 | bytes 1794064 | tf_op jit(solution)/shard_map/mul | solution.py:108
  195.9 2.4 mul.572
  198.3 1.1 mul.571
  199.4 3.2 add_select_fusion.3
  202.7 0.8 gather_fusion.6
  203.6 1.0 select_convert_fusion
  204.5 13.1 %all-to-all-start.2 = ((bf16[32,8,1024]{2,1,0:T(8,128)(2,1)}), bf16[32,8,1024]{2,1,0:T(8,128)(2,1)S(1)}, u32[]{:S(2)}, u32[]{:S(2)}) async-start(bf16[32,8,1024]{2,1,0:T(8,128)(2,1)} %select_convert_fusion), calls=%async_computation.2 | async-start | bytes 1048576 | tf_op jit(solution)/shard_map/all_to_all | solution.py:210
  218.2 13.5 %psum.46 = f32[16,4,8]{2,0,1:T(8,128)S(1)} all-reduce(f32[16,4,8]{2,0,1:T(8,128)S(1)} %fusion.61), channel_id=1, replica_groups=mesh['req'=32,'head'=4,'row'=4] {'row'}, use_global_device_ids=true, to_apply=%region_19.24 | all-reduce | flops 512 | bytes 4096 | tf_op jit(solution)/shard_map/psum | solution.py:126
  231.9 11.8 %psum.47 = f32[16,4,8]{2,0,1:T(8,128)S(1)} all-reduce(f32[16,4,8]{2,0,1:T(8,128)S(1)} %multiply_reduce_fusion.9), channel_id=1, replica_groups=mesh['req'=32,'head'=4,'row'=4] {'row'}, use_global_device_ids=true, to_apply=%region_21.26 | all-reduce | flops 512 | bytes 4096 | tf_op jit(solution)/shard_map/psum | solution.py:129
  244.6 0.8 copy.83
  245.5 0.7 gather_fusion.9
  246.2 0.7 broadcast_select_fusion.3
  246.9 117.4 %all-reduce.11.cloned.1.call-done = bf16[64,4,512]{2,1,0:T(4,128)(2,1)} async-done(((bf16[64,4,512]{2,1,0:T(4,128)(2,1)}), bf16[64,4,512]{2,1,0:T(4,128)(2,1)}) %all-reduce.11.cloned.1.call-update) | async-done | bytes 262160
  364.2 1.3 constant_dynamic-slice_fusion
  365.7 0.7 gather_fusion.7
  366.4 0.9 broadcast_select_fusion.1
  (162 shorter events, 10.2 us)
Async XLA Ops:
  7.2 149.2 %copy-start = (bf16[96,512]{1,0:T(8,128)(2,1)S(1)}, bf16[96,512]{1,0:T(8,128)(2,1)}, u32[]{:S(2)}) copy-start(bf16[96,512]{1,0:T(8,128)(2,1)} %param.37) | copy-start | bytes 294916
  7.2 38.5 %copy-start.24 = (f32[5,512]{1,0:T(8,128)S(1)}, f32[5,512]{1,0:T(8,128)}, u32[]{:S(2)}) copy-start(f32[5,512]{1,0:T(8,128)} %param.31) | copy-start | bytes 30724
  7.2 39.1 %copy-start.17 = (f32[16,512]{1,0:T(8,128)S(1)}, f32[16,512]{1,0:T(8,128)}, u32[]{:S(2)}) copy-start(f32[16,512]{1,0:T(8,128)} %param.30) | copy-start | bytes 98308
  7.2 40.5 %copy-start.11 = (f32[16,8,1024]{2,1,0:T(8,128)S(1)}, f32[16,8,1024]{2,1,0:T(8,128)}, u32[]{:S(2)}) copy-start(f32[16,8,1024]{2,1,0:T(8,128)} %param.29) | copy-start | bytes 1572868
  9.5 34.7 %copy-start.26 = (pred[32]{0:T(512)(128)(4,1)}, pred[32]{0:T(512)(128)(4,1)S(1)}, u32[]{:S(2)}) copy-start(pred[32]{0:T(512)(128)(4,1)S(1)} %get-tuple-element.18) | copy-start | bytes 100
  9.5 38.2 %copy-start.22 = (s32[1024]{0:T(1024)}, s32[1024]{0:T(1024)S(1)}, u32[]{:S(2)}) copy-start(s32[1024]{0:T(1024)S(1)} %pad_clamp_fusion.1) | copy-start | bytes 12292
  23.4 30.9 %all-to-all-start.3 = ((bf16[32,2,256]{2,1,0:T(2,128)(2,1)}), bf16[32,2,256]{2,1,0:T(2,128)(2,1)S(1)}, u32[]{:S(2)}, u32[]{:S(2)}) async-start(bf16[32,2,256]{2,1,0:T(2,128)(2,1)} %reshape.568), calls=%async_computation.3 | async-start | bytes 65536 | tf_op jit(solution)/shard_map/all_to_all | solution.py:217
  54.3 20.4 %all-to-all-start.1 = ((f32[32,1,512]{2,1,0:T(1,128)}), f32[32,1,512]{2,1,0:T(1,128)S(1)}, u32[]{:S(2)}, u32[]{:S(2)}) async-start(f32[32,1,512]{2,1,0:T(1,128)} %copy.78), calls=%async_computation.1 | async-start | bytes 131072 | tf_op jit(solution)/shard_map/all_to_all | solution.py:177
  61.7 20.9 %copy-start.10 = (bf16[8,16,2048]{2,1,0:T(8,128)(2,1)S(1)}, bf16[8,16,2048]{2,1,0:T(8,128)(2,1)}, u32[]{:S(2)}) copy-start(bf16[8,16,2048]{2,1,0:T(8,128)(2,1)} %param.43) | copy-start | bytes 1572868
  74.7 88.3 %all-to-all-start = ((f32[32,8,1024]{2,1,0:T(8,128)}), f32[32,8,1024]{2,1,0:T(8,128)S(1)}, u32[]{:S(2)}, u32[]{:S(2)}) async-start(f32[32,8,1024]{2,1,0:T(8,128)} %broadcast_select_fusion), calls=%async_computation | async-start | bytes 2097152 | tf_op jit(solution)/shard_map/all_to_all | solution.py:174
  79.9 5.8 %copy-start.19 = (f32[1,512]{1,0:T(1,128)S(1)}, f32[1,512]{1,0:T(1,128)}, u32[]{:S(2)}) copy-start(f32[1,512]{1,0:T(1,128)} %get-tuple-element.62) | copy-start | bytes 6148
  79.9 76.5 %all-reduce.13.cloned.1.call-start = ((), (), s32[]{:S(2)}) async-start(), calls=%async_computation.5 | async-start | bytes 2883584 | tf_op jit(solution)/shard_map/psum | solution.py:80
  80.0 7.0 %copy-start.23 = (s32[1024]{0:T(1024)}, s32[1024]{0:T(1024)S(1)}, u32[]{:S(2)}) copy-start(s32[1024]{0:T(1024)S(1)} %pad_clamp_fusion.2) | copy-start | bytes 12292
  82.9 4.9 %copy-start.18 = (f32[1,512]{1,0:T(1,128)S(1)}, f32[1,512]{1,0:T(1,128)}, u32[]{:S(2)}) copy-start(f32[1,512]{1,0:T(1,128)} %get-tuple-element.61) | copy-start | bytes 6148
  83.2 6.6 %copy-start.20 = (f32[1,512]{1,0:T(1,128)S(1)}, f32[1,512]{1,0:T(1,128)}, u32[]{:S(2)}) copy-start(f32[1,512]{1,0:T(1,128)} %get-tuple-element.63) | copy-start | bytes 6148
  89.7 2.0 copy-start.31
  89.7 2.0 copy-start.33
  89.7 2.1 copy-start.30
  89.7 2.1 copy-start.34
  89.7 17.5 %copy-start.35 = (bf16[96,512]{1,0:T(8,128)(2,1)S(1)}, bf16[96,512]{1,0:T(8,128)(2,1)}, u32[]{:S(2)}) copy-start(bf16[96,512]{1,0:T(8,128)(2,1)} %param.34) | copy-start | bytes 294916
  89.8 17.5 %copy-start.36 = (f32[512]{0:T(512)S(1)}, f32[512]{0:T(512)}, u32[]{:S(2)}) copy-start(f32[512]{0:T(512)} %param.35) | copy-start | bytes 6148
  107.6 1.3 copy-start.6
  107.6 1.3 copy-start.7
  107.6 2.4 copy-start.8
  107.6 3.6 copy-start.9
  111.3 45.1 %copy-start.37 = (f32[512]{0:T(512)S(1)}, f32[512]{0:T(512)}, u32[]{:S(2)}) copy-start(f32[512]{0:T(512)} %param.39) | copy-start | bytes 6148
  111.3 45.1 %copy-start.38 = (f32[512]{0:T(512)S(1)}, f32[512]{0:T(512)}, u32[]{:S(2)}) copy-start(f32[512]{0:T(512)} %param.40) | copy-start | bytes 6148
  111.3 45.1 %copy-start.39 = (f32[512]{0:T(512)S(1)}, f32[512]{0:T(512)}, u32[]{:S(2)}) copy-start(f32[512]{0:T(512)} %param.38) | copy-start | bytes 6148
  156.4 3.3 copy-start.5
  156.4 3.3 copy-start.28
  179.4 2.4 copy-start.1
  187.4 3.6 copy-start.2
  195.9 3.5 copy-start.3
  195.9 3.5 copy-start.4
  202.6 0.9 copy-start.27
  202.7 15.1 %copy-start.12 = (f32[16,8,16]{2,1,0:T(8,128)S(1)}, f32[16,8,16]{2,1,0:T(8,128)}, u32[]{:S(2)}) copy-start(f32[16,8,16]{2,1,0:T(8,128)} %get-tuple-element.20) | copy-start | bytes 24580
  202.7 15.1 %copy-start.13 = (f32[16,8,16]{2,1,0:T(8,128)S(1)}, f32[16,8,16]{2,1,0:T(8,128)}, u32[]{:S(2)}) copy-start(f32[16,8,16]{2,1,0:T(8,128)} %get-tuple-element.22) | copy-start | bytes 24580
  202.7 15.2 %copy-start.14 = (f32[16,8,16]{2,1,0:T(8,128)S(1)}, f32[16,8,16]{2,1,0:T(8,128)}, u32[]{:S(2)}) copy-start(f32[16,8,16]{2,1,0:T(8,128)} %get-tuple-element.6) | copy-start | bytes 24580
  202.7 15.2 %copy-start.15 = (f32[16,8,16]{2,1,0:T(8,128)S(1)}, f32[16,8,16]{2,1,0:T(8,128)}, u32[]{:S(2)}) copy-start(f32[16,8,16]{2,1,0:T(8,128)} %get-tuple-element.8) | copy-start | bytes 24580
  202.7 15.2 %copy-start.21 = (pred[16]{0:T(512)(128)(4,1)S(1)}, pred[16]{0:T(512)(128)(4,1)}, u32[]{:S(2)}) copy-start(pred[16]{0:T(512)(128)(4,1)} %get-tuple-element.64) | copy-start | bytes 52
  203.6 40.2 %copy-start.29 = (f32[8,16]{1,0:T(8,128)S(1)}, f32[8,16]{1,0:T(8,128)}, u32[]{:S(2)}) copy-start(f32[8,16]{1,0:T(8,128)} %param.42) | copy-start | bytes 1540
  203.6 40.2 %copy-start.32 = (pred[16,4]{0,1:T(4,128)(4,1)S(1)}, pred[16,4]{0,1:T(4,128)(4,1)}, u32[]{:S(2)}) copy-start(pred[16,4]{0,1:T(4,128)(4,1)} %iota_compare_fusion.3) | copy-start | bytes 196
  204.5 161.0 %all-to-all-start.2 = ((bf16[32,8,1024]{2,1,0:T(8,128)(2,1)}), bf16[32,8,1024]{2,1,0:T(8,128)(2,1)S(1)}, u32[]{:S(2)}, u32[]{:S(2)}) async-start(bf16[32,8,1024]{2,1,0:T(8,128)(2,1)} %select_convert_fusion), calls=%async_computation.2 | async-start | bytes 1048576 | tf_op jit(solution)/shard_map/all_to_all | solution.py:210
  217.7 146.5 %all-reduce.11.cloned.1.call-start = ((), (), s32[]{:S(2)}) async-start(), calls=%async_computation.4 | async-start | bytes 524288
  218.2 27.3 %copy-start.16 = (bf16[32,1,512]{2,1,0:T(2,128)(2,1)S(1)}, bf16[32,1,512]{2,1,0:T(2,128)(2,1)}, u32[]{:S(2)}) copy-start(bf16[32,1,512]{2,1,0:T(2,128)(2,1)} %reshape.569) | copy-start | bytes 98308
  231.9 14.2 %copy-start.25 = (pred[16]{0:T(512)(128)(4,1)S(1)}, pred[16]{0:T(512)(128)(4,1)}, u32[]{:S(2)}) copy-start(pred[16]{0:T(512)(128)(4,1)} %get-tuple-element.16) | copy-start | bytes 52
Sparse Core Ops, SparseCore 0:
  91.8 64.5 all-reduce.12
  245.5 118.6 all-reduce.10
where the time goes:
time: 375 us; the launch traced here: 374 us
  waiting for transfers between devices  178 us (47%)
  blocking collectives  51 us (14%)
  starting transfers between devices  44.5 us (12%)
  local copies, waits for them, and re-layouts  42.2 us (11%)
  other arithmetic  35.7 us (10%)
  between operations  15.7 us (4%)
  matrix products  6.99 us (2%)
    unnamed x3, waiting for transfers between devices  117 us
    psum x1, waiting for transfers between devices, time_mix(): lax.psum((recept_part, key_part, decay_part, learn_part), 'row')  43.9 us
    mul x4, other arithmetic, time_mix(): removed[..., None]  20.2 us
    all_to_all x1, starting transfers between devices, per_device(): lax.all_to_all(pick_rows(last_token, homeward).astype(jnp.bfloat16), 'req...  18.8 us
    psum x1, blocking collectives, time_mix(): lax.psum((recept_part, key_part, decay_part, learn_part), 'row')  15.2 us
    psum x1, blocking collectives, time_mix(): head_sum = lax.psum(jnp.sum(groupwise_results, axis=-1), 'row')  13.5 us
    all_to_all x1, starting transfers between devices, per_device(): lax.all_to_all(pick_rows(flat_state, homeward).astype(jnp.bfloat16), 'req...  13.1 us
    all_to_all x1, waiting for transfers between devices, per_device(): lax.all_to_all(pick_rows(prior_activation_sheets, leaving), 'req', split_...  11.9 us
  transfers between devices with their start and end apart: 6, of which 4 were waited for; matrix products, arithmetic and copies ran while one was open for 10% of the time, Pallas kernels for 0%

commit v1 on v0

v1 whole, which is shorter than its diff:
```python
import functools

import jax
import jax.numpy as jnp
import numpy as np
from jax import lax
from jax.experimental import pallas as pl
from jax.experimental.pallas import tpu as pltpu
from jax.sharding import PartitionSpec as P

CHANNEL_SPAN = 64
TS = 4
REQ_DEV = 16
HEADS = 8
ROWS = 16
FEATS = HEADS * CHANNEL_SPAN
VALS = HEADS * ROWS
TOK = REQ_DEV * TS
LANES = 128
DECAY_AT = 2 * FEATS + VALS
LEARN_AT = DECAY_AT + LANES
WIDTH = LEARN_AT + LANES
F32 = jnp.float32
BF16 = jnp.bfloat16
VMEM = pl.BlockSpec(memory_space=pltpu.VMEM)
SMEM = pl.BlockSpec(memory_space=pltpu.SMEM)


def value_lane(head, row):
    return (row % 2) * 64 + head * 8 + row // 2


def constant_matrices():
    lanes = np.arange(256)
    halves = (lanes[:, None] // 64 == lanes[None, :] // 64).astype(np.float32)
    c = np.arange(VALS)
    lane_head = (c % 64) // 8
    same_head = (lane_head[:, None] == lane_head[None, :]).astype(np.float32)
    head_to_lanes = (np.arange(FEATS)[:, None] // 64 == lane_head[None, :]).astype(np.float32)
    to_natural = np.zeros((VALS, VALS), np.float32)
    spread_values = np.zeros((FEATS, FEATS), np.float32)
    for head in range(HEADS):
        for row in range(ROWS):
            to_natural[value_lane(head, row), head * ROWS + row] = 1
            for part in range(4):
                spread_values[head * 64 + part * ROWS + row, part * VALS + value_lane(head, row)] = 1
    return halves, same_head, head_to_lanes, to_natural, spread_values


def dot(a, b):
    return jnp.dot(a, b, preferred_element_type=F32)


def dot_split(a, b):
    high = a.astype(BF16)
    low = (a - high.astype(F32)).astype(BF16)
    return dot(high, b) + dot(low, b)


def call(kernel, outs, in_specs, args, scratch=(), flops=0, name=None):
    size = sum(int(np.prod(a.shape)) * a.dtype.itemsize for a in args)
    size += sum(int(np.prod(o.shape)) * o.dtype.itemsize for o in outs)
    single = len(outs) == 1
    return pl.pallas_call(
        kernel,
        out_shape=outs[0] if single else outs,
        in_specs=in_specs,
        out_specs=VMEM if single else [VMEM] * len(outs),
        scratch_shapes=list(scratch),
        cost_estimate=pl.CostEstimate(flops=flops, bytes_accessed=size, transcendentals=0),
        compiler_params=pltpu.CompilerParams(vmem_limit_bytes=32 * 2**20),
        name=name,
    )(*args)


def pack_kernel(dest_ref, x_ref, out_ref):
    for q in range(REQ_DEV):
        out_ref[dest_ref[q]] = x_ref[q]


def mix_kernel(
    source_ref, got_ref, last_ref, shift_ref, blend_ref, proj_ref, value_ref, decay_ref, learn_ref,
    out_ref, new_shift_ref, tokens,
):
    for page in range(REQ_DEV):
        tile = got_ref[source_ref[page]].astype(F32)
        for part in range(4):
            tokens[part, pl.ds(page, TS, stride=REQ_DEV), :] = tile[part * TS:(part + 1) * TS]
    current = jnp.concatenate([tokens[part] for part in range(4)], axis=1)
    before = jnp.concatenate([shift_ref[...], current[:-REQ_DEV]], axis=0)
    towards = before - current
    mixed = [(current + towards * blend_ref[b:b + 1, :]).astype(BF16) for b in range(5)]
    recept = dot(mixed[0], proj_ref[0]).astype(BF16)
    key = dot(mixed[2], proj_ref[1]).astype(BF16)
    value = dot(mixed[3], value_ref[...]).astype(BF16)
    decay = dot(mixed[1], decay_ref[...]).astype(BF16)
    learn = dot(mixed[4], learn_ref[...]).astype(BF16)
    pad = jnp.zeros((TOK, LANES - decay.shape[1]), BF16)
    for part in range(4):
        out_ref[part, :, 0:FEATS] = recept
        out_ref[part, :, FEATS:2 * FEATS] = key
        out_ref[part, :, 2 * FEATS:DECAY_AT] = value[:, part * VALS:(part + 1) * VALS]
        out_ref[part, :, DECAY_AT:LEARN_AT] = jnp.concatenate([decay, pad], axis=1)
        out_ref[part, :, LEARN_AT:WIDTH] = jnp.concatenate([learn, pad], axis=1)
    kept = last_ref[...]
    picked = current * jnp.concatenate([kept] * 4, axis=1)
    total = picked[0:REQ_DEV]
    for t in range(1, TS):
        total = total + picked[t * REQ_DEV:(t + 1) * REQ_DEV]
    new_shift_ref[...] = total


def state_kernel(
    got_ref, live_ref, state_ref, decay_ref, decay_offset_ref, learn_ref, learn_offset_ref, gain_ref,
    correction_ref, reward_ref, halves_ref, same_head_ref, head_to_lanes_ref,
    new_state_ref, reading_ref, bonus_ref, stat_ref, spread, states,
):
    total = got_ref[0].astype(F32)
    for part in range(1, 4):
        total = total + got_ref[part].astype(F32)
    recept = total[:, 0:FEATS]
    key = total[:, FEATS:2 * FEATS]
    value = total[:, 2 * FEATS:DECAY_AT]
    rank = decay_ref.shape[0]
    decay_low = jnp.tanh(total[:, DECAY_AT:DECAY_AT + rank]).astype(BF16)
    learn_low = total[:, LEARN_AT:LEARN_AT + learn_ref.shape[0]].astype(BF16)
    decay_in = decay_offset_ref[...] + dot(decay_low, decay_ref[...])
    learn = jax.nn.sigmoid(learn_offset_ref[...] + dot(learn_low, learn_ref[...]))
    decay = jnp.exp(jax.nn.sigmoid(decay_in) * (-float(np.exp(-0.5))))
    halves = halves_ref[...]
    scaled = key * gain_ref[...]
    squares = scaled * scaled
    norm = jnp.concatenate(
        [dot_split(squares[:, 0:256], halves), dot_split(squares[:, 256:512], halves)], axis=1
    )
    key_dir = scaled * lax.rsqrt(norm + 1e-6)
    key_adj = key * (1.0 + (learn - 1.0) * correction_ref[...])
    live = live_ref[...]
    live_wide = jnp.concatenate([live] * 4, axis=1)
    reward = dot_split(recept * key_adj * reward_ref[...], head_to_lanes_ref[...])
    bonus_ref[...] = reward * value * live
    vectors = [
        key_dir,
        jnp.where(live_wide > 0, decay, 1.0),
        key_dir * learn * live_wide,
        key_adj * live_wide,
        recept * live_wide,
    ]
    low_half = lax.broadcasted_iota(jnp.int32, (TOK, LANES), 1) < 64
    for at, vector in enumerate(vectors):
        for pair in range(HEADS // 2):
            block = vector[:, pair * LANES:(pair + 1) * LANES]
            turned = pltpu.roll(block, 64, 1)
            spread[at, 2 * pair] = jnp.where(low_half, block, turned)
            spread[at, 2 * pair + 1] = jnp.where(low_half, turned, block)
    lane = lax.broadcasted_iota(jnp.int32, (REQ_DEV, 256), 1)
    lane_key = lane % 64 - lane // 128
    value_pair = jnp.concatenate([value, value], axis=1)
    for head in range(HEADS):
        for quad in range(4):
            at = (head * 4 + quad) * REQ_DEV
            for half in range(2):
                for group in range(2):
                    start = group * 512 + (quad * 2 + half) * 8 + head
                    states[at + group * 8:at + group * 8 + 8, half * LANES:(half + 1) * LANES] = (
                        state_ref[pl.ds(start, 8, stride=64), :]
                    )
    for t in range(TS):
        rows = slice(t * REQ_DEV, (t + 1) * REQ_DEV)
        value_now = value_pair[rows]
        reading = jnp.zeros((REQ_DEV, LANES), F32)
        for head in range(HEADS):
            direction, keep, remove, add, query = [
                jnp.concatenate([jnp.concatenate([spread[at, head, rows, :]] * 2, axis=1)] * 4, axis=0)
                for at in range(5)
            ]
            masks = [lane_key == head * 8 + 2 * quad for quad in range(4)]
            place = slice(head * 64, (head + 1) * 64)
            state = states[place, :]
            removed = dot((state * direction).astype(BF16), halves)
            values = jnp.concatenate([jnp.where(m, value_now, 0.0) for m in masks], axis=0)
            spread_value = dot(values.astype(BF16), halves)
            state = state * keep - removed * remove + spread_value * add
            if t < TS - 1:
                states[place, :] = state
            else:
                for quad in range(4):
                    for half in range(2):
                        for group in range(2):
                            at = quad * REQ_DEV + group * 8
                            start = group * 512 + (quad * 2 + half) * 8 + head
                            new_state_ref[pl.ds(start, 8, stride=64), :] = state[
                                at:at + 8, half * LANES:(half + 1) * LANES
                            ]
            read = dot((state * query).astype(BF16), halves)
            for quad in range(4):
                part = jnp.where(masks[quad], read[quad * REQ_DEV:(quad + 1) * REQ_DEV], 0.0)
                reading = reading + part[:, 0:LANES] + part[:, LANES:256]
        reading_ref[rows, :] = reading
    reading = reading_ref[...]
    same_head = same_head_ref[...]
    head_sum = dot_split(reading, same_head)
    away = reading - head_sum * (1.0 / ROWS)
    away_sum = dot_split(away * away, same_head)
    stat = jnp.where(low_half, head_sum, away_sum)
    for part in range(4):
        stat_ref[part] = stat


def norm_kernel(source_ref, stat_ref, reading_ref, bonus_ref, gain_ref, to_natural_ref, out_ref, rows):
    low_half = lax.broadcasted_iota(jnp.int32, (TOK, LANES), 1) < 64
    sums, squares = [], []
    for part in range(4):
        stat = stat_ref[part]
        turned = pltpu.roll(stat, 64, 1)
        sums.append(jnp.where(low_half, stat, turned))
        squares.append(jnp.where(low_half, turned, stat))
    mean = (sums[0] + sums[1] + sums[2] + sums[3]) * (1.0 / CHANNEL_SPAN)
    spread = squares[0] + squares[1] + squares[2] + squares[3]
    for part in range(4):
        gap = sums[part] * (1.0 / ROWS) - mean
        spread = spread + gap * gap * float(ROWS)
    scale = lax.rsqrt(spread * (1.0 / CHANNEL_SPAN) + 0.00064)
    normed = (reading_ref[...] - mean) * scale * gain_ref[...] + bonus_ref[...]
    rows[...] = dot(normed.astype(BF16), to_natural_ref[...])
    for page in range(REQ_DEV):
        out_ref[source_ref[page]] = rows[pl.ds(page, TS, stride=REQ_DEV), :].astype(BF16)


def output_kernel(dest_ref, got_ref, proj_ref, out_ref, rows):
    for q in range(REQ_DEV):
        rows[q * TS:(q + 1) * TS, :] = got_ref[dest_ref[q]].astype(F32)
    terms = dot(rows[...].astype(BF16), proj_ref[...]).astype(BF16)
    for head in range(4):
        for part in range(4):
            out_ref[head * 4 + part] = terms[
                head * REQ_DEV:(head + 1) * REQ_DEV, part * FEATS:(part + 1) * FEATS
            ]


def shaped(shape, dtype):
    return jax.ShapeDtypeStruct(shape, dtype)


def per_device(
    incoming_activations,
    genuine_symbol_number,
    caller_sheet_slot,
    memory_sheets,
    prior_activation_sheets,
    blend_fractions,
    first_projectors,
    fading_narrow_projector,
    fading_widen_projector,
    fading_offset,
    context_step_narrowing,
    context_step_widening,
    context_step_offset,
    erasure_address_gain,
    address_correction,
    reward_coefficients,
    groupwise_gain,
    final_projector,
):
    groups = lax.axis_size("req")
    halves, same_head, head_to_lanes, to_natural, spread_values = [
        jnp.asarray(m, BF16) for m in constant_matrices()
    ]
    first = lax.axis_index("req") * REQ_DEV
    dest = lax.dynamic_slice_in_dim(caller_sheet_slot, first, REQ_DEV) // REQ_DEV
    pages = first + jnp.arange(REQ_DEV, dtype=jnp.int32)
    holder = caller_sheet_slot[None, :] == pages[:, None]
    everyone = jnp.arange(caller_sheet_slot.shape[0], dtype=jnp.int32)
    source = jnp.sum(jnp.where(holder, everyone[None, :], 0), axis=1) // REQ_DEV
    count = jnp.sum(jnp.where(holder, genuine_symbol_number[None, :], 0), axis=1)
    position = jnp.arange(TS, dtype=jnp.int32)[:, None]
    live = jnp.broadcast_to((position < count[None, :]).astype(F32)[..., None], (TS, REQ_DEV, LANES))
    last = jnp.broadcast_to(
        (position == count[None, :] - 1).astype(F32)[..., None], (TS, REQ_DEV, LANES)
    )
    live, last = live.reshape(TOK, LANES), last.reshape(TOK, LANES)

    tiles = incoming_activations.reshape(4, TS, 4, LANES).transpose(0, 2, 1, 3).reshape(4, 16, LANES)
    everywhere = jnp.broadcast_to(tiles[None], (4, 4, 16, LANES))
    mine = lax.all_to_all(everywhere, "head", 0, 0, tiled=True).reshape(REQ_DEV, 16, LANES)
    packed = call(
        pack_kernel, [shaped((groups, 16, LANES), BF16)], [SMEM, VMEM], (dest, mine), name="pack"
    )
    got = lax.all_to_all(packed, "req", 0, 0, tiled=True)
    value_projector = dot(first_projectors[2], spread_values).astype(BF16)
    partial, new_shift = call(
        mix_kernel,
        [shaped((4, TOK, WIDTH), BF16), shaped((REQ_DEV, FEATS), F32)],
        [SMEM] + [VMEM] * 8,
        (
            source, got, last, prior_activation_sheets, blend_fractions, first_projectors[0:2],
            value_projector, fading_narrow_projector, context_step_narrowing,
        ),
        scratch=[pltpu.VMEM((4, TOK, LANES), F32)],
        flops=2 * TOK * FEATS * (3 * FEATS + 192),
        name="mix",
    )
    sheets = memory_sheets.reshape(REQ_DEV, HEADS, 8, LANES).transpose(0, 2, 1, 3)
    sheets = sheets.reshape(REQ_DEV * HEADS * 8, LANES)
    sums = lax.all_to_all(partial, "row", 0, 0, tiled=True)
    new_state, reading, bonus, stat = call(
        state_kernel,
        [
            shaped((REQ_DEV * HEADS * 8, LANES), F32),
            shaped((TOK, LANES), F32),
            shaped((TOK, LANES), F32),
            shaped((4, TOK, LANES), F32),
        ],
        [VMEM] * 13,
        (
            sums,
            live,
            sheets,
            fading_widen_projector,
            fading_offset[None],
            context_step_widening,
            context_step_offset[None],
            erasure_address_gain[None],
            address_correction[None],
            reward_coefficients.reshape(1, FEATS),
            halves,
            same_head,
            head_to_lanes,
        ),
        scratch=[pltpu.VMEM((5, HEADS, TOK, LANES), F32), pltpu.VMEM((512, 256), F32)],
        flops=2 * 3 * TS * 512 * 256 * 256,
        name="state",
    )
    stats = lax.all_to_all(stat, "row", 0, 0, tiled=True)
    gain = groupwise_gain.reshape(HEADS, 8, 2).transpose(2, 0, 1).reshape(1, VALS)
    leaving = call(
        norm_kernel,
        [shaped((groups, TS, LANES), BF16)],
        [SMEM] + [VMEM] * 5,
        (source, stats, reading, bonus, gain, to_natural),
        scratch=[pltpu.VMEM((TOK, LANES), F32)],
        name="norm",
    )
    back = lax.all_to_all(leaving, "req", 0, 0, tiled=True)
    terms = call(
        output_kernel,
        [shaped((16, 16, FEATS), BF16)],
        [SMEM, VMEM, VMEM],
        (dest, back, final_projector.reshape(VALS, 4 * FEATS)),
        scratch=[pltpu.VMEM((TOK, LANES), F32)],
        flops=2 * TOK * VALS * 4 * FEATS,
        name="output",
    )
    arrived = lax.all_to_all(terms, ("head", "row"), 0, 0, tiled=True)
    mixed = jnp.sum(arrived.astype(F32), axis=0).astype(BF16).reshape(4, TS, FEATS)
    new_state = new_state.reshape(REQ_DEV, 8, HEADS, LANES).transpose(0, 2, 1, 3)
    return (mixed, new_state.reshape(REQ_DEV, HEADS, 8 * LANES), new_shift)


def solution(mesh):
    placed = (
        P(("req", "head"), None, "row"),
        P(),
        P(),
        P("req", "head", "row"),
        P("req", "row"),
        P(None, "row"),
        P(None, "row", "head"),
        P("row", None),
        P(None, "head"),
        P("head"),
        P("row", None),
        P(None, "head"),
        P("head"),
        P("head"),
        P("head"),
        P("head", None),
        P("head", "row"),
        P("head", "row", None),
    )
    return jax.shard_map(
        per_device,
        mesh=mesh,
        in_specs=placed,
        out_specs=(P(("req", "head"), None, "row"), P("req", "head", "row"), P("req", "row")),
        check_vma=False,
    )
```

time: 375 us -> 109 us (0.29)
  waiting for transfers between devices: 178 us -> 29.2 us
  local copies, waits for them, and re-layouts: 42.2 us -> 4.37 us
  other arithmetic: 35.7 us -> 1.72 us
  blocking collectives: 51 us -> 29.4 us
  between operations: 15.7 us -> 0.96 us
  starting transfers between devices: 44.5 us -> 29.8 us
  Pallas kernels: 0 us -> 11.3 us
  matrix products: 6.99 us -> 1.48 us
    unnamed x3 -> x0, waiting for transfers between devices: 117 us -> none
    psum x1 -> x0, waiting for transfers between devices: 43.9 us -> none  [time_mix(): lax.psum((recept_part, key_part, decay_part, learn_part), 'row')]
    psum x3 -> x0, blocking collectives: 40.5 us -> none  [the longest x1 15.2 us: time_mix(): lax.psum((recept_part, key_part, decay_part, learn_part), 'row')]
    all_to_all x0 -> x2, blocking collectives: none -> 29.4 us  [the longest x1 19.1 us: per_device(): back = lax.all_to_all(leaving, 'req', 0, 0, tiled=True)]
    mul x5 -> x0, other arithmetic: 21 us -> none  [the longest x4 20.2 us: time_mix(): removed[..., None]]
    mul x20 -> x0, local copies, waits for them, and re-layouts: 21 us -> none  [the longest x6 11 us: time_mix(): payload_entries[:, position][..., None]]
    all_to_all x4, starting transfers between devices: 44.4 us -> 29.8 us  [the longest x1 17.3 us: per_device(): got = lax.all_to_all(packed, 'req', 0, 0, tiled=True)]
    all_to_all x4, waiting for transfers between devices: 16.8 us -> 29.2 us  [the longest x1 12.5 us: per_device(): got = lax.all_to_all(packed, 'req', 0, 0, tiled=True)]
  transfers between devices with their start and end apart: 6 -> 4, of which waited for: 4 -> 4; matrix products, arithmetic and copies ran while one was open for 10% -> 5% of each run, Pallas kernels for 0% -> 0%
where the time goes in v1:
time: 109 us; the launch traced here: 108 us
  starting transfers between devices  29.8 us (27%)
  blocking collectives  29.4 us (27%)
  waiting for transfers between devices  29.2 us (27%)
  Pallas kernels  11.3 us (10%)
  local copies, waits for them, and re-layouts  4.37 us (4%)
  other arithmetic  1.72 us (2%)
  matrix products  1.48 us (1%)
    all_to_all x1, blocking collectives, per_device(): back = lax.all_to_all(leaving, 'req', 0, 0, tiled=True)  19.1 us
    all_to_all x1, starting transfers between devices, per_device(): got = lax.all_to_all(packed, 'req', 0, 0, tiled=True)  17.3 us
    all_to_all x1, waiting for transfers between devices, per_device(): got = lax.all_to_all(packed, 'req', 0, 0, tiled=True)  12.5 us
    pallas_call x5, Pallas kernels, call(): pl.pallas_call(kernel, out_shape=outs[0] if single else outs, in_specs=in...  11.3 us
    all_to_all x1, blocking collectives, per_device(): arrived = lax.all_to_all(terms, ('head', 'row'), 0, 0, tiled=True)  10.3 us
    all_to_all x1, waiting for transfers between devices, per_device(): sums = lax.all_to_all(partial, 'row', 0, 0, tiled=True)  9.36 us
    all_to_all x1, starting transfers between devices, per_device(): lax.all_to_all(everywhere, 'head', 0, 0, tiled=True)  5.14 us
    all_to_all x1, waiting for transfers between devices, per_device(): stats = lax.all_to_all(stat, 'row', 0, 0, tiled=True)  4.54 us
  transfers between devices with their start and end apart: 4, of which 4 were waited for; matrix products, arithmetic and copies ran while one was open for 5% of the time, Pallas kernels for 0%

profile of v1, /device:TPU:1, one launch (start us, length us, event | category | flops | bytes accessed | tf_op | source)
XLA Modules:
  0.0 108.2 jit_solution(15248428841758003251)
XLA Ops:
  0.6 0.0 copy-start.14
  0.6 0.0 copy-start.15
  0.7 1.4 %broadcast_in_dim.59 = bf16[4,4,16,128]{3,2,1,0:T(8,128)(2,1)} broadcast(bf16[4,16,128]{2,1,0:T(8,128)(2,1)} %bitcast.42), dimensions={1,2,3} | broadcast | bytes 81920 | tf_op jit(solution)/shard_map/broadcast_in_dim | solution.py:284
  2.0 5.1 %all-to-all-start = ((bf16[4,4,16,128]{3,2,1,0:T(8,128)(2,1)}), bf16[4,4,16,128]{3,2,1,0:T(8,128)(2,1)S(1)}, u32[]{:S(2)}, u32[]{:S(2)}) async-start(bf16[4,4,16,128]{3,2,1,0:T(8,128)(2,1)} %broadcast_in_dim.59), calls=%async_computation | async-start | bytes 131072 | tf_op jit(solution)/shard_map/all_to_all | solution.py:285
  7.2 0.9 fusion.4
  8.1 0.8 and_select_fusion.1.dest_ref
  8.8 2.8 %all-to-all-done = bf16[4,4,16,128]{3,2,1,0:T(8,128)(2,1)S(1)} async-done(((bf16[4,4,16,128]{3,2,1,0:T(8,128)(2,1)}), bf16[4,4,16,128]{3,2,1,0:T(8,128)(2,1)S(1)}, u32[]{:S(2)}, u32[]{:S(2)}) %all-to-all-start) | async-done | bytes 65568 | tf_op jit(solution)/shard_map/all_to_all | solution.py:285
  11.7 1.2 %pack.1 = bf16[32,16,128]{2,1,0:T(8,128)(2,1)} custom-call(s32[16]{0:T(128)S(1)} %and_select_fusion.1.dest_ref, bf16[16,16,128]{2,1,0:T(8,128)(2,1)S(1)} %bitcast.35), custom_call_target="tpu_custom_call" | custom-call | bytes 196672 | tf_op jit(solution)/shard_map/pack/pallas_call | solution.py:64
  12.9 17.3 %all-to-all-start.1 = ((bf16[32,16,128]{2,1,0:T(8,128)(2,1)}), bf16[32,16,128]{2,1,0:T(8,128)(2,1)S(1)}, u32[]{:S(2)}, u32[]{:S(2)}) async-start(bf16[32,16,128]{2,1,0:T(8,128)(2,1)} %pack.1), calls=%async_computation.1 | async-start | bytes 262144 | tf_op jit(solution)/shard_map/all_to_all | solution.py:289
  30.3 0.1 eq.44
  30.3 0.1 lt.22
  30.4 0.1 eq.42
  30.5 1.3 %slice.6.proj_ref = bf16[2,512,512]{2,1,0:T(8,128)(2,1)S(1)} slice(bf16[3,512,512]{2,1,0:T(8,128)(2,1)} %param.29), slice={[0:2], [0:512], [0:512]} | slice | bytes 2097152 | tf_op jit(solution)/shard_map/slice | solution.py:296
  31.8 0.0 copy-done.14
  31.8 0.0 copy-start.1
  31.8 0.0 copy-start.3
  31.9 0.1 copy.39.decay_ref
  32.0 0.0 copy-done.15
  32.0 0.1 copy.40.learn_ref
  32.1 0.0 copy-done.18
  32.1 1.5 %fusion.value_ref = bf16[512,512]{1,0:T(8,128)(2,1)S(1)} fusion(bf16[512,512]{1,0:T(8,128)(2,1)S(1)} %copy-done.18, bf16[3,512,512]{2,1,0:T(8,128)(2,1)} %param.29), kind=kOutput, calls=%fused_computation.1 | convolution fusion | flops 268697600 | bytes 1572864 | tf_op jit(solution)/shard_map/dot_general | solution.py:51
  33.6 12.5 %all-to-all-done.1.got_ref = bf16[32,16,128]{2,1,0:T(8,128)(2,1)S(1)} async-done(((bf16[32,16,128]{2,1,0:T(8,128)(2,1)}), bf16[32,16,128]{2,1,0:T(8,128)(2,1)S(1)}, u32[]{:S(2)}, u32[]{:S(2)}) %all-to-all-start.1) | async-done | bytes 131104 | tf_op jit(solution)/shard_map/all_to_all | solution.py:289
  46.1 0.1 broadcast_in_dim.61.last_ref
  46.2 0.0 copy-done.1
  46.2 0.0 copy-done.3
  46.2 0.0 copy-start.4
  46.2 0.0 copy-start.5
  46.2 0.0 copy-start.6
  46.2 0.0 copy-start.7
  46.2 0.0 copy-start.8
  46.2 0.0 copy-start.9
  46.2 0.0 copy-start.10
  46.3 0.0 copy-start.11
  46.3 0.0 copy-start.12
  46.3 0.0 copy-start.13
  46.3 1.9 %mix.1 = (bf16[4,64,1408]{2,1,0:T(8,128)(2,1)}, f32[16,512]{1,0:T(8,128)}) custom-call(s32[16]{0:T(128)S(1)} %and_select_fusion.source_ref, bf16[32,16,128]{2,1,0:T(8,128)(2,1)S(1)} %all-to-all-done.1.got_ref, f32[64,128]{1,0:T(8,128)S(1)} %broadcast_in_dim.61.last_ref, f32[16,512]{1,0:T(8,128)S(1)} %copy-done.1, f32[5,512]{1,0:T(8,128)S(1)} %copy-done.3, ...), custom_call_target="tpu_custom_call" | custom-call | flops 113246208 | bytes 2730048 | tf_op jit(solution)/shard_map/mix/pallas_call | solution.py:64
  48.2 4.0 %all-to-all-start.2 = ((bf16[4,64,1408]{2,1,0:T(8,128)(2,1)}), bf16[4,64,1408]{2,1,0:T(8,128)(2,1)S(1)}, u32[]{:S(2)}, u32[]{:S(2)}) async-start(bf16[4,64,1408]{2,1,0:T(8,128)(2,1)} %get-tuple-element.9), calls=%async_computation.2 | async-start | bytes 1441792 | tf_op jit(solution)/shard_map/all_to_all | solution.py:305
  52.2 0.0 copy-done.17
  52.2 0.1 reshape.97.reward_ref
  52.3 9.4 %all-to-all-done.2.got_ref = bf16[4,64,1408]{2,1,0:T(8,128)(2,1)S(1)} async-done(((bf16[4,64,1408]{2,1,0:T(8,128)(2,1)}), bf16[4,64,1408]{2,1,0:T(8,128)(2,1)S(1)}, u32[]{:S(2)}, u32[]{:S(2)}) %all-to-all-start.2) | async-done | bytes 720928 | tf_op jit(solution)/shard_map/all_to_all | solution.py:305
  61.6 0.1 broadcast_in_dim.62.live_ref
  61.7 0.0 copy-done.4
  61.7 0.0 copy-done.5
  61.7 0.0 copy-done.6
  61.7 0.0 copy-done.7
  61.7 0.0 copy-done.8
  61.7 0.0 copy-done.9
  61.8 0.0 copy-done.10
  61.8 0.0 copy-done.11
  61.8 0.0 copy-done.12
  61.8 0.0 copy-start.16
  61.8 0.0 copy-start.2
  61.8 0.0 copy-start
  61.8 6.6 %state.1 = (f32[1024,128]{1,0:T(8,128)}, f32[64,128]{1,0:T(8,128)S(1)}, f32[64,128]{1,0:T(8,128)S(1)}, f32[4,64,128]{2,1,0:T(8,128)}) custom-call(bf16[4,64,1408]{2,1,0:T(8,128)(2,1)S(1)} %all-to-all-done.2.got_ref, f32[64,128]{1,0:T(8,128)S(1)} %broadcast_in_dim.62.live_ref, f32[1024,128]{1,0:T(8,128)S(1)} %bitcast.36, bf16[96,512]{1,0:T(8,128)(2,1)S(1)} %copy-done.5, ...), custom_call_target="tpu_custom_call" | custom-call | flops 805306368 | bytes 2500608 | tf_op jit(solution)/shard_map/state/pallas_call | solution.py:64
  68.5 3.3 %all-to-all-start.3 = ((f32[4,64,128]{2,1,0:T(8,128)}), f32[4,64,128]{2,1,0:T(8,128)S(1)}, u32[]{:S(2)}, u32[]{:S(2)}) async-start(f32[4,64,128]{2,1,0:T(8,128)} %get-tuple-element.10), calls=%async_computation.3 | async-start | bytes 262144 | tf_op jit(solution)/shard_map/all_to_all | solution.py:334
  71.8 0.1 copy.41
  71.9 0.1 copy.42
  72.0 0.1 reshape.99.gain_ref
  72.0 4.5 %all-to-all-done.3.stat_ref = f32[4,64,128]{2,1,0:T(8,128)S(1)} async-done(((f32[4,64,128]{2,1,0:T(8,128)}), f32[4,64,128]{2,1,0:T(8,128)S(1)}, u32[]{:S(2)}, u32[]{:S(2)}) %all-to-all-start.3) | async-done | bytes 131104 | tf_op jit(solution)/shard_map/all_to_all | solution.py:334
  76.6 0.8 norm.1
  77.4 19.1 %all_to_all.30.got_ref = bf16[32,4,128]{2,1,0:T(4,128)(2,1)S(1)} all-to-all(bf16[32,4,128]{2,1,0:T(4,128)(2,1)S(1)} %norm.1), channel_id=1, replica_groups=mesh['req'=32,'head'=4,'row'=4] {'req'}, dimensions={0} | all-to-all | bytes 65536 | tf_op jit(solution)/shard_map/all_to_all | solution.py:344
  96.5 0.8 output.1
  97.3 10.3 %all_to_all.31 = bf16[16,16,512]{2,1,0:T(8,128)(2,1)S(1)} all-to-all(bf16[16,16,512]{2,1,0:T(8,128)(2,1)S(1)} %output.1), channel_id=1, replica_groups=mesh['req'=32,'head'=4,'row'=4] {'head','row'}, dimensions={0} | all-to-all | bytes 524288 | tf_op jit(solution)/shard_map/all_to_all | solution.py:354
  107.6 0.6 reshape.101
  (14 shorter events, 0.1 us)
Async XLA Ops:
  0.6 31.2 %copy-start.14 = (bf16[512,96]{0,1:T(8,128)(2,1)S(1)}, bf16[512,96]{0,1:T(8,128)(2,1)}, u32[]{:S(2)}) copy-start(bf16[512,96]{0,1:T(8,128)(2,1)} %param.30) | copy-start | bytes 294916
  0.6 31.3 %copy-start.15 = (bf16[512,96]{0,1:T(8,128)(2,1)S(1)}, bf16[512,96]{0,1:T(8,128)(2,1)}, u32[]{:S(2)}) copy-start(bf16[512,96]{0,1:T(8,128)(2,1)} %param.33) | copy-start | bytes 294916
  2.0 30.1 %copy-start.18 = (bf16[512,512]{1,0:T(8,128)(2,1)S(1)}, bf16[512,512]{1,0:T(8,128)(2,1)}, u32[]{:S(2)}) copy-start(bf16[512,512]{1,0:T(8,128)(2,1)} %constant.52.clone) | copy-start | bytes 1572868
  2.0 9.6 %all-to-all-start = ((bf16[4,4,16,128]{3,2,1,0:T(8,128)(2,1)}), bf16[4,4,16,128]{3,2,1,0:T(8,128)(2,1)S(1)}, u32[]{:S(2)}, u32[]{:S(2)}) async-start(bf16[4,4,16,128]{3,2,1,0:T(8,128)(2,1)} %broadcast_in_dim.59), calls=%async_computation | async-start | bytes 131072 | tf_op jit(solution)/shard_map/all_to_all | solution.py:285
  12.9 33.2 %all-to-all-start.1 = ((bf16[32,16,128]{2,1,0:T(8,128)(2,1)}), bf16[32,16,128]{2,1,0:T(8,128)(2,1)S(1)}, u32[]{:S(2)}, u32[]{:S(2)}) async-start(bf16[32,16,128]{2,1,0:T(8,128)(2,1)} %pack.1), calls=%async_computation.1 | async-start | bytes 262144 | tf_op jit(solution)/shard_map/all_to_all | solution.py:289
  31.8 14.3 %copy-start.1 = (f32[16,512]{1,0:T(8,128)S(1)}, f32[16,512]{1,0:T(8,128)}, u32[]{:S(2)}) copy-start(f32[16,512]{1,0:T(8,128)} %shift_ref.1) | copy-start | bytes 98308
  31.8 14.3 %copy-start.3 = (f32[5,512]{1,0:T(8,128)S(1)}, f32[5,512]{1,0:T(8,128)}, u32[]{:S(2)}) copy-start(f32[5,512]{1,0:T(8,128)} %blend_ref.1) | copy-start | bytes 30724
  46.2 6.0 %copy-start.17 = (f32[8,64]{1,0:T(8,128)S(1)}, f32[8,64]{1,0:T(8,128)}, u32[]{:S(2)}) copy-start(f32[8,64]{1,0:T(8,128)} %param.38) | copy-start | bytes 6148
  46.2 15.5 %copy-start.4 = (f32[16,8,1024]{2,1,0:T(8,128)S(1)}, f32[16,8,1024]{2,1,0:T(8,128)}, u32[]{:S(2)}) copy-start(f32[16,8,1024]{2,1,0:T(8,128)} %param.26) | copy-start | bytes 1572868
  46.2 15.5 %copy-start.5 = (bf16[96,512]{1,0:T(8,128)(2,1)S(1)}, bf16[96,512]{1,0:T(8,128)(2,1)}, u32[]{:S(2)}) copy-start(bf16[96,512]{1,0:T(8,128)(2,1)} %decay_ref.2) | copy-start | bytes 294916
  46.2 15.5 %copy-start.6 = (bf16[96,512]{1,0:T(8,128)(2,1)S(1)}, bf16[96,512]{1,0:T(8,128)(2,1)}, u32[]{:S(2)}) copy-start(bf16[96,512]{1,0:T(8,128)(2,1)} %learn_ref.2) | copy-start | bytes 294916
  46.2 15.5 %copy-start.7 = (f32[512]{0:T(512)S(1)}, f32[512]{0:T(512)}, u32[]{:S(2)}) copy-start(f32[512]{0:T(512)} %param.32) | copy-start | bytes 6148
  46.2 15.5 %copy-start.8 = (f32[512]{0:T(512)S(1)}, f32[512]{0:T(512)}, u32[]{:S(2)}) copy-start(f32[512]{0:T(512)} %param.35) | copy-start | bytes 6148
  46.2 15.5 %copy-start.9 = (f32[512]{0:T(512)S(1)}, f32[512]{0:T(512)}, u32[]{:S(2)}) copy-start(f32[512]{0:T(512)} %param.36) | copy-start | bytes 6148
  46.2 15.5 %copy-start.10 = (f32[512]{0:T(512)S(1)}, f32[512]{0:T(512)}, u32[]{:S(2)}) copy-start(f32[512]{0:T(512)} %param.37) | copy-start | bytes 6148
  46.3 15.5 %copy-start.11 = (bf16[256,256]{1,0:T(8,128)(2,1)S(1)}, bf16[256,256]{1,0:T(8,128)(2,1)}, u32[]{:S(2)}) copy-start(bf16[256,256]{1,0:T(8,128)(2,1)} %constant.48.clone.halves_ref) | copy-start | bytes 393220
  46.3 15.5 %copy-start.12 = (bf16[512,128]{1,0:T(8,128)(2,1)S(1)}, bf16[512,128]{1,0:T(8,128)(2,1)}, u32[]{:S(2)}) copy-start(bf16[512,128]{1,0:T(8,128)(2,1)} %constant.50.clone.head_to_lanes_ref) | copy-start | bytes 393220
  46.3 15.5 %copy-start.13 = (bf16[128,128]{1,0:T(8,128)(2,1)S(1)}, bf16[128,128]{1,0:T(8,128)(2,1)}, u32[]{:S(2)}) copy-start(bf16[128,128]{1,0:T(8,128)(2,1)} %constant.49.clone.same_head_ref) | copy-start | bytes 98308
  48.2 13.4 %all-to-all-start.2 = ((bf16[4,64,1408]{2,1,0:T(8,128)(2,1)}), bf16[4,64,1408]{2,1,0:T(8,128)(2,1)S(1)}, u32[]{:S(2)}, u32[]{:S(2)}) async-start(bf16[4,64,1408]{2,1,0:T(8,128)(2,1)} %get-tuple-element.9), calls=%async_computation.2 | async-start | bytes 1441792 | tf_op jit(solution)/shard_map/all_to_all | solution.py:305
  61.8 10.0 %copy-start.16 = (f32[8,16]{1,0:T(8,128)S(1)}, f32[8,16]{1,0:T(8,128)}, u32[]{:S(2)}) copy-start(f32[8,16]{1,0:T(8,128)} %param.39) | copy-start | bytes 1540
  61.8 14.8 %copy-start.2 = (bf16[128,128]{1,0:T(8,128)(2,1)S(1)}, bf16[128,128]{1,0:T(8,128)(2,1)}, u32[]{:S(2)}) copy-start(bf16[128,128]{1,0:T(8,128)(2,1)} %constant.51.clone.to_natural_ref) | copy-start | bytes 98308
  61.8 34.7 %copy-start = (bf16[8,16,2048]{2,1,0:T(8,128)(2,1)S(1)}, bf16[8,16,2048]{2,1,0:T(8,128)(2,1)}, u32[]{:S(2)}) copy-start(bf16[8,16,2048]{2,1,0:T(8,128)(2,1)} %param.40) | copy-start | bytes 1572868
  68.5 8.1 %all-to-all-start.3 = ((f32[4,64,128]{2,1,0:T(8,128)}), f32[4,64,128]{2,1,0:T(8,128)S(1)}, u32[]{:S(2)}, u32[]{:S(2)}) async-start(f32[4,64,128]{2,1,0:T(8,128)} %get-tuple-element.10), calls=%async_computation.3 | async-start | bytes 262144 | tf_op jit(solution)/shard_map/all_to_all | solution.py:334

commit v2 on v1

--- a/solution.py
+++ b/solution.py
@@ -24,6 +24,7 @@
 BF16 = jnp.bfloat16
 VMEM = pl.BlockSpec(memory_space=pltpu.VMEM)
 SMEM = pl.BlockSpec(memory_space=pltpu.SMEM)
+ANY = pl.BlockSpec(memory_space=pl.ANY)
 
 
 def value_lane(head, row):
@@ -44,7 +45,10 @@
             to_natural[value_lane(head, row), head * ROWS + row] = 1
             for part in range(4):
                 spread_values[head * 64 + part * ROWS + row, part * VALS + value_lane(head, row)] = 1
-    return halves, same_head, head_to_lanes, to_natural, spread_values
+    unpack = np.zeros((LANES, 2, LANES), np.float32)
+    for side in range(2):
+        unpack[side * 64:(side + 1) * 64, side] = same_head[side * 64:(side + 1) * 64]
+    return halves, same_head, head_to_lanes, to_natural, spread_values, unpack.reshape(LANES, 256)
 
 
 def dot(a, b):
@@ -57,7 +61,7 @@
     return dot(high, b) + dot(low, b)
 
 
-def call(kernel, outs, in_specs, args, scratch=(), flops=0, name=None):
+def call(kernel, outs, in_specs, args, scratch=(), flops=0, name=None, out_spec=VMEM):
     size = sum(int(np.prod(a.shape)) * a.dtype.itemsize for a in args)
     size += sum(int(np.prod(o.shape)) * o.dtype.itemsize for o in outs)
     single = len(outs) == 1
@@ -65,7 +69,7 @@
         kernel,
         out_shape=outs[0] if single else outs,
         in_specs=in_specs,
-        out_specs=VMEM if single else [VMEM] * len(outs),
+        out_specs=out_spec if single else [out_spec] * len(outs),
         scratch_shapes=list(scratch),
         cost_estimate=pl.CostEstimate(flops=flops, bytes_accessed=size, transcendentals=0),
         compiler_params=pltpu.CompilerParams(vmem_limit_bytes=32 * 2**20),
@@ -73,9 +77,23 @@
     )(*args)
 
 
-def pack_kernel(dest_ref, x_ref, out_ref):
-    for q in range(REQ_DEV):
-        out_ref[dest_ref[q]] = x_ref[q]
+def fan_kernel(x_ref, out_ref, done):
+    copies = [pltpu.make_async_copy(x_ref, out_ref.at[at], done.at[at]) for at in range(4)]
+    for copy in copies:
+        copy.start()
+    for copy in copies:
+        copy.wait()
+
+
+def pack_kernel(dest_ref, x_ref, out_ref, done):
+    copies = [
+        pltpu.make_async_copy(x_ref.at[q], out_ref.at[dest_ref[q]], done.at[q])
+        for q in range(REQ_DEV)
+    ]
+    for copy in copies:
+        copy.start()
+    for copy in copies:
+        copy.wait()
 
 
 def mix_kernel(
@@ -113,16 +131,26 @@
 def state_kernel(
     got_ref, live_ref, state_ref, decay_ref, decay_offset_ref, learn_ref, learn_offset_ref, gain_ref,
     correction_ref, reward_ref, halves_ref, same_head_ref, head_to_lanes_ref,
-    new_state_ref, reading_ref, bonus_ref, stat_ref, spread, states,
+    new_state_ref, reading_ref, bonus_ref, stat_ref, spread, states, factors,
 ):
+    lane = lax.broadcasted_iota(jnp.int32, (REQ_DEV, 256), 1)
+    lane_key = lane % 64 - lane // 128
+    for head in range(HEADS):
+        for quad in range(4):
+            at = (head * 4 + quad) * REQ_DEV
+            for half in range(2):
+                for group in range(2):
+                    start = group * 512 + (quad * 2 + half) * 8 + head
+                    states[at + group * 8:at + group * 8 + 8, half * LANES:(half + 1) * LANES] = (
+                        state_ref[pl.ds(start, 8, stride=64), :]
+                    )
     total = got_ref[0].astype(F32)
     for part in range(1, 4):
         total = total + got_ref[part].astype(F32)
     recept = total[:, 0:FEATS]
     key = total[:, FEATS:2 * FEATS]
     value = total[:, 2 * FEATS:DECAY_AT]
-    rank = decay_ref.shape[0]
-    decay_low = jnp.tanh(total[:, DECAY_AT:DECAY_AT + rank]).astype(BF16)
+    decay_low = jnp.tanh(total[:, DECAY_AT:DECAY_AT + decay_ref.shape[0]]).astype(BF16)
     learn_low = total[:, LEARN_AT:LEARN_AT + learn_ref.shape[0]].astype(BF16)
     decay_in = decay_offset_ref[...] + dot(decay_low, decay_ref[...])
     learn = jax.nn.sigmoid(learn_offset_ref[...] + dot(learn_low, learn_ref[...]))
@@ -130,15 +158,12 @@
     halves = halves_ref[...]
     scaled = key * gain_ref[...]
     squares = scaled * scaled
-    norm = jnp.concatenate(
-        [dot_split(squares[:, 0:256], halves), dot_split(squares[:, 256:512], halves)], axis=1
-    )
+    norm = dot_split(jnp.concatenate([squares[:, 0:256], squares[:, 256:512]], axis=0), halves)
+    norm = jnp.concatenate([norm[0:TOK], norm[TOK:2 * TOK]], axis=1)
     key_dir = scaled * lax.rsqrt(norm + 1e-6)
     key_adj = key * (1.0 + (learn - 1.0) * correction_ref[...])
     live = live_ref[...]
     live_wide = jnp.concatenate([live] * 4, axis=1)
-    reward = dot_split(recept * key_adj * reward_ref[...], head_to_lanes_ref[...])
-    bonus_ref[...] = reward * value * live
     vectors = [
         key_dir,
         jnp.where(live_wide > 0, decay, 1.0),
@@ -153,75 +178,89 @@
             turned = pltpu.roll(block, 64, 1)
             spread[at, 2 * pair] = jnp.where(low_half, block, turned)
             spread[at, 2 * pair + 1] = jnp.where(low_half, turned, block)
-    lane = lax.broadcasted_iota(jnp.int32, (REQ_DEV, 256), 1)
-    lane_key = lane % 64 - lane // 128
     value_pair = jnp.concatenate([value, value], axis=1)
-    for head in range(HEADS):
-        for quad in range(4):
-            at = (head * 4 + quad) * REQ_DEV
-            for half in range(2):
-                for group in range(2):
-                    start = group * 512 + (quad * 2 + half) * 8 + head
-                    states[at + group * 8:at + group * 8 + 8, half * LANES:(half + 1) * LANES] = (
-                        state_ref[pl.ds(start, 8, stride=64), :]
-                    )
-    for t in range(TS):
-        rows = slice(t * REQ_DEV, (t + 1) * REQ_DEV)
-        value_now = value_pair[rows]
-        reading = jnp.zeros((REQ_DEV, LANES), F32)
+    masks = [[lane_key == head * 8 + 2 * quad for quad in range(4)] for head in range(HEADS)]
+
+    def vector_at(at, head, t):
+        row = spread[at, head, t * REQ_DEV:(t + 1) * REQ_DEV, :]
+        return jnp.concatenate([jnp.concatenate([row, row], axis=1)] * 4, axis=0)
+
+    for t in range(TS + 1):
         for head in range(HEADS):
-            direction, keep, remove, add, query = [
-                jnp.concatenate([jnp.concatenate([spread[at, head, rows, :]] * 2, axis=1)] * 4, axis=0)
-                for at in range(5)
-            ]
-            masks = [lane_key == head * 8 + 2 * quad for quad in range(4)]
             place = slice(head * 64, (head + 1) * 64)
             state = states[place, :]
-            removed = dot((state * direction).astype(BF16), halves)
-            values = jnp.concatenate([jnp.where(m, value_now, 0.0) for m in masks], axis=0)
-            spread_value = dot(values.astype(BF16), halves)
-            state = state * keep - removed * remove + spread_value * add
-            if t < TS - 1:
-                states[place, :] = state
-            else:
+            if t > 0:
+                removed = product[head * 64:(head + 1) * 64]
+                added = product[512 + head * 64:512 + (head + 1) * 64]
+                state = (
+                    state * vector_at(1, head, t - 1)
+                    - removed * vector_at(2, head, t - 1)
+                    + added * vector_at(3, head, t - 1)
+                )
+                if t < TS:
+                    states[place, :] = state
+                else:
+                    for quad in range(4):
+                        for half in range(2):
+                            for group in range(2):
+                                at = quad * REQ_DEV + group * 8
+                                start = group * 512 + (quad * 2 + half) * 8 + head
+                                new_state_ref[pl.ds(start, 8, stride=64), :] = state[
+                                    at:at + 8, half * LANES:(half + 1) * LANES
+                                ]
+                query = (state * vector_at(4, head, t - 1)).astype(BF16)
+                factors[1024 + head * 64:1024 + (head + 1) * 64, :] = query
+            if t < TS:
+                factors[place, :] = (state * vector_at(0, head, t)).astype(BF16)
+                now = value_pair[t * REQ_DEV:(t + 1) * REQ_DEV]
+                picked = jnp.concatenate([jnp.where(m, now, 0.0) for m in masks[head]], axis=0)
+                factors[512 + head * 64:512 + (head + 1) * 64, :] = picked.astype(BF16)
+        first = 0 if t < TS else 1024
+        last = 1536 if t > 0 else 1024
+        product = dot(factors[first:last, :], halves)
+        if t > 0:
+            read = product[1024 - first:]
+            reading = jnp.zeros((REQ_DEV, LANES), F32)
+            for head in range(HEADS):
                 for quad in range(4):
-                    for half in range(2):
-                        for group in range(2):
-                            at = quad * REQ_DEV + group * 8
-                            start = group * 512 + (quad * 2 + half) * 8 + head
-                            new_state_ref[pl.ds(start, 8, stride=64), :] = state[
-                                at:at + 8, half * LANES:(half + 1) * LANES
-                            ]
-            read = dot((state * query).astype(BF16), halves)
-            for quad in range(4):
-                part = jnp.where(masks[quad], read[quad * REQ_DEV:(quad + 1) * REQ_DEV], 0.0)
-                reading = reading + part[:, 0:LANES] + part[:, LANES:256]
-        reading_ref[rows, :] = reading
+                    at = (head * 4 + quad) * REQ_DEV
+                    part = jnp.where(masks[head][quad], read[at:at + REQ_DEV], 0.0)
+                    reading = reading + part[:, 0:LANES] + part[:, LANES:256]
+            reading_ref[(t - 1) * REQ_DEV:t * REQ_DEV, :] = reading
+    reward = dot_split(recept * key_adj * reward_ref[...], head_to_lanes_ref[...])
+    bonus_ref[...] = reward * value * live
     reading = reading_ref[...]
     same_head = same_head_ref[...]
     head_sum = dot_split(reading, same_head)
     away = reading - head_sum * (1.0 / ROWS)
     away_sum = dot_split(away * away, same_head)
     stat = jnp.where(low_half, head_sum, away_sum)
+    slot = lax.broadcasted_iota(jnp.int32, (8, LANES), 1) % 8
+    packed = jnp.zeros((8, LANES), F32)
+    for group in range(8):
+        packed = packed + jnp.where(slot == group, stat[group * 8:(group + 1) * 8], 0.0)
     for part in range(4):
-        stat_ref[part] = stat
-
-
-def norm_kernel(source_ref, stat_ref, reading_ref, bonus_ref, gain_ref, to_natural_ref, out_ref, rows):
-    low_half = lax.broadcasted_iota(jnp.int32, (TOK, LANES), 1) < 64
-    sums, squares = [], []
+        stat_ref[part] = packed
+
+
+def norm_kernel(source_ref, stat_ref, reading_ref, bonus_ref, gain_ref, unpack_ref, to_natural_ref, out_ref, rows):
+    lane = lax.broadcasted_iota(jnp.int32, (8, LANES), 1)
+    stats = [stat_ref[part] for part in range(4)]
+    mean = (stats[0] + stats[1] + stats[2] + stats[3]) * (1.0 / CHANNEL_SPAN)
+    away = pltpu.roll(stats[0] + stats[1] + stats[2] + stats[3], 64, 1)
     for part in range(4):
-        stat = stat_ref[part]
-        turned = pltpu.roll(stat, 64, 1)
-        sums.append(jnp.where(low_half, stat, turned))
-        squares.append(jnp.where(low_half, turned, stat))
-    mean = (sums[0] + sums[1] + sums[2] + sums[3]) * (1.0 / CHANNEL_SPAN)
-    spread = squares[0] + squares[1] + squares[2] + squares[3]
-    for part in range(4):
-        gap = sums[part] * (1.0 / ROWS) - mean
-        spread = spread + gap * gap * float(ROWS)
-    scale = lax.rsqrt(spread * (1.0 / CHANNEL_SPAN) + 0.00064)
-    normed = (reading_ref[...] - mean) * scale * gain_ref[...] + bonus_ref[...]
+        gap = stats[part] * (1.0 / ROWS) - mean
+        away = away + gap * gap * float(ROWS)
+    scale = lax.rsqrt(jnp.where(lane < 64, away, 0.0) * (1.0 / CHANNEL_SPAN) + 0.00064)
+    both = jnp.where(lane < 64, mean, pltpu.roll(scale, 64, 1))
+    packed = jnp.concatenate([jnp.where(lane % 8 == group, both, 0.0) for group in range(8)], axis=0)
+    high = packed.astype(BF16)
+    rest = packed - high.astype(F32)
+    middle = rest.astype(BF16)
+    low = (rest - middle.astype(F32)).astype(BF16)
+    opened = dot(jnp.concatenate([high, middle, low], axis=0), unpack_ref[...])
+    opened = opened[0:TOK] + opened[TOK:2 * TOK] + opened[2 * TOK:3 * TOK]
+    normed = (reading_ref[...] - opened[:, 0:LANES]) * opened[:, LANES:256] * gain_ref[...] + bonus_ref[...]
     rows[...] = dot(normed.astype(BF16), to_natural_ref[...])
     for page in range(REQ_DEV):
         out_ref[source_ref[page]] = rows[pl.ds(page, TS, stride=REQ_DEV), :].astype(BF16)
@@ -263,7 +302,7 @@
     final_projector,
 ):
     groups = lax.axis_size("req")
-    halves, same_head, head_to_lanes, to_natural, spread_values = [
+    halves, same_head, head_to_lanes, to_natural, spread_values, unpack = [
         jnp.asarray(m, BF16) for m in constant_matrices()
     ]
     first = lax.axis_index("req") * REQ_DEV
@@ -281,10 +320,24 @@
     live, last = live.reshape(TOK, LANES), last.reshape(TOK, LANES)
 
     tiles = incoming_activations.reshape(4, TS, 4, LANES).transpose(0, 2, 1, 3).reshape(4, 16, LANES)
-    everywhere = jnp.broadcast_to(tiles[None], (4, 4, 16, LANES))
+    everywhere = call(
+        fan_kernel,
+        [shaped((4, 4, 16, LANES), BF16)],
+        [ANY],
+        (tiles,),
+        scratch=[pltpu.SemaphoreType.DMA((4,))],
+        name="fan",
+        out_spec=ANY,
+    )
     mine = lax.all_to_all(everywhere, "head", 0, 0, tiled=True).reshape(REQ_DEV, 16, LANES)
     packed = call(
-        pack_kernel, [shaped((groups, 16, LANES), BF16)], [SMEM, VMEM], (dest, mine), name="pack"
+        pack_kernel,
+        [shaped((groups, 16, LANES), BF16)],
+        [SMEM, ANY],
+        (dest, mine),
+        scratch=[pltpu.SemaphoreType.DMA((REQ_DEV,))],
+        name="pack",
+        out_spec=ANY,
     )
     got = lax.all_to_all(packed, "req", 0, 0, tiled=True)
     value_projector = dot(first_projectors[2], spread_values).astype(BF16)
@@ -309,7 +362,7 @@
             shaped((REQ_DEV * HEADS * 8, LANES), F32),
             shaped((TOK, LANES), F32),
             shaped((TOK, LANES), F32),
-            shaped((4, TOK, LANES), F32),
+            shaped((4, 8, LANES), F32),
         ],
         [VMEM] * 13,
         (
@@ -327,7 +380,7 @@
             same_head,
             head_to_lanes,
         ),
-        scratch=[pltpu.VMEM((5, HEADS, TOK, LANES), F32), pltpu.VMEM((512, 256), F32)],
+        scratch=[pltpu.VMEM((5, HEADS, TOK, LANES), F32), pltpu.VMEM((512, 256), F32), pltpu.VMEM((1536, 256), BF16)],
         flops=2 * 3 * TS * 512 * 256 * 256,
         name="state",
     )
@@ -336,8 +389,8 @@
     leaving = call(
         norm_kernel,
         [shaped((groups, TS, LANES), BF16)],
-        [SMEM] + [VMEM] * 5,
-        (source, stats, reading, bonus, gain, to_natural),
+        [SMEM] + [VMEM] * 6,
+        (source, stats, reading, bonus, gain, unpack, to_natural),
         scratch=[pltpu.VMEM((TOK, LANES), F32)],
         name="norm",
     )

time: 109 us -> 105 us (0.963)
  Pallas kernels: 11.3 us -> 8.7 us
    pallas_call x5 -> x6, Pallas kernels: 11.3 us -> 8.7 us  [call(): pl.pallas_call(kernel, out_shape=outs[0] if single else outs, in_specs=in...]
    broadcast_in_dim x1 -> x0, local copies, waits for them, and re-layouts: 1.39 us -> none  [per_device(): everywhere = jnp.broadcast_to(tiles[None], (4, 4, 16, LANES))]
where the time goes in v2:
time: 105 us; the launch traced here: 104 us
  starting transfers between devices  29.8 us (28%)
  blocking collectives  29.3 us (28%)
  waiting for transfers between devices  28.5 us (27%)
  Pallas kernels  8.7 us (8%)
  local copies, waits for them, and re-layouts  3.7 us (4%)
  other arithmetic  1.72 us (2%)
  matrix products  1.48 us (1%)
    all_to_all x1, blocking collectives, per_device(): back = lax.all_to_all(leaving, 'req', 0, 0, tiled=True)  19.1 us
    all_to_all x1, starting transfers between devices, per_device(): got = lax.all_to_all(packed, 'req', 0, 0, tiled=True)  17.4 us
    all_to_all x1, waiting for transfers between devices, per_device(): got = lax.all_to_all(packed, 'req', 0, 0, tiled=True)  12.4 us
    all_to_all x1, blocking collectives, per_device(): arrived = lax.all_to_all(terms, ('head', 'row'), 0, 0, tiled=True)  10.3 us
    all_to_all x1, waiting for transfers between devices, per_device(): sums = lax.all_to_all(partial, 'row', 0, 0, tiled=True)  9.33 us
    pallas_call x6, Pallas kernels, call(): pl.pallas_call(kernel, out_shape=outs[0] if single else outs, in_specs=in...  8.7 us
    all_to_all x1, starting transfers between devices, per_device(): lax.all_to_all(everywhere, 'head', 0, 0, tiled=True)  5.16 us
    all_to_all x1, starting transfers between devices, per_device(): sums = lax.all_to_all(partial, 'row', 0, 0, tiled=True)  4.01 us
  transfers between devices with their start and end apart: 4, of which 4 were waited for; matrix products, arithmetic and copies ran while one was open for 5% of the time, Pallas kernels for 0%

profile of v2, /device:TPU:1, one launch (start us, length us, event | category | flops | bytes accessed | tf_op | source)
XLA Modules:
  0.0 104.2 jit_solution(10619750718120398397)
XLA Ops:
  0.6 0.0 copy-start.5
  0.6 0.7 copy-done.5
  1.4 0.7 fan.1
  2.0 0.0 copy-start.20
  2.0 5.2 %all-to-all-start = ((bf16[4,4,16,128]{3,2,1,0:T(8,128)(2,1)}), bf16[4,4,16,128]{3,2,1,0:T(8,128)(2,1)S(1)}, u32[]{:S(2)}, u32[]{:S(2)}) async-start(bf16[4,4,16,128]{3,2,1,0:T(8,128)(2,1)} %fan.1), calls=%async_computation | async-start | bytes 131072 | tf_op jit(solution)/shard_map/all_to_all | solution.py:332
  7.2 0.9 fusion.4
  8.1 0.8 and_select_fusion.1.dest_ref
  8.8 2.8 %all-to-all-done = bf16[4,4,16,128]{3,2,1,0:T(8,128)(2,1)S(1)} async-done(((bf16[4,4,16,128]{3,2,1,0:T(8,128)(2,1)}), bf16[4,4,16,128]{3,2,1,0:T(8,128)(2,1)S(1)}, u32[]{:S(2)}, u32[]{:S(2)}) %all-to-all-start) | async-done | bytes 65568 | tf_op jit(solution)/shard_map/all_to_all | solution.py:332
  11.7 1.3 %pack.1 = bf16[32,16,128]{2,1,0:T(8,128)(2,1)} custom-call(s32[16]{0:T(128)S(1)} %and_select_fusion.1.dest_ref, bf16[16,16,128]{2,1,0:T(8,128)(2,1)S(1)} %bitcast.35), custom_call_target="tpu_custom_call" | custom-call | bytes 196672 | tf_op jit(solution)/shard_map/pack/pallas_call | solution.py:68
  13.0 17.4 %all-to-all-start.1 = ((bf16[32,16,128]{2,1,0:T(8,128)(2,1)}), bf16[32,16,128]{2,1,0:T(8,128)(2,1)S(1)}, u32[]{:S(2)}, u32[]{:S(2)}) async-start(bf16[32,16,128]{2,1,0:T(8,128)(2,1)} %pack.1), calls=%async_computation.1 | async-start | bytes 262144 | tf_op jit(solution)/shard_map/all_to_all | solution.py:342
  30.4 0.1 eq.44
  30.5 0.1 lt.22
  30.6 0.1 eq.42
  30.7 1.3 %slice.6.proj_ref = bf16[2,512,512]{2,1,0:T(8,128)(2,1)S(1)} slice(bf16[3,512,512]{2,1,0:T(8,128)(2,1)} %param.30), slice={[0:2], [0:512], [0:512]} | slice | bytes 2097152 | tf_op jit(solution)/shard_map/slice | solution.py:349
  32.0 0.0 copy-done.16
  32.0 0.0 copy-start.2
  32.0 0.0 copy-start.4
  32.0 0.1 copy.35.decay_ref
  32.1 0.0 copy-done.17
  32.1 0.1 copy.36.learn_ref
  32.3 0.0 copy-done.20
  32.3 1.5 %fusion.value_ref = bf16[512,512]{1,0:T(8,128)(2,1)S(1)} fusion(bf16[512,512]{1,0:T(8,128)(2,1)S(1)} %copy-done.20, bf16[3,512,512]{2,1,0:T(8,128)(2,1)} %param.30), kind=kOutput, calls=%fused_computation.1 | convolution fusion | flops 268697600 | bytes 1572864 | tf_op jit(solution)/shard_map/dot_general | solution.py:55
  33.8 12.4 %all-to-all-done.1.got_ref = bf16[32,16,128]{2,1,0:T(8,128)(2,1)S(1)} async-done(((bf16[32,16,128]{2,1,0:T(8,128)(2,1)}), bf16[32,16,128]{2,1,0:T(8,128)(2,1)S(1)}, u32[]{:S(2)}, u32[]{:S(2)}) %all-to-all-start.1) | async-done | bytes 131104 | tf_op jit(solution)/shard_map/all_to_all | solution.py:342
  46.2 0.1 broadcast_in_dim.52.last_ref
  46.3 0.0 copy-done.2
  46.3 0.0 copy-done.4
  46.3 0.0 copy-start.6
  46.3 0.0 copy-start.7
  46.3 0.0 copy-start.8
  46.3 0.0 copy-start.9
  46.4 0.0 copy-start.10
  46.4 0.0 copy-start.11
  46.4 0.0 copy-start.12
  46.4 0.0 copy-start.13
  46.4 0.0 copy-start.14
  46.4 0.0 copy-start.15
  46.4 1.9 %mix.1 = (bf16[4,64,1408]{2,1,0:T(8,128)(2,1)}, f32[16,512]{1,0:T(8,128)}) custom-call(s32[16]{0:T(128)S(1)} %and_select_fusion.source_ref, bf16[32,16,128]{2,1,0:T(8,128)(2,1)S(1)} %all-to-all-done.1.got_ref, f32[64,128]{1,0:T(8,128)S(1)} %broadcast_in_dim.52.last_ref, f32[16,512]{1,0:T(8,128)S(1)} %copy-done.2, f32[5,512]{1,0:T(8,128)S(1)} %copy-done.4, ...), custom_call_target="tpu_custom_call" | custom-call | flops 113246208 | bytes 2730048 | tf_op jit(solution)/shard_map/mix/pallas_call | solution.py:68
  48.3 4.0 %all-to-all-start.2 = ((bf16[4,64,1408]{2,1,0:T(8,128)(2,1)}), bf16[4,64,1408]{2,1,0:T(8,128)(2,1)S(1)}, u32[]{:S(2)}, u32[]{:S(2)}) async-start(bf16[4,64,1408]{2,1,0:T(8,128)(2,1)} %get-tuple-element.9), calls=%async_computation.2 | async-start | bytes 1441792 | tf_op jit(solution)/shard_map/all_to_all | solution.py:358
  52.3 0.0 copy-done.19
  52.3 0.0 copy-start.3
  52.4 0.1 reshape.100.reward_ref
  52.4 9.3 %all-to-all-done.2.got_ref = bf16[4,64,1408]{2,1,0:T(8,128)(2,1)S(1)} async-done(((bf16[4,64,1408]{2,1,0:T(8,128)(2,1)}), bf16[4,64,1408]{2,1,0:T(8,128)(2,1)S(1)}, u32[]{:S(2)}, u32[]{:S(2)}) %all-to-all-start.2) | async-done | bytes 720928 | tf_op jit(solution)/shard_map/all_to_all | solution.py:358
  61.8 0.1 broadcast_in_dim.53.live_ref
  61.8 0.0 copy-done.6
  61.8 0.0 copy-done.7
  61.8 0.0 copy-done.8
  61.8 0.0 copy-done.9
  61.9 0.0 copy-done.10
  61.9 0.0 copy-done.11
  61.9 0.0 copy-done.12
  61.9 0.0 copy-start
  61.9 3.1 %state.1 = (f32[1024,128]{1,0:T(8,128)}, f32[64,128]{1,0:T(8,128)S(1)}, f32[64,128]{1,0:T(8,128)S(1)}, f32[4,8,128]{2,1,0:T(8,128)}) custom-call(bf16[4,64,1408]{2,1,0:T(8,128)(2,1)S(1)} %all-to-all-done.2.got_ref, f32[64,128]{1,0:T(8,128)S(1)} %broadcast_in_dim.53.live_ref, f32[1024,128]{1,0:T(8,128)S(1)} %bitcast.37, bf16[96,512]{1,0:T(8,128)(2,1)S(1)} %copy-done.7, ...), custom_call_target="tpu_custom_call" | custom-call | flops 805306368 | bytes 2385920 | tf_op jit(solution)/shard_map/state/pallas_call | solution.py:68
  65.0 3.3 %all-to-all-start.3 = ((f32[4,8,128]{2,1,0:T(8,128)}), f32[4,8,128]{2,1,0:T(8,128)S(1)}, u32[]{:S(2)}, u32[]{:S(2)}) async-start(f32[4,8,128]{2,1,0:T(8,128)} %get-tuple-element.10), calls=%async_computation.3 | async-start | bytes 32768 | tf_op jit(solution)/shard_map/all_to_all | solution.py:387
  68.3 0.1 copy.37
  68.4 0.1 copy.38
  68.4 0.1 reshape.102.gain_ref
  68.5 3.9 %all-to-all-done.3.stat_ref = f32[4,8,128]{2,1,0:T(8,128)S(1)} async-done(((f32[4,8,128]{2,1,0:T(8,128)}), f32[4,8,128]{2,1,0:T(8,128)S(1)}, u32[]{:S(2)}, u32[]{:S(2)}) %all-to-all-start.3) | async-done | bytes 16416 | tf_op jit(solution)/shard_map/all_to_all | solution.py:387
  72.5 0.0 copy-done.1
  72.5 1.0 norm.1
  73.5 19.1 %all_to_all.30.got_ref = bf16[32,4,128]{2,1,0:T(4,128)(2,1)S(1)} all-to-all(bf16[32,4,128]{2,1,0:T(4,128)(2,1)S(1)} %norm.1), channel_id=1, replica_groups=mesh['req'=32,'head'=4,'row'=4] {'req'}, dimensions={0} | all-to-all | bytes 65536 | tf_op jit(solution)/shard_map/all_to_all | solution.py:397
  92.5 0.0 copy-done
  92.5 0.8 output.1
  93.3 10.3 %all_to_all.31 = bf16[16,16,512]{2,1,0:T(8,128)(2,1)S(1)} all-to-all(bf16[16,16,512]{2,1,0:T(8,128)(2,1)S(1)} %output.1), channel_id=1, replica_groups=mesh['req'=32,'head'=4,'row'=4] {'head','row'}, dimensions={0} | all-to-all | bytes 524288 | tf_op jit(solution)/shard_map/all_to_all | solution.py:407
  103.6 0.6 reshape.104
  (18 shorter events, 0.1 us)
Async XLA Ops:
  0.6 0.7 copy-start.5
  1.3 30.6 %copy-start.16 = (bf16[512,96]{0,1:T(8,128)(2,1)S(1)}, bf16[512,96]{0,1:T(8,128)(2,1)}, u32[]{:S(2)}) copy-start(bf16[512,96]{0,1:T(8,128)(2,1)} %param.31) | copy-start | bytes 294916
  1.4 30.8 %copy-start.17 = (bf16[512,96]{0,1:T(8,128)(2,1)S(1)}, bf16[512,96]{0,1:T(8,128)(2,1)}, u32[]{:S(2)}) copy-start(bf16[512,96]{0,1:T(8,128)(2,1)} %param.34) | copy-start | bytes 294916
  2.0 30.3 %copy-start.20 = (bf16[512,512]{1,0:T(8,128)(2,1)S(1)}, bf16[512,512]{1,0:T(8,128)(2,1)}, u32[]{:S(2)}) copy-start(bf16[512,512]{1,0:T(8,128)(2,1)} %constant.54.clone) | copy-start | bytes 1572868
  2.0 9.6 %all-to-all-start = ((bf16[4,4,16,128]{3,2,1,0:T(8,128)(2,1)}), bf16[4,4,16,128]{3,2,1,0:T(8,128)(2,1)S(1)}, u32[]{:S(2)}, u32[]{:S(2)}) async-start(bf16[4,4,16,128]{3,2,1,0:T(8,128)(2,1)} %fan.1), calls=%async_computation | async-start | bytes 131072 | tf_op jit(solution)/shard_map/all_to_all | solution.py:332
  13.0 33.2 %all-to-all-start.1 = ((bf16[32,16,128]{2,1,0:T(8,128)(2,1)}), bf16[32,16,128]{2,1,0:T(8,128)(2,1)S(1)}, u32[]{:S(2)}, u32[]{:S(2)}) async-start(bf16[32,16,128]{2,1,0:T(8,128)(2,1)} %pack.1), calls=%async_computation.1 | async-start | bytes 262144 | tf_op jit(solution)/shard_map/all_to_all | solution.py:342
  32.0 14.3 %copy-start.2 = (f32[16,512]{1,0:T(8,128)S(1)}, f32[16,512]{1,0:T(8,128)}, u32[]{:S(2)}) copy-start(f32[16,512]{1,0:T(8,128)} %shift_ref.1) | copy-start | bytes 98308
  32.0 14.3 %copy-start.4 = (f32[5,512]{1,0:T(8,128)S(1)}, f32[5,512]{1,0:T(8,128)}, u32[]{:S(2)}) copy-start(f32[5,512]{1,0:T(8,128)} %blend_ref.1) | copy-start | bytes 30724
  46.3 6.0 %copy-start.19 = (f32[8,64]{1,0:T(8,128)S(1)}, f32[8,64]{1,0:T(8,128)}, u32[]{:S(2)}) copy-start(f32[8,64]{1,0:T(8,128)} %param.39) | copy-start | bytes 6148
  46.3 15.5 %copy-start.6 = (f32[16,8,1024]{2,1,0:T(8,128)S(1)}, f32[16,8,1024]{2,1,0:T(8,128)}, u32[]{:S(2)}) copy-start(f32[16,8,1024]{2,1,0:T(8,128)} %param.27) | copy-start | bytes 1572868
  46.3 15.5 %copy-start.7 = (bf16[96,512]{1,0:T(8,128)(2,1)S(1)}, bf16[96,512]{1,0:T(8,128)(2,1)}, u32[]{:S(2)}) copy-start(bf16[96,512]{1,0:T(8,128)(2,1)} %decay_ref.2) | copy-start | bytes 294916
  46.3 15.5 %copy-start.8 = (bf16[96,512]{1,0:T(8,128)(2,1)S(1)}, bf16[96,512]{1,0:T(8,128)(2,1)}, u32[]{:S(2)}) copy-start(bf16[96,512]{1,0:T(8,128)(2,1)} %learn_ref.2) | copy-start | bytes 294916
  46.3 15.5 %copy-start.9 = (f32[512]{0:T(512)S(1)}, f32[512]{0:T(512)}, u32[]{:S(2)}) copy-start(f32[512]{0:T(512)} %param.33) | copy-start | bytes 6148
  46.4 15.5 %copy-start.10 = (f32[512]{0:T(512)S(1)}, f32[512]{0:T(512)}, u32[]{:S(2)}) copy-start(f32[512]{0:T(512)} %param.36) | copy-start | bytes 6148
  46.4 15.5 %copy-start.11 = (f32[512]{0:T(512)S(1)}, f32[512]{0:T(512)}, u32[]{:S(2)}) copy-start(f32[512]{0:T(512)} %param.37) | copy-start | bytes 6148
  46.4 15.5 %copy-start.12 = (f32[512]{0:T(512)S(1)}, f32[512]{0:T(512)}, u32[]{:S(2)}) copy-start(f32[512]{0:T(512)} %param.38) | copy-start | bytes 6148
  46.4 15.5 %copy-start.13 = (bf16[256,256]{1,0:T(8,128)(2,1)S(1)}, bf16[256,256]{1,0:T(8,128)(2,1)}, u32[]{:S(2)}) copy-start(bf16[256,256]{1,0:T(8,128)(2,1)} %constant.50.clone.halves_ref) | copy-start | bytes 393220
  46.4 15.5 %copy-start.14 = (bf16[512,128]{1,0:T(8,128)(2,1)S(1)}, bf16[512,128]{1,0:T(8,128)(2,1)}, u32[]{:S(2)}) copy-start(bf16[512,128]{1,0:T(8,128)(2,1)} %constant.52.clone.head_to_lanes_ref) | copy-start | bytes 393220
  46.4 15.5 %copy-start.15 = (bf16[128,128]{1,0:T(8,128)(2,1)S(1)}, bf16[128,128]{1,0:T(8,128)(2,1)}, u32[]{:S(2)}) copy-start(bf16[128,128]{1,0:T(8,128)(2,1)} %constant.51.clone.same_head_ref) | copy-start | bytes 98308
  48.3 13.4 %all-to-all-start.2 = ((bf16[4,64,1408]{2,1,0:T(8,128)(2,1)}), bf16[4,64,1408]{2,1,0:T(8,128)(2,1)S(1)}, u32[]{:S(2)}, u32[]{:S(2)}) async-start(bf16[4,64,1408]{2,1,0:T(8,128)(2,1)} %get-tuple-element.9), calls=%async_computation.2 | async-start | bytes 1441792 | tf_op jit(solution)/shard_map/all_to_all | solution.py:358
  52.3 16.0 %copy-start.18 = (f32[8,16]{1,0:T(8,128)S(1)}, f32[8,16]{1,0:T(8,128)}, u32[]{:S(2)}) copy-start(f32[8,16]{1,0:T(8,128)} %param.40) | copy-start | bytes 1540
  52.3 20.1 %copy-start.1 = (bf16[128,256]{1,0:T(8,128)(2,1)S(1)}, bf16[128,256]{1,0:T(8,128)(2,1)}, u32[]{:S(2)}) copy-start(bf16[128,256]{1,0:T(8,128)(2,1)} %constant.55.clone.unpack_ref) | copy-start | bytes 196612
  52.3 20.1 %copy-start.3 = (bf16[128,128]{1,0:T(8,128)(2,1)S(1)}, bf16[128,128]{1,0:T(8,128)(2,1)}, u32[]{:S(2)}) copy-start(bf16[128,128]{1,0:T(8,128)(2,1)} %constant.53.clone.to_natural_ref) | copy-start | bytes 98308
  61.9 30.6 %copy-start = (bf16[8,16,2048]{2,1,0:T(8,128)(2,1)S(1)}, bf16[8,16,2048]{2,1,0:T(8,128)(2,1)}, u32[]{:S(2)}) copy-start(bf16[8,16,2048]{2,1,0:T(8,128)(2,1)} %param.41) | copy-start | bytes 1572868
  65.0 7.4 %all-to-all-start.3 = ((f32[4,8,128]{2,1,0:T(8,128)}), f32[4,8,128]{2,1,0:T(8,128)S(1)}, u32[]{:S(2)}, u32[]{:S(2)}) async-start(f32[4,8,128]{2,1,0:T(8,128)} %get-tuple-element.10), calls=%async_computation.3 | async-start | bytes 32768 | tf_op jit(solution)/shard_map/all_to_all | solution.py:387

commit v3 on v2

--- a/solution.py
+++ b/solution.py
@@ -85,19 +85,13 @@
         copy.wait()
 
 
-def pack_kernel(dest_ref, x_ref, out_ref, done):
-    copies = [
-        pltpu.make_async_copy(x_ref.at[q], out_ref.at[dest_ref[q]], done.at[q])
-        for q in range(REQ_DEV)
-    ]
-    for copy in copies:
-        copy.start()
-    for copy in copies:
-        copy.wait()
+def pack_kernel(slot_ref, first_ref, x_ref, out_ref):
+    for q in range(REQ_DEV):
+        out_ref[slot_ref[first_ref[0] + q] // REQ_DEV] = x_ref[q]
 
 
 def mix_kernel(
-    source_ref, got_ref, last_ref, shift_ref, blend_ref, proj_ref, value_ref, decay_ref, learn_ref,
+    source_ref, count_ref, got_ref, shift_ref, blend_ref, proj_ref, decay_ref, learn_ref, spread_ref,
     out_ref, new_shift_ref, tokens,
 ):
     for page in range(REQ_DEV):
@@ -107,12 +101,20 @@
     current = jnp.concatenate([tokens[part] for part in range(4)], axis=1)
     before = jnp.concatenate([shift_ref[...], current[:-REQ_DEV]], axis=0)
     towards = before - current
-    mixed = [(current + towards * blend_ref[b:b + 1, :]).astype(BF16) for b in range(5)]
-    recept = dot(mixed[0], proj_ref[0]).astype(BF16)
-    key = dot(mixed[2], proj_ref[1]).astype(BF16)
-    value = dot(mixed[3], value_ref[...]).astype(BF16)
-    decay = dot(mixed[1], decay_ref[...]).astype(BF16)
-    learn = dot(mixed[4], learn_ref[...]).astype(BF16)
+
+    def mixed(branch):
+        return (current + towards * blend_ref[branch:branch + 1, :]).astype(BF16)
+
+    def low_rank(rows, weight):
+        return lax.dot_general(
+            rows, weight, (((1,), (1,)), ((), ())), preferred_element_type=F32
+        ).astype(BF16)
+
+    value = dot(dot(mixed(3), proj_ref[2]).astype(BF16), spread_ref[...]).astype(BF16)
+    recept = dot(mixed(0), proj_ref[0]).astype(BF16)
+    key = dot(mixed(2), proj_ref[1]).astype(BF16)
+    decay = low_rank(mixed(1), decay_ref[...])
+    learn = low_rank(mixed(4), learn_ref[...])
     pad = jnp.zeros((TOK, LANES - decay.shape[1]), BF16)
     for part in range(4):
         out_ref[part, :, 0:FEATS] = recept
@@ -120,16 +122,14 @@
         out_ref[part, :, 2 * FEATS:DECAY_AT] = value[:, part * VALS:(part + 1) * VALS]
         out_ref[part, :, DECAY_AT:LEARN_AT] = jnp.concatenate([decay, pad], axis=1)
         out_ref[part, :, LEARN_AT:WIDTH] = jnp.concatenate([learn, pad], axis=1)
-    kept = last_ref[...]
-    picked = current * jnp.concatenate([kept] * 4, axis=1)
-    total = picked[0:REQ_DEV]
-    for t in range(1, TS):
-        total = total + picked[t * REQ_DEV:(t + 1) * REQ_DEV]
-    new_shift_ref[...] = total
+    for page in range(REQ_DEV):
+        row = (count_ref[page] - 1) * REQ_DEV + page
+        for part in range(4):
+            new_shift_ref[page:page + 1, part * LANES:(part + 1) * LANES] = tokens[part, pl.ds(row, 1), :]
 
 
 def state_kernel(
-    got_ref, live_ref, state_ref, decay_ref, decay_offset_ref, learn_ref, learn_offset_ref, gain_ref,
+    count_ref, got_ref, state_ref, decay_ref, decay_offset_ref, learn_ref, learn_offset_ref, gain_ref,
     correction_ref, reward_ref, halves_ref, same_head_ref, head_to_lanes_ref,
     new_state_ref, reading_ref, bonus_ref, stat_ref, spread, states, factors,
 ):
@@ -162,7 +162,11 @@
     norm = jnp.concatenate([norm[0:TOK], norm[TOK:2 * TOK]], axis=1)
     key_dir = scaled * lax.rsqrt(norm + 1e-6)
     key_adj = key * (1.0 + (learn - 1.0) * correction_ref[...])
-    live = live_ref[...]
+    page_row = lax.broadcasted_iota(jnp.int32, (REQ_DEV, LANES), 0)
+    counts = jnp.zeros((REQ_DEV, LANES), jnp.int32)
+    for page in range(REQ_DEV):
+        counts = jnp.where(page_row == page, count_ref[page], counts)
+    live = jnp.concatenate([jnp.where(counts > t, 1.0, 0.0) for t in range(TS)], axis=0)
     live_wide = jnp.concatenate([live] * 4, axis=1)
     vectors = [
         key_dir,
@@ -266,9 +270,9 @@
         out_ref[source_ref[page]] = rows[pl.ds(page, TS, stride=REQ_DEV), :].astype(BF16)
 
 
-def output_kernel(dest_ref, got_ref, proj_ref, out_ref, rows):
+def output_kernel(slot_ref, first_ref, got_ref, proj_ref, out_ref, rows):
     for q in range(REQ_DEV):
-        rows[q * TS:(q + 1) * TS, :] = got_ref[dest_ref[q]].astype(F32)
+        rows[q * TS:(q + 1) * TS, :] = got_ref[slot_ref[first_ref[0] + q] // REQ_DEV].astype(F32)
     terms = dot(rows[...].astype(BF16), proj_ref[...]).astype(BF16)
     for head in range(4):
         for part in range(4):
@@ -306,48 +310,42 @@
         jnp.asarray(m, BF16) for m in constant_matrices()
     ]
     first = lax.axis_index("req") * REQ_DEV
-    dest = lax.dynamic_slice_in_dim(caller_sheet_slot, first, REQ_DEV) // REQ_DEV
     pages = first + jnp.arange(REQ_DEV, dtype=jnp.int32)
     holder = caller_sheet_slot[None, :] == pages[:, None]
-    everyone = jnp.arange(caller_sheet_slot.shape[0], dtype=jnp.int32)
-    source = jnp.sum(jnp.where(holder, everyone[None, :], 0), axis=1) // REQ_DEV
+    groups_of = lax.shift_right_logical(jnp.arange(caller_sheet_slot.shape[0], dtype=jnp.int32), 4)
+    source = jnp.sum(jnp.where(holder, groups_of[None, :], 0), axis=1)
     count = jnp.sum(jnp.where(holder, genuine_symbol_number[None, :], 0), axis=1)
-    position = jnp.arange(TS, dtype=jnp.int32)[:, None]
-    live = jnp.broadcast_to((position < count[None, :]).astype(F32)[..., None], (TS, REQ_DEV, LANES))
-    last = jnp.broadcast_to(
-        (position == count[None, :] - 1).astype(F32)[..., None], (TS, REQ_DEV, LANES)
-    )
-    live, last = live.reshape(TOK, LANES), last.reshape(TOK, LANES)
+    first = first.astype(jnp.int32)[None]
+    gain = groupwise_gain.reshape(HEADS, 8, 2).transpose(2, 0, 1).reshape(1, VALS)
+    reward = reward_coefficients.reshape(1, FEATS)
 
     tiles = incoming_activations.reshape(4, TS, 4, LANES).transpose(0, 2, 1, 3).reshape(4, 16, LANES)
     everywhere = call(
         fan_kernel,
         [shaped((4, 4, 16, LANES), BF16)],
-        [ANY],
+        [pl.BlockSpec(memory_space=pltpu.HBM)],
         (tiles,),
         scratch=[pltpu.SemaphoreType.DMA((4,))],
         name="fan",
         out_spec=ANY,
     )
     mine = lax.all_to_all(everywhere, "head", 0, 0, tiled=True).reshape(REQ_DEV, 16, LANES)
+    mine, source, count, gain, reward = lax.optimization_barrier((mine, source, count, gain, reward))
     packed = call(
         pack_kernel,
         [shaped((groups, 16, LANES), BF16)],
-        [SMEM, ANY],
-        (dest, mine),
-        scratch=[pltpu.SemaphoreType.DMA((REQ_DEV,))],
+        [SMEM, SMEM, VMEM],
+        (caller_sheet_slot, first, mine),
         name="pack",
-        out_spec=ANY,
     )
     got = lax.all_to_all(packed, "req", 0, 0, tiled=True)
-    value_projector = dot(first_projectors[2], spread_values).astype(BF16)
     partial, new_shift = call(
         mix_kernel,
         [shaped((4, TOK, WIDTH), BF16), shaped((REQ_DEV, FEATS), F32)],
-        [SMEM] + [VMEM] * 8,
+        [SMEM] * 2 + [VMEM] * 7,
         (
-            source, got, last, prior_activation_sheets, blend_fractions, first_projectors[0:2],
-            value_projector, fading_narrow_projector, context_step_narrowing,
+            source, count, got, prior_activation_sheets, blend_fractions, first_projectors,
+            fading_narrow_projector.T, context_step_narrowing.T, spread_values,
         ),
         scratch=[pltpu.VMEM((4, TOK, LANES), F32)],
         flops=2 * TOK * FEATS * (3 * FEATS + 192),
@@ -364,10 +362,10 @@
             shaped((TOK, LANES), F32),
             shaped((4, 8, LANES), F32),
         ],
-        [VMEM] * 13,
+        [SMEM] + [VMEM] * 12,
         (
+            count,
             sums,
-            live,
             sheets,
             fading_widen_projector,
             fading_offset[None],
@@ -375,7 +373,7 @@
             context_step_offset[None],
             erasure_address_gain[None],
             address_correction[None],
-            reward_coefficients.reshape(1, FEATS),
+            reward,
             halves,
             same_head,
             head_to_lanes,
@@ -385,7 +383,6 @@
         name="state",
     )
     stats = lax.all_to_all(stat, "row", 0, 0, tiled=True)
-    gain = groupwise_gain.reshape(HEADS, 8, 2).transpose(2, 0, 1).reshape(1, VALS)
     leaving = call(
         norm_kernel,
         [shaped((groups, TS, LANES), BF16)],
@@ -398,8 +395,8 @@
     terms = call(
         output_kernel,
         [shaped((16, 16, FEATS), BF16)],
-        [SMEM, VMEM, VMEM],
-        (dest, back, final_projector.reshape(VALS, 4 * FEATS)),
+        [SMEM, SMEM, VMEM, VMEM],
+        (caller_sheet_slot, first, back, final_projector.reshape(VALS, 4 * FEATS)),
         scratch=[pltpu.VMEM((TOK, LANES), F32)],
         flops=2 * TOK * VALS * 4 * FEATS,
         name="output",

time: 105 us -> 109 us (1.038)
  blocking collectives: 29.3 us -> 82.1 us
  waiting for transfers between devices: 28.5 us -> 1.89 us
  starting transfers between devices: 29.8 us -> 5.02 us
  local copies, waits for them, and re-layouts: 3.7 us -> 9.48 us
  matrix products: 1.48 us -> 0 us
    all_to_all x0 -> x3, blocking collectives: none -> 53 us  [the longest x1 33 us: per_device(): got = lax.all_to_all(packed, 'req', 0, 0, tiled=True)]
    all_to_all x3 -> x0, waiting for transfers between devices: 25.7 us -> none  [the longest x1 12.4 us: per_device(): got = lax.all_to_all(packed, 'req', 0, 0, tiled=True)]
    all_to_all x3 -> x0, starting transfers between devices: 24.6 us -> none  [the longest x1 17.4 us: per_device(): got = lax.all_to_all(packed, 'req', 0, 0, tiled=True)]
    unnamed x45, local copies, waits for them, and re-layouts: 1.14 us -> 7.93 us
    dot_general x1 -> x0, matrix products: 1.48 us -> none  [dot(): return jnp.dot(a, b, preferred_element_type=F32)]
    slice x1 -> x0, local copies, waits for them, and re-layouts: 1.3 us -> none  [per_device(): first_projectors[0:2]]
  transfers between devices with their start and end apart: 4 -> 1, of which waited for: 4 -> 1; matrix products, arithmetic and copies ran while one was open for 5% -> 2% of each run, Pallas kernels for 0% -> 0%
where the time goes in v3:
time: 109 us
  blocking collectives  82.1 us (75%)
  local copies, waits for them, and re-layouts  9.48 us (9%)
  Pallas kernels  8.29 us (8%)
  starting transfers between devices  5.02 us (5%)
  waiting for transfers between devices  1.89 us (2%)
    all_to_all x1, blocking collectives, per_device(): got = lax.all_to_all(packed, 'req', 0, 0, tiled=True)  33 us
    all_to_all x1, blocking collectives, per_device(): back = lax.all_to_all(leaving, 'req', 0, 0, tiled=True)  18.9 us
    all_to_all x1, blocking collectives, per_device(): sums = lax.all_to_all(partial, 'row', 0, 0, tiled=True)  13.4 us
    all_to_all x1, blocking collectives, per_device(): arrived = lax.all_to_all(terms, ('head', 'row'), 0, 0, tiled=True)  10.3 us
    pallas_call x6, Pallas kernels, call(): pl.pallas_call(kernel, out_shape=outs[0] if single else outs, in_specs=in...  8.29 us
    unnamed x45, local copies, waits for them, and re-layouts  7.93 us
    all_to_all x1, blocking collectives, per_device(): stats = lax.all_to_all(stat, 'row', 0, 0, tiled=True)  6.55 us
    all_to_all x1, starting transfers between devices, per_device(): lax.all_to_all(everywhere, 'head', 0, 0, tiled=True)  5.02 us
  transfers between devices with their start and end apart: 1, of which 1 were waited for; matrix products, arithmetic and copies ran while one was open for 2% of the time, Pallas kernels for 0%

profile of v3, /device:TPU:1, one launch (start us, length us, event | category | flops | bytes accessed | tf_op | source)
XLA Modules:
  0.0 108.6 jit_solution(11538161588709518270)
XLA Ops:
  0.6 0.0 copy-start.11
  0.6 0.7 copy-done.11
  1.3 0.7 fan.1
  2.0 5.0 %all-to-all-start = ((bf16[4,4,16,128]{3,2,1,0:T(8,128)(2,1)}), bf16[4,4,16,128]{3,2,1,0:T(8,128)(2,1)S(1)}, u32[]{:S(2)}, u32[]{:S(2)}) async-start(bf16[4,4,16,128]{3,2,1,0:T(8,128)(2,1)} %fan.1), calls=%async_computation | async-start | bytes 131072 | tf_op jit(solution)/shard_map/all_to_all | solution.py:332
  7.0 0.9 fusion.1
  7.9 0.8 reshape.57.reward_ref
  8.7 0.8 copy.31
  9.5 0.1 copy.32
  9.5 0.1 reshape.56.gain_ref
  9.6 1.9 %all-to-all-done = bf16[4,4,16,128]{3,2,1,0:T(8,128)(2,1)S(1)} async-done(((bf16[4,4,16,128]{3,2,1,0:T(8,128)(2,1)}), bf16[4,4,16,128]{3,2,1,0:T(8,128)(2,1)S(1)}, u32[]{:S(2)}, u32[]{:S(2)}) %all-to-all-start) | async-done | bytes 65568 | tf_op jit(solution)/shard_map/all_to_all | solution.py:332
  11.5 0.0 copy-start.8
  11.5 0.7 copy-done.8
  12.2 0.7 pack.1
  12.9 33.0 %all_to_all.30.got_ref = bf16[32,16,128]{2,1,0:T(8,128)(2,1)S(1)} all-to-all(bf16[32,16,128]{2,1,0:T(8,128)(2,1)S(1)} %pack.1), channel_id=1, replica_groups=mesh['req'=32,'head'=4,'row'=4] {'req'}, dimensions={0} | all-to-all | bytes 262144 | tf_op jit(solution)/shard_map/all_to_all | solution.py:341
  45.9 0.0 copy-start
  45.9 1.4 %copy-done = bf16[3,512,512]{2,1,0:T(8,128)(2,1)S(1)} copy-done((bf16[3,512,512]{2,1,0:T(8,128)(2,1)S(1)}, bf16[3,512,512]{2,1,0:T(8,128)(2,1)}, u32[]{:S(2)}) %copy-start) | copy-done | bytes 1572888
  47.3 0.0 copy-start.2
  47.3 1.0 copy-done.2
  48.3 0.0 copy-start.3
  48.3 0.9 copy-done.3
  49.2 0.0 copy-start.4
  49.2 0.9 copy-done.4
  50.1 0.0 copy-start.6
  50.1 0.8 copy-done.6
  50.9 0.0 copy-start.10
  50.9 0.7 copy-done.10
  51.6 0.0 copy-start.12
  51.6 0.0 copy-start.13
  51.6 0.0 copy-start.14
  51.6 0.0 copy-start.15
  51.6 0.0 copy-start.16
  51.6 0.0 copy-start.17
  51.6 0.0 copy-start.18
  51.6 0.0 copy-start.19
  51.6 0.0 copy-start.20
  51.6 0.0 copy-start.21
  51.7 1.7 %mix.1 = (bf16[4,64,1408]{2,1,0:T(8,128)(2,1)S(1)}, f32[16,512]{1,0:T(8,128)}) custom-call(s32[16]{0:T(128)S(1)} %get-tuple-element.14.source_ref, s32[16]{0:T(128)S(1)} %get-tuple-element.15.count_ref, bf16[32,16,128]{2,1,0:T(8,128)(2,1)S(1)} %all_to_all.30.got_ref, f32[16,512]{1,0:T(8,128)S(1)} %copy-done.6, f32[5,512]{1,0:T(8,128)S(1)} %copy-done.10, ...), custom_call_target="tpu_custom_call" | custom-call | flops 113246208 | bytes 3221632 | tf_op jit(solution)/shard_map/mix/pallas_call | solution.py:68
  53.4 13.4 %all_to_all.31.got_ref = bf16[4,64,1408]{2,1,0:T(8,128)(2,1)S(1)} all-to-all(bf16[4,64,1408]{2,1,0:T(8,128)(2,1)S(1)} %get-tuple-element.17), channel_id=1, replica_groups=mesh['req'=32,'head'=4,'row'=4] {'row'}, dimensions={0} | all-to-all | bytes 1441792 | tf_op jit(solution)/shard_map/all_to_all | solution.py:356
  66.8 0.0 copy-start.5
  66.8 0.0 copy-start.7
  66.8 0.0 copy-done.12
  66.8 0.0 copy-done.13
  66.8 0.0 copy-done.14
  66.9 0.0 copy-done.15
  66.9 0.0 copy-done.16
  66.9 0.0 copy-done.17
  66.9 0.0 copy-done.18
  66.9 0.0 copy-done.19
  66.9 0.0 copy-done.20
  66.9 0.0 copy-done.21
  66.9 0.0 copy-start.1
  66.9 0.0 copy-start.9
  67.0 3.4 %state.1 = (f32[1024,128]{1,0:T(8,128)}, f32[64,128]{1,0:T(8,128)S(1)}, f32[64,128]{1,0:T(8,128)S(1)}, f32[4,8,128]{2,1,0:T(8,128)S(1)}) custom-call(s32[16]{0:T(128)S(1)} %get-tuple-element.15.count_ref, bf16[4,64,1408]{2,1,0:T(8,128)(2,1)S(1)} %all_to_all.31.got_ref, f32[1024,128]{1,0:T(8,128)S(1)} %bitcast.32, bf16[96,512]{1,0:T(8,128)(2,1)S(1)} %copy-done.13, ...), custom_call_target="tpu_custom_call" | custom-call | flops 805306368 | bytes 2353216 | tf_op jit(solution)/shard_map/state/pallas_call | solution.py:68
  70.4 6.5 %all_to_all.32.stat_ref = f32[4,8,128]{2,1,0:T(8,128)S(1)} all-to-all(f32[4,8,128]{2,1,0:T(8,128)S(1)} %get-tuple-element.19), channel_id=1, replica_groups=mesh['req'=32,'head'=4,'row'=4] {'row'}, dimensions={0} | all-to-all | bytes 32768 | tf_op jit(solution)/shard_map/all_to_all | solution.py:385
  76.9 0.0 copy-done.5
  76.9 0.0 copy-done.7
  76.9 1.0 norm.1
  77.9 18.9 %all_to_all.33.got_ref = bf16[32,4,128]{2,1,0:T(4,128)(2,1)S(1)} all-to-all(bf16[32,4,128]{2,1,0:T(4,128)(2,1)S(1)} %norm.1), channel_id=1, replica_groups=mesh['req'=32,'head'=4,'row'=4] {'req'}, dimensions={0} | all-to-all | bytes 65536 | tf_op jit(solution)/shard_map/all_to_all | solution.py:394
  96.8 0.0 copy-done.1
  96.8 0.0 copy-done.9
  96.8 0.8 output.1
  97.6 10.3 %all_to_all.34 = bf16[16,16,512]{2,1,0:T(8,128)(2,1)S(1)} all-to-all(bf16[16,16,512]{2,1,0:T(8,128)(2,1)S(1)} %output.1), channel_id=1, replica_groups=mesh['req'=32,'head'=4,'row'=4] {'head','row'}, dimensions={0} | all-to-all | bytes 524288 | tf_op jit(solution)/shard_map/all_to_all | solution.py:404
  108.0 0.6 reshape.61
  (3 shorter events, 0.1 us)
Async XLA Ops:
  0.6 0.7 copy-start.11
  2.0 9.5 %all-to-all-start = ((bf16[4,4,16,128]{3,2,1,0:T(8,128)(2,1)}), bf16[4,4,16,128]{3,2,1,0:T(8,128)(2,1)S(1)}, u32[]{:S(2)}, u32[]{:S(2)}) async-start(bf16[4,4,16,128]{3,2,1,0:T(8,128)(2,1)} %fan.1), calls=%async_computation | async-start | bytes 131072 | tf_op jit(solution)/shard_map/all_to_all | solution.py:332
  11.5 0.7 copy-start.8
  45.9 1.4 %copy-start = (bf16[3,512,512]{2,1,0:T(8,128)(2,1)S(1)}, bf16[3,512,512]{2,1,0:T(8,128)(2,1)}, u32[]{:S(2)}) copy-start(bf16[3,512,512]{2,1,0:T(8,128)(2,1)} %proj_ref.1) | copy-start | bytes 4718596
  47.3 1.0 copy-start.2
  48.3 0.9 copy-start.3
  49.2 0.9 copy-start.4
  50.1 0.8 copy-start.6
  50.9 0.7 copy-start.10
  51.6 15.3 %copy-start.12 = (f32[16,8,1024]{2,1,0:T(8,128)S(1)}, f32[16,8,1024]{2,1,0:T(8,128)}, u32[]{:S(2)}) copy-start(f32[16,8,1024]{2,1,0:T(8,128)} %param.27) | copy-start | bytes 1572868
  51.6 15.3 %copy-start.13 = (bf16[96,512]{1,0:T(8,128)(2,1)S(1)}, bf16[96,512]{1,0:T(8,128)(2,1)}, u32[]{:S(2)}) copy-start(bf16[96,512]{1,0:T(8,128)(2,1)} %decay_ref.1) | copy-start | bytes 294916
  51.6 15.3 %copy-start.14 = (bf16[96,512]{1,0:T(8,128)(2,1)S(1)}, bf16[96,512]{1,0:T(8,128)(2,1)}, u32[]{:S(2)}) copy-start(bf16[96,512]{1,0:T(8,128)(2,1)} %learn_ref.1) | copy-start | bytes 294916
  51.6 15.3 %copy-start.15 = (f32[512]{0:T(512)S(1)}, f32[512]{0:T(512)}, u32[]{:S(2)}) copy-start(f32[512]{0:T(512)} %param.33) | copy-start | bytes 6148
  51.6 15.3 %copy-start.16 = (f32[512]{0:T(512)S(1)}, f32[512]{0:T(512)}, u32[]{:S(2)}) copy-start(f32[512]{0:T(512)} %param.36) | copy-start | bytes 6148
  51.6 15.3 %copy-start.17 = (f32[512]{0:T(512)S(1)}, f32[512]{0:T(512)}, u32[]{:S(2)}) copy-start(f32[512]{0:T(512)} %param.37) | copy-start | bytes 6148
  51.6 15.3 %copy-start.18 = (f32[512]{0:T(512)S(1)}, f32[512]{0:T(512)}, u32[]{:S(2)}) copy-start(f32[512]{0:T(512)} %param.38) | copy-start | bytes 6148
  51.6 15.3 %copy-start.19 = (bf16[512,128]{1,0:T(8,128)(2,1)S(1)}, bf16[512,128]{1,0:T(8,128)(2,1)}, u32[]{:S(2)}) copy-start(bf16[512,128]{1,0:T(8,128)(2,1)} %constant.29.clone.head_to_lanes_ref) | copy-start | bytes 393220
  51.6 15.3 %copy-start.20 = (bf16[256,256]{1,0:T(8,128)(2,1)S(1)}, bf16[256,256]{1,0:T(8,128)(2,1)}, u32[]{:S(2)}) copy-start(bf16[256,256]{1,0:T(8,128)(2,1)} %constant.27.clone.halves_ref) | copy-start | bytes 393220
  51.6 15.3 %copy-start.21 = (bf16[128,128]{1,0:T(8,128)(2,1)S(1)}, bf16[128,128]{1,0:T(8,128)(2,1)}, u32[]{:S(2)}) copy-start(bf16[128,128]{1,0:T(8,128)(2,1)} %constant.28.clone.same_head_ref) | copy-start | bytes 98308
  66.8 10.1 %copy-start.5 = (bf16[128,256]{1,0:T(8,128)(2,1)S(1)}, bf16[128,256]{1,0:T(8,128)(2,1)}, u32[]{:S(2)}) copy-start(bf16[128,256]{1,0:T(8,128)(2,1)} %constant.32.clone.unpack_ref) | copy-start | bytes 196612
  66.8 10.1 %copy-start.7 = (bf16[128,128]{1,0:T(8,128)(2,1)S(1)}, bf16[128,128]{1,0:T(8,128)(2,1)}, u32[]{:S(2)}) copy-start(bf16[128,128]{1,0:T(8,128)(2,1)} %constant.30.clone.to_natural_ref) | copy-start | bytes 98308
  66.9 29.9 %copy-start.1 = (bf16[8,16,2048]{2,1,0:T(8,128)(2,1)S(1)}, bf16[8,16,2048]{2,1,0:T(8,128)(2,1)}, u32[]{:S(2)}) copy-start(bf16[8,16,2048]{2,1,0:T(8,128)(2,1)} %param.41) | copy-start | bytes 1572868
  66.9 29.9 %copy-start.9 = (s32[512]{0:T(512)S(1)}, s32[512]{0:T(512)}, u32[]{:S(2)}) copy-start(s32[512]{0:T(512)} %slot_ref.3) | copy-start | bytes 6148

commit v4 on v3

--- a/solution.py
+++ b/solution.py
@@ -61,7 +61,7 @@
     return dot(high, b) + dot(low, b)
 
 
-def call(kernel, outs, in_specs, args, scratch=(), flops=0, name=None, out_spec=VMEM):
+def call(kernel, outs, in_specs, args, scratch=(), flops=0, name=None, out_spec=VMEM, vmem=32 * 2**20):
     size = sum(int(np.prod(a.shape)) * a.dtype.itemsize for a in args)
     size += sum(int(np.prod(o.shape)) * o.dtype.itemsize for o in outs)
     single = len(outs) == 1
@@ -69,25 +69,43 @@
         kernel,
         out_shape=outs[0] if single else outs,
         in_specs=in_specs,
-        out_specs=out_spec if single else [out_spec] * len(outs),
+        out_specs=out_spec if single else [out_spec] * len(outs) if out_spec is VMEM else out_spec,
         scratch_shapes=list(scratch),
         cost_estimate=pl.CostEstimate(flops=flops, bytes_accessed=size, transcendentals=0),
-        compiler_params=pltpu.CompilerParams(vmem_limit_bytes=32 * 2**20),
+        compiler_params=pltpu.CompilerParams(vmem_limit_bytes=vmem),
         name=name,
     )(*args)
 
 
-def fan_kernel(x_ref, out_ref, done):
-    copies = [pltpu.make_async_copy(x_ref, out_ref.at[at], done.at[at]) for at in range(4)]
+def first_request():
+    return lax.axis_index("req") * REQ_DEV
+
+
+def fan_kernel(slot_ref, x_ref, out_ref, slot_out_ref, done):
+    copy = pltpu.make_async_copy(slot_ref, slot_out_ref, done)
+    copy.start()
+    for at in range(4):
+        out_ref[at] = x_ref[...]
+    copy.wait()
+
+
+def pack_kernel(slot_ref, x_ref, out_ref, first_ref):
+    first = first_request()
+    first_ref[0] = first
+    for q in range(REQ_DEV):
+        out_ref[slot_ref[first + q] // REQ_DEV] = x_ref[q]
+
+
+def stage_kernel(*refs):
+    count = len(refs) // 2
+    done = refs[-1]
+    copies = [
+        pltpu.make_async_copy(refs[at], refs[count + at], done.at[at]) for at in range(count)
+    ]
     for copy in copies:
         copy.start()
     for copy in copies:
         copy.wait()
-
-
-def pack_kernel(slot_ref, first_ref, x_ref, out_ref):
-    for q in range(REQ_DEV):
-        out_ref[slot_ref[first_ref[0] + q] // REQ_DEV] = x_ref[q]
 
 
 def mix_kernel(
@@ -162,10 +180,7 @@
     norm = jnp.concatenate([norm[0:TOK], norm[TOK:2 * TOK]], axis=1)
     key_dir = scaled * lax.rsqrt(norm + 1e-6)
     key_adj = key * (1.0 + (learn - 1.0) * correction_ref[...])
-    page_row = lax.broadcasted_iota(jnp.int32, (REQ_DEV, LANES), 0)
-    counts = jnp.zeros((REQ_DEV, LANES), jnp.int32)
-    for page in range(REQ_DEV):
-        counts = jnp.where(page_row == page, count_ref[page], counts)
+    counts = count_ref[...]
     live = jnp.concatenate([jnp.where(counts > t, 1.0, 0.0) for t in range(TS)], axis=0)
     live_wide = jnp.concatenate([live] * 4, axis=1)
     vectors = [
@@ -270,9 +285,10 @@
         out_ref[source_ref[page]] = rows[pl.ds(page, TS, stride=REQ_DEV), :].astype(BF16)
 
 
-def output_kernel(slot_ref, first_ref, got_ref, proj_ref, out_ref, rows):
+def output_kernel(slot_ref, got_ref, proj_ref, out_ref, rows):
+    first = first_request()
     for q in range(REQ_DEV):
-        rows[q * TS:(q + 1) * TS, :] = got_ref[slot_ref[first_ref[0] + q] // REQ_DEV].astype(F32)
+        rows[q * TS:(q + 1) * TS, :] = got_ref[slot_ref[first + q] // REQ_DEV].astype(F32)
     terms = dot(rows[...].astype(BF16), proj_ref[...]).astype(BF16)
     for head in range(4):
         for part in range(4):
@@ -309,44 +325,57 @@
     halves, same_head, head_to_lanes, to_natural, spread_values, unpack = [
         jnp.asarray(m, BF16) for m in constant_matrices()
     ]
-    first = lax.axis_index("req") * REQ_DEV
+    tiles = incoming_activations.reshape(4, TS, 4, LANES).transpose(0, 2, 1, 3).reshape(4, 16, LANES)
+    everywhere, slot_table = call(
+        fan_kernel,
+        [shaped((4, 4, 16, LANES), BF16), shaped(caller_sheet_slot.shape, jnp.int32)],
+        [ANY, VMEM],
+        (caller_sheet_slot, tiles),
+        scratch=[pltpu.SemaphoreType.DMA],
+        name="fan",
+    )
+    mine = lax.all_to_all(everywhere, "head", 0, 0, tiled=True).reshape(REQ_DEV, 16, LANES)
+    packed, first = call(
+        pack_kernel,
+        [shaped((groups, 16, LANES), BF16), shaped((1,), jnp.int32)],
+        [SMEM, VMEM],
+        (slot_table, mine),
+        name="pack",
+        out_spec=[VMEM, SMEM],
+    )
+    slots, valid, gain, reward, first, *weights = lax.optimization_barrier(
+        (
+            caller_sheet_slot, genuine_symbol_number, groupwise_gain, reward_coefficients, first,
+            prior_activation_sheets, blend_fractions, first_projectors, fading_narrow_projector.T,
+            context_step_narrowing.T, spread_values,
+        )
+    )
+    weights = call(
+        stage_kernel,
+        [shaped(w.shape, w.dtype) for w in weights],
+        [ANY] * len(weights),
+        weights,
+        scratch=[pltpu.SemaphoreType.DMA((len(weights),))],
+        name="stage",
+        vmem=121 * 2**19,
+    )
     pages = first + jnp.arange(REQ_DEV, dtype=jnp.int32)
-    holder = caller_sheet_slot[None, :] == pages[:, None]
-    groups_of = lax.shift_right_logical(jnp.arange(caller_sheet_slot.shape[0], dtype=jnp.int32), 4)
+    holder = slots[None, :] == pages[:, None]
+    groups_of = lax.shift_right_logical(jnp.arange(slots.shape[0], dtype=jnp.int32), 4)
     source = jnp.sum(jnp.where(holder, groups_of[None, :], 0), axis=1)
-    count = jnp.sum(jnp.where(holder, genuine_symbol_number[None, :], 0), axis=1)
-    first = first.astype(jnp.int32)[None]
-    gain = groupwise_gain.reshape(HEADS, 8, 2).transpose(2, 0, 1).reshape(1, VALS)
-    reward = reward_coefficients.reshape(1, FEATS)
-
-    tiles = incoming_activations.reshape(4, TS, 4, LANES).transpose(0, 2, 1, 3).reshape(4, 16, LANES)
-    everywhere = call(
-        fan_kernel,
-        [shaped((4, 4, 16, LANES), BF16)],
-        [pl.BlockSpec(memory_space=pltpu.HBM)],
-        (tiles,),
-        scratch=[pltpu.SemaphoreType.DMA((4,))],
-        name="fan",
-        out_spec=ANY,
-    )
-    mine = lax.all_to_all(everywhere, "head", 0, 0, tiled=True).reshape(REQ_DEV, 16, LANES)
-    mine, source, count, gain, reward = lax.optimization_barrier((mine, source, count, gain, reward))
-    packed = call(
-        pack_kernel,
-        [shaped((groups, 16, LANES), BF16)],
-        [SMEM, SMEM, VMEM],
-        (caller_sheet_slot, first, mine),
-        name="pack",
-    )
+    count = jnp.sum(jnp.where(holder, valid[None, :], 0), axis=1)
+    count_wide = jnp.broadcast_to(count[:, None], (REQ_DEV, LANES))
+    gain = gain.reshape(HEADS, 8, 2).transpose(2, 0, 1).reshape(1, VALS)
+    reward = reward.reshape(1, FEATS)
     got = lax.all_to_all(packed, "req", 0, 0, tiled=True)
+    got, source, count, count_wide, gain, reward, *weights = lax.optimization_barrier(
+        (got, source, count, count_wide, gain, reward, *weights)
+    )
     partial, new_shift = call(
         mix_kernel,
         [shaped((4, TOK, WIDTH), BF16), shaped((REQ_DEV, FEATS), F32)],
         [SMEM] * 2 + [VMEM] * 7,
-        (
-            source, count, got, prior_activation_sheets, blend_fractions, first_projectors,
-            fading_narrow_projector.T, context_step_narrowing.T, spread_values,
-        ),
+        (source, count, got, *weights),
         scratch=[pltpu.VMEM((4, TOK, LANES), F32)],
         flops=2 * TOK * FEATS * (3 * FEATS + 192),
         name="mix",
@@ -362,9 +391,9 @@
             shaped((TOK, LANES), F32),
             shaped((4, 8, LANES), F32),
         ],
-        [SMEM] + [VMEM] * 12,
+        [VMEM] * 13,
         (
-            count,
+            count_wide,
             sums,
             sheets,
             fading_widen_projector,
@@ -395,8 +424,8 @@
     terms = call(
         output_kernel,
         [shaped((16, 16, FEATS), BF16)],
-        [SMEM, SMEM, VMEM, VMEM],
-        (caller_sheet_slot, first, back, final_projector.reshape(VALS, 4 * FEATS)),
+        [SMEM, VMEM, VMEM],
+        (slot_table, back, final_projector.reshape(VALS, 4 * FEATS)),
         scratch=[pltpu.VMEM((TOK, LANES), F32)],
         flops=2 * TOK * VALS * 4 * FEATS,
         name="output",

time: 109 us -> 109 us (level)
  blocking collectives: 82.1 us -> 58.4 us
  starting transfers between devices: 5.02 us -> 17.4 us
  waiting for transfers between devices: 1.89 us -> 10.2 us
  Pallas kernels: 8.29 us -> 10.8 us
    all_to_all x1, blocking collectives: 33 us -> 9.29 us  [per_device(): lax.all_to_all(everywhere, 'head', 0, 0, tiled=True)]
    all_to_all x1, starting transfers between devices: 5.02 us -> 17.4 us  [per_device(): got = lax.all_to_all(packed, 'req', 0, 0, tiled=True)]
    all_to_all x1, waiting for transfers between devices: 1.89 us -> 10.2 us  [per_device(): got = lax.all_to_all(packed, 'req', 0, 0, tiled=True)]
    pallas_call x6 -> x7, Pallas kernels: 8.29 us -> 10.8 us  [call(): pl.pallas_call(kernel, out_shape=outs[0] if single else outs, in_specs=in...]
    unnamed x45 -> x46, local copies, waits for them, and re-layouts: 7.93 us -> 7.18 us
  transfers between devices with their start and end apart: 1 -> 1, of which waited for: 1 -> 1; matrix products, arithmetic and copies ran while one was open for 2% -> 2% of each run, Pallas kernels for 0% -> 3%
where the time goes in v4:
time: 109 us; the launch traced here: 108 us
  blocking collectives  58.4 us (54%)
  starting transfers between devices  17.4 us (16%)
  Pallas kernels  10.8 us (10%)
  waiting for transfers between devices  10.2 us (9%)
  local copies, waits for them, and re-layouts  9.55 us (9%)
    all_to_all x1, blocking collectives, per_device(): back = lax.all_to_all(leaving, 'req', 0, 0, tiled=True)  18.9 us
    all_to_all x1, starting transfers between devices, per_device(): got = lax.all_to_all(packed, 'req', 0, 0, tiled=True)  17.4 us
    all_to_all x1, blocking collectives, per_device(): sums = lax.all_to_all(partial, 'row', 0, 0, tiled=True)  13.4 us
    pallas_call x7, Pallas kernels, call(): pl.pallas_call(kernel, out_shape=outs[0] if single else outs, in_specs=in...  10.8 us
    all_to_all x1, blocking collectives, per_device(): arrived = lax.all_to_all(terms, ('head', 'row'), 0, 0, tiled=True)  10.3 us
    all_to_all x1, waiting for transfers between devices, per_device(): got = lax.all_to_all(packed, 'req', 0, 0, tiled=True)  10.2 us
    all_to_all x1, blocking collectives, per_device(): lax.all_to_all(everywhere, 'head', 0, 0, tiled=True)  9.29 us
    unnamed x46, local copies, waits for them, and re-layouts  7.18 us
  transfers between devices with their start and end apart: 1, of which 1 were waited for; matrix products, arithmetic and copies ran while one was open for 2% of the time, Pallas kernels for 3%

profile of v4, /device:TPU:1, one launch (start us, length us, event | category | flops | bytes accessed | tf_op | source)
XLA Modules:
  0.0 108.1 jit_solution(11076707076803534361)
XLA Ops:
  0.6 0.0 copy-start.9
  0.6 0.7 copy-done.9
  1.3 0.0 copy-start.10
  1.4 0.7 copy-done.10
  2.0 0.0 copy-start.11
  2.0 0.0 copy-start.22
  2.1 9.3 %all_to_all.30 = bf16[4,4,16,128]{3,2,1,0:T(8,128)(2,1)S(1)} all-to-all(bf16[4,4,16,128]{3,2,1,0:T(8,128)(2,1)S(1)} %get-tuple-element.43), channel_id=1, replica_groups=mesh['req'=32,'head'=4,'row'=4] {'head'}, dimensions={0} | all-to-all | bytes 131072 | tf_op jit(solution)/shard_map/all_to_all | solution.py:337
  11.4 1.3 %pack.1 = (bf16[32,16,128]{2,1,0:T(8,128)(2,1)}, s32[1]{0:T(128)}) custom-call(s32[512]{0:T(512)S(1)} %get-tuple-element.42.slot_ref, bf16[16,16,128]{2,1,0:T(8,128)(2,1)S(1)} %bitcast.28), custom_call_target="tpu_custom_call" | custom-call | bytes 198660 | tf_op jit(solution)/shard_map/pack/pallas_call | solution.py:68
  12.7 17.4 %all-to-all-start.1 = ((bf16[32,16,128]{2,1,0:T(8,128)(2,1)}), bf16[32,16,128]{2,1,0:T(8,128)(2,1)S(1)}, u32[]{:S(2)}, u32[]{:S(2)}) async-start(bf16[32,16,128]{2,1,0:T(8,128)(2,1)} %get-tuple-element.44), calls=%async_computation.1 | async-start | bytes 262144 | tf_op jit(solution)/shard_map/all_to_all | solution.py:370
  30.1 0.8 reshape.58.reward_ref
  30.8 0.8 copy.31
  31.6 0.1 copy.32
  31.7 0.1 reshape.57.gain_ref
  31.8 3.1 %stage.1 = (f32[16,512]{1,0:T(8,128)}, f32[5,512]{1,0:T(8,128)}, bf16[3,512,512]{2,1,0:T(8,128)(2,1)}, bf16[96,512]{1,0:T(8,128)(2,1)}, bf16[96,512]{1,0:T(8,128)(2,1)}, /*index=5*/bf16[512,512]{1,0:T(8,128)(2,1)}) custom-call(f32[16,512]{1,0:T(8,128)} %refs_0_, f32[5,512]{1,0:T(8,128)} %refs_1_, bf16[3,512,512]{2,1,0:T(8,128)(2,1)} %refs_2_, ...), custom_call_target="tpu_custom_call" | custom-call | bytes 4673536 | tf_op jit(solution)/shard_map/stage/pallas_call | solution.py:68
  34.8 0.7 iota_add_fusion
  35.5 0.0 copy-done.11
  35.5 0.0 copy-done.22
  35.5 0.2 fusion.1
  35.7 10.2 %all-to-all-done.1.got_ref = bf16[32,16,128]{2,1,0:T(8,128)(2,1)S(1)} async-done(((bf16[32,16,128]{2,1,0:T(8,128)(2,1)}), bf16[32,16,128]{2,1,0:T(8,128)(2,1)S(1)}, u32[]{:S(2)}, u32[]{:S(2)}) %all-to-all-start.1) | async-done | bytes 131104 | tf_op jit(solution)/shard_map/all_to_all | solution.py:370
  45.9 0.1 broadcast_in_dim.43.count_ref
  46.0 0.0 copy-start
  46.0 1.4 %copy-done = bf16[3,512,512]{2,1,0:T(8,128)(2,1)S(1)} copy-done((bf16[3,512,512]{2,1,0:T(8,128)(2,1)S(1)}, bf16[3,512,512]{2,1,0:T(8,128)(2,1)}, u32[]{:S(2)}) %copy-start) | copy-done | bytes 1572888
  47.4 0.0 copy-start.2
  47.4 1.0 copy-done.2
  48.4 0.0 copy-start.3
  48.4 0.9 copy-done.3
  49.3 0.9 copy-done.4
  50.2 0.0 copy-start.6
  50.2 0.8 copy-done.6
  51.0 0.0 copy-start.8
  51.0 0.7 copy-done.8
  51.7 0.0 copy-start.12
  51.7 0.0 copy-start.13
  51.7 0.0 copy-start.14
  51.7 0.0 copy-start.15
  51.7 0.0 copy-start.16
  51.7 0.0 copy-start.17
  51.7 0.0 copy-start.18
  51.8 0.0 copy-start.19
  51.8 0.0 copy-start.20
  51.8 0.0 copy-start.21
  51.8 1.7 %mix.1 = (bf16[4,64,1408]{2,1,0:T(8,128)(2,1)S(1)}, f32[16,512]{1,0:T(8,128)}) custom-call(s32[16]{0:T(128)S(1)} %get-tuple-element.63.source_ref, s32[16]{0:T(128)S(1)} %get-tuple-element.65.count_ref, bf16[32,16,128]{2,1,0:T(8,128)(2,1)S(1)} %all-to-all-done.1.got_ref, f32[16,512]{1,0:T(8,128)S(1)} %copy-done.6, f32[5,512]{1,0:T(8,128)S(1)} %copy-done.8, ...), custom_call_target="tpu_custom_call" | custom-call | flops 113246208 | bytes 3221632 | tf_op jit(solution)/shard_map/mix/pallas_call | solution.py:68
  53.5 13.4 %all_to_all.31.got_ref = bf16[4,64,1408]{2,1,0:T(8,128)(2,1)S(1)} all-to-all(bf16[4,64,1408]{2,1,0:T(8,128)(2,1)S(1)} %get-tuple-element.73), channel_id=1, replica_groups=mesh['req'=32,'head'=4,'row'=4] {'row'}, dimensions={0} | all-to-all | bytes 1441792 | tf_op jit(solution)/shard_map/all_to_all | solution.py:385
  67.0 0.0 copy-done.12
  67.0 0.0 copy-done.13
  67.0 0.0 copy-done.14
  67.0 0.0 copy-done.15
  67.0 0.0 copy-done.16
  67.0 0.0 copy-done.17
  67.0 0.0 copy-done.18
  67.0 0.0 copy-done.19
  67.0 0.0 copy-done.20
  67.1 0.0 copy-done.21
  67.1 0.0 copy-start.1
  67.1 2.8 %state.1 = (f32[1024,128]{1,0:T(8,128)}, f32[64,128]{1,0:T(8,128)S(1)}, f32[64,128]{1,0:T(8,128)S(1)}, f32[4,8,128]{2,1,0:T(8,128)S(1)}) custom-call(s32[16,128]{1,0:T(8,128)S(1)} %broadcast_in_dim.43.count_ref, bf16[4,64,1408]{2,1,0:T(8,128)(2,1)S(1)} %all_to_all.31.got_ref, f32[1024,128]{1,0:T(8,128)S(1)} %bitcast.30, bf16[96,512]{1,0:T(8,128)(2,1)S(1)} %copy-done.13, ...), custom_call_target="tpu_custom_call" | custom-call | flops 805306368 | bytes 2361344 | tf_op jit(solution)/shard_map/state/pallas_call | solution.py:68
  69.9 6.5 %all_to_all.32.stat_ref = f32[4,8,128]{2,1,0:T(8,128)S(1)} all-to-all(f32[4,8,128]{2,1,0:T(8,128)S(1)} %get-tuple-element.75), channel_id=1, replica_groups=mesh['req'=32,'head'=4,'row'=4] {'row'}, dimensions={0} | all-to-all | bytes 32768 | tf_op jit(solution)/shard_map/all_to_all | solution.py:414
  76.5 0.0 copy-done.5
  76.5 0.0 copy-done.7
  76.5 1.0 norm.1
  77.5 18.9 %all_to_all.33.got_ref = bf16[32,4,128]{2,1,0:T(4,128)(2,1)S(1)} all-to-all(bf16[32,4,128]{2,1,0:T(4,128)(2,1)S(1)} %norm.1), channel_id=1, replica_groups=mesh['req'=32,'head'=4,'row'=4] {'req'}, dimensions={0} | all-to-all | bytes 65536 | tf_op jit(solution)/shard_map/all_to_all | solution.py:423
  96.3 0.0 copy-done.1
  96.3 0.8 output.1
  97.2 10.3 %all_to_all.34 = bf16[16,16,512]{2,1,0:T(8,128)(2,1)S(1)} all-to-all(bf16[16,16,512]{2,1,0:T(8,128)(2,1)S(1)} %output.1), channel_id=1, replica_groups=mesh['req'=32,'head'=4,'row'=4] {'head','row'}, dimensions={0} | all-to-all | bytes 524288 | tf_op jit(solution)/shard_map/all_to_all | solution.py:433
  107.5 0.6 reshape.62
  (6 shorter events, 0.1 us)
Async XLA Ops:
  0.6 0.7 copy-start.9
  1.3 0.7 copy-start.10
  2.0 33.5 %copy-start.11 = (s32[512]{0:T(512)S(1)}, s32[512]{0:T(512)}, u32[]{:S(2)}) copy-start(s32[512]{0:T(512)} %slot_ref.1) | copy-start | bytes 6148
  2.0 33.5 %copy-start.22 = (s32[512]{0:T(512)S(1)}, s32[512]{0:T(512)}, u32[]{:S(2)}) copy-start(s32[512]{0:T(512)} %param.25) | copy-start | bytes 6148
  12.7 33.2 %all-to-all-start.1 = ((bf16[32,16,128]{2,1,0:T(8,128)(2,1)}), bf16[32,16,128]{2,1,0:T(8,128)(2,1)S(1)}, u32[]{:S(2)}, u32[]{:S(2)}) async-start(bf16[32,16,128]{2,1,0:T(8,128)(2,1)} %get-tuple-element.44), calls=%async_computation.1 | async-start | bytes 262144 | tf_op jit(solution)/shard_map/all_to_all | solution.py:370
  46.0 1.4 %copy-start = (bf16[3,512,512]{2,1,0:T(8,128)(2,1)S(1)}, bf16[3,512,512]{2,1,0:T(8,128)(2,1)}, u32[]{:S(2)}) copy-start(bf16[3,512,512]{2,1,0:T(8,128)(2,1)} %get-tuple-element.69.proj_ref) | copy-start | bytes 4718596
  47.4 1.0 copy-start.2
  48.4 0.9 copy-start.3
  49.3 0.9 copy-start.4
  50.2 0.8 copy-start.6
  51.0 0.7 copy-start.8
  51.7 15.3 %copy-start.12 = (f32[16,8,1024]{2,1,0:T(8,128)S(1)}, f32[16,8,1024]{2,1,0:T(8,128)}, u32[]{:S(2)}) copy-start(f32[16,8,1024]{2,1,0:T(8,128)} %param.27) | copy-start | bytes 1572868
  51.7 15.3 %copy-start.13 = (bf16[96,512]{1,0:T(8,128)(2,1)S(1)}, bf16[96,512]{1,0:T(8,128)(2,1)}, u32[]{:S(2)}) copy-start(bf16[96,512]{1,0:T(8,128)(2,1)} %decay_ref.1) | copy-start | bytes 294916
  51.7 15.3 %copy-start.14 = (bf16[96,512]{1,0:T(8,128)(2,1)S(1)}, bf16[96,512]{1,0:T(8,128)(2,1)}, u32[]{:S(2)}) copy-start(bf16[96,512]{1,0:T(8,128)(2,1)} %learn_ref.1) | copy-start | bytes 294916
  51.7 15.3 %copy-start.15 = (f32[512]{0:T(512)S(1)}, f32[512]{0:T(512)}, u32[]{:S(2)}) copy-start(f32[512]{0:T(512)} %param.33) | copy-start | bytes 6148
  51.7 15.3 %copy-start.16 = (f32[512]{0:T(512)S(1)}, f32[512]{0:T(512)}, u32[]{:S(2)}) copy-start(f32[512]{0:T(512)} %param.36) | copy-start | bytes 6148
  51.7 15.3 %copy-start.17 = (f32[512]{0:T(512)S(1)}, f32[512]{0:T(512)}, u32[]{:S(2)}) copy-start(f32[512]{0:T(512)} %param.37) | copy-start | bytes 6148
  51.7 15.3 %copy-start.18 = (f32[512]{0:T(512)S(1)}, f32[512]{0:T(512)}, u32[]{:S(2)}) copy-start(f32[512]{0:T(512)} %param.38) | copy-start | bytes 6148
  51.8 15.3 %copy-start.19 = (bf16[512,128]{1,0:T(8,128)(2,1)S(1)}, bf16[512,128]{1,0:T(8,128)(2,1)}, u32[]{:S(2)}) copy-start(bf16[512,128]{1,0:T(8,128)(2,1)} %constant.21.clone.head_to_lanes_ref) | copy-start | bytes 393220
  51.8 15.3 %copy-start.20 = (bf16[256,256]{1,0:T(8,128)(2,1)S(1)}, bf16[256,256]{1,0:T(8,128)(2,1)}, u32[]{:S(2)}) copy-start(bf16[256,256]{1,0:T(8,128)(2,1)} %constant.19.clone.halves_ref) | copy-start | bytes 393220
  51.8 15.3 %copy-start.21 = (bf16[128,128]{1,0:T(8,128)(2,1)S(1)}, bf16[128,128]{1,0:T(8,128)(2,1)}, u32[]{:S(2)}) copy-start(bf16[128,128]{1,0:T(8,128)(2,1)} %constant.20.clone.same_head_ref) | copy-start | bytes 98308
  67.0 9.5 %copy-start.5 = (bf16[128,256]{1,0:T(8,128)(2,1)S(1)}, bf16[128,256]{1,0:T(8,128)(2,1)}, u32[]{:S(2)}) copy-start(bf16[128,256]{1,0:T(8,128)(2,1)} %constant.24.clone.unpack_ref) | copy-start | bytes 196612
  67.0 9.5 %copy-start.7 = (bf16[128,128]{1,0:T(8,128)(2,1)S(1)}, bf16[128,128]{1,0:T(8,128)(2,1)}, u32[]{:S(2)}) copy-start(bf16[128,128]{1,0:T(8,128)(2,1)} %constant.22.clone.to_natural_ref) | copy-start | bytes 98308
  67.1 29.3 %copy-start.1 = (bf16[8,16,2048]{2,1,0:T(8,128)(2,1)S(1)}, bf16[8,16,2048]{2,1,0:T(8,128)(2,1)}, u32[]{:S(2)}) copy-start(bf16[8,16,2048]{2,1,0:T(8,128)(2,1)} %param.41) | copy-start | bytes 1572868

commit v5 on v3

--- a/solution.py
+++ b/solution.py
@@ -162,10 +162,7 @@
     norm = jnp.concatenate([norm[0:TOK], norm[TOK:2 * TOK]], axis=1)
     key_dir = scaled * lax.rsqrt(norm + 1e-6)
     key_adj = key * (1.0 + (learn - 1.0) * correction_ref[...])
-    page_row = lax.broadcasted_iota(jnp.int32, (REQ_DEV, LANES), 0)
-    counts = jnp.zeros((REQ_DEV, LANES), jnp.int32)
-    for page in range(REQ_DEV):
-        counts = jnp.where(page_row == page, count_ref[page], counts)
+    counts = count_ref[...]
     live = jnp.concatenate([jnp.where(counts > t, 1.0, 0.0) for t in range(TS)], axis=0)
     live_wide = jnp.concatenate([live] * 4, axis=1)
     vectors = [
@@ -315,6 +312,7 @@
     groups_of = lax.shift_right_logical(jnp.arange(caller_sheet_slot.shape[0], dtype=jnp.int32), 4)
     source = jnp.sum(jnp.where(holder, groups_of[None, :], 0), axis=1)
     count = jnp.sum(jnp.where(holder, genuine_symbol_number[None, :], 0), axis=1)
+    count_wide = jnp.broadcast_to(count[:, None], (REQ_DEV, LANES))
     first = first.astype(jnp.int32)[None]
     gain = groupwise_gain.reshape(HEADS, 8, 2).transpose(2, 0, 1).reshape(1, VALS)
     reward = reward_coefficients.reshape(1, FEATS)
@@ -326,16 +324,20 @@
         [pl.BlockSpec(memory_space=pltpu.HBM)],
         (tiles,),
         scratch=[pltpu.SemaphoreType.DMA((4,))],
+        flops=6 * 10**9,
         name="fan",
         out_spec=ANY,
     )
     mine = lax.all_to_all(everywhere, "head", 0, 0, tiled=True).reshape(REQ_DEV, 16, LANES)
-    mine, source, count, gain, reward = lax.optimization_barrier((mine, source, count, gain, reward))
+    mine, source, count, count_wide, gain, reward = lax.optimization_barrier(
+        (mine, source, count, count_wide, gain, reward)
+    )
     packed = call(
         pack_kernel,
         [shaped((groups, 16, LANES), BF16)],
         [SMEM, SMEM, VMEM],
         (caller_sheet_slot, first, mine),
+        flops=6 * 10**9,
         name="pack",
     )
     got = lax.all_to_all(packed, "req", 0, 0, tiled=True)
@@ -362,9 +364,9 @@
             shaped((TOK, LANES), F32),
             shaped((4, 8, LANES), F32),
         ],
-        [SMEM] + [VMEM] * 12,
+        [VMEM] * 13,
         (
-            count,
+            count_wide,
             sums,
             sheets,
             fading_widen_projector,

time: 109 us -> 102 us (0.936)
  local copies, waits for them, and re-layouts: 9.48 us -> 1.83 us
  waiting for transfers between devices: 1.89 us -> 3.93 us
    unnamed x45 -> x49, local copies, waits for them, and re-layouts: 7.93 us -> 0.9 us
    all_to_all x1, waiting for transfers between devices: 1.89 us -> 3.93 us  [per_device(): lax.all_to_all(everywhere, 'head', 0, 0, tiled=True)]
  transfers between devices with their start and end apart: 1 -> 1, of which waited for: 1 -> 1; matrix products, arithmetic and copies ran while one was open for 2% -> 0% of each run, Pallas kernels for 0% -> 0%
where the time goes in v5:
time: 102 us
  blocking collectives  82.3 us (81%)
  Pallas kernels  7.74 us (8%)
  starting transfers between devices  5.02 us (5%)
  waiting for transfers between devices  3.93 us (4%)
  local copies, waits for them, and re-layouts  1.83 us (2%)
    all_to_all x1, blocking collectives, per_device(): got = lax.all_to_all(packed, 'req', 0, 0, tiled=True)  33.1 us
    all_to_all x1, blocking collectives, per_device(): back = lax.all_to_all(leaving, 'req', 0, 0, tiled=True)  18.9 us
    all_to_all x1, blocking collectives, per_device(): sums = lax.all_to_all(partial, 'row', 0, 0, tiled=True)  13.4 us
    all_to_all x1, blocking collectives, per_device(): arrived = lax.all_to_all(terms, ('head', 'row'), 0, 0, tiled=True)  10.3 us
    pallas_call x6, Pallas kernels, call(): pl.pallas_call(kernel, out_shape=outs[0] if single else outs, in_specs=in...  7.74 us
    all_to_all x1, blocking collectives, per_device(): stats = lax.all_to_all(stat, 'row', 0, 0, tiled=True)  6.55 us
    all_to_all x1, starting transfers between devices, per_device(): lax.all_to_all(everywhere, 'head', 0, 0, tiled=True)  5.02 us
    all_to_all x1, waiting for transfers between devices, per_device(): lax.all_to_all(everywhere, 'head', 0, 0, tiled=True)  3.93 us
  transfers between devices with their start and end apart: 1, of which 1 were waited for; matrix products, arithmetic and copies ran while one was open for 0% of the time, Pallas kernels for 0%

profile of v5, /device:TPU:1, one launch (start us, length us, event | category | flops | bytes accessed | tf_op | source)
XLA Modules:
  0.0 101.9 jit_solution(13782669760150832183)
XLA Ops:
  0.6 0.0 copy-start.13
  0.6 0.7 copy-done.13
  1.4 0.0 copy-start.9
  1.4 0.0 copy-start.23
  1.4 0.0 copy-start.22
  1.4 0.0 copy-start.21
  1.4 0.7 fan.1
  2.0 5.0 %all-to-all-start = ((bf16[4,4,16,128]{3,2,1,0:T(8,128)(2,1)}), bf16[4,4,16,128]{3,2,1,0:T(8,128)(2,1)S(1)}, u32[]{:S(2)}, u32[]{:S(2)}) async-start(bf16[4,4,16,128]{3,2,1,0:T(8,128)(2,1)} %fan.1), calls=%async_computation | async-start | bytes 131072 | tf_op jit(solution)/shard_map/all_to_all | solution.py:331
  7.1 0.0 copy-done.9
  7.1 0.0 copy-done.23
  7.1 0.2 fusion.1
  7.3 0.0 copy-done.22
  7.3 0.1 reshape.58.reward_ref
  7.4 0.0 copy-done.21
  7.4 0.1 copy.31
  7.4 0.1 copy.32
  7.5 0.1 reshape.57.gain_ref
  7.6 3.9 %all-to-all-done = bf16[4,4,16,128]{3,2,1,0:T(8,128)(2,1)S(1)} async-done(((bf16[4,4,16,128]{3,2,1,0:T(8,128)(2,1)}), bf16[4,4,16,128]{3,2,1,0:T(8,128)(2,1)S(1)}, u32[]{:S(2)}, u32[]{:S(2)}) %all-to-all-start) | async-done | bytes 65568 | tf_op jit(solution)/shard_map/all_to_all | solution.py:331
  11.5 0.1 broadcast_in_dim.47.count_ref
  11.6 0.0 copy-start
  11.6 0.0 copy-start.2
  11.6 0.0 copy-start.6
  11.6 0.0 copy-start.8
  11.6 0.7 pack.1
  12.3 33.1 %all_to_all.30.got_ref = bf16[32,16,128]{2,1,0:T(8,128)(2,1)S(1)} all-to-all(bf16[32,16,128]{2,1,0:T(8,128)(2,1)S(1)} %pack.1), channel_id=1, replica_groups=mesh['req'=32,'head'=4,'row'=4] {'req'}, dimensions={0} | all-to-all | bytes 262144 | tf_op jit(solution)/shard_map/all_to_all | solution.py:343
  45.4 0.0 copy-done
  45.4 0.0 copy-done.2
  45.4 0.0 copy-done.3
  45.4 0.0 copy-done.4
  45.5 0.0 copy-done.6
  45.5 0.0 copy-done.8
  45.5 0.0 copy-start.10
  45.5 0.0 copy-start.11
  45.5 0.0 copy-start.12
  45.5 0.0 copy-start.14
  45.5 0.0 copy-start.15
  45.5 0.0 copy-start.16
  45.5 0.0 copy-start.17
  45.6 0.0 copy-start.18
  45.6 0.0 copy-start.19
  45.6 0.0 copy-start.20
  45.6 1.7 %mix.1 = (bf16[4,64,1408]{2,1,0:T(8,128)(2,1)S(1)}, f32[16,512]{1,0:T(8,128)}) custom-call(s32[16]{0:T(128)S(1)} %get-tuple-element.15.source_ref, s32[16]{0:T(128)S(1)} %get-tuple-element.17.count_ref, bf16[32,16,128]{2,1,0:T(8,128)(2,1)S(1)} %all_to_all.30.got_ref, f32[16,512]{1,0:T(8,128)S(1)} %copy-done.6, f32[5,512]{1,0:T(8,128)S(1)} %copy-done.8, ...), custom_call_target="tpu_custom_call" | custom-call | flops 113246208 | bytes 3221632 | tf_op jit(solution)/shard_map/mix/pallas_call | solution.py:68
  47.3 13.4 %all_to_all.31.got_ref = bf16[4,64,1408]{2,1,0:T(8,128)(2,1)S(1)} all-to-all(bf16[4,64,1408]{2,1,0:T(8,128)(2,1)S(1)} %get-tuple-element.19), channel_id=1, replica_groups=mesh['req'=32,'head'=4,'row'=4] {'row'}, dimensions={0} | all-to-all | bytes 1441792 | tf_op jit(solution)/shard_map/all_to_all | solution.py:358
  60.8 0.0 copy-done.10
  60.8 0.0 copy-done.11
  60.8 0.0 copy-done.12
  60.8 0.0 copy-done.14
  60.8 0.0 copy-done.15
  60.8 0.0 copy-done.16
  60.8 0.0 copy-done.17
  60.8 0.0 copy-done.18
  60.9 0.0 copy-done.19
  60.9 0.0 copy-done.20
  60.9 0.0 copy-start.1
  60.9 2.9 %state.1 = (f32[1024,128]{1,0:T(8,128)}, f32[64,128]{1,0:T(8,128)S(1)}, f32[64,128]{1,0:T(8,128)S(1)}, f32[4,8,128]{2,1,0:T(8,128)S(1)}) custom-call(s32[16,128]{1,0:T(8,128)S(1)} %broadcast_in_dim.47.count_ref, bf16[4,64,1408]{2,1,0:T(8,128)(2,1)S(1)} %all_to_all.31.got_ref, f32[1024,128]{1,0:T(8,128)S(1)} %bitcast.31, bf16[96,512]{1,0:T(8,128)(2,1)S(1)} %copy-done.11, ...), custom_call_target="tpu_custom_call" | custom-call | flops 805306368 | bytes 2361344 | tf_op jit(solution)/shard_map/state/pallas_call | solution.py:68
  63.7 6.5 %all_to_all.32.stat_ref = f32[4,8,128]{2,1,0:T(8,128)S(1)} all-to-all(f32[4,8,128]{2,1,0:T(8,128)S(1)} %get-tuple-element.21), channel_id=1, replica_groups=mesh['req'=32,'head'=4,'row'=4] {'row'}, dimensions={0} | all-to-all | bytes 32768 | tf_op jit(solution)/shard_map/all_to_all | solution.py:387
  70.3 0.0 copy-done.5
  70.3 0.0 copy-done.7
  70.3 1.0 norm.1
  71.3 18.9 %all_to_all.33.got_ref = bf16[32,4,128]{2,1,0:T(4,128)(2,1)S(1)} all-to-all(bf16[32,4,128]{2,1,0:T(4,128)(2,1)S(1)} %norm.1), channel_id=1, replica_groups=mesh['req'=32,'head'=4,'row'=4] {'req'}, dimensions={0} | all-to-all | bytes 65536 | tf_op jit(solution)/shard_map/all_to_all | solution.py:396
  90.2 0.0 copy-done.1
  90.2 0.8 output.1
  91.0 10.3 %all_to_all.34 = bf16[16,16,512]{2,1,0:T(8,128)(2,1)S(1)} all-to-all(bf16[16,16,512]{2,1,0:T(8,128)(2,1)S(1)} %output.1), channel_id=1, replica_groups=mesh['req'=32,'head'=4,'row'=4] {'head','row'}, dimensions={0} | all-to-all | bytes 524288 | tf_op jit(solution)/shard_map/all_to_all | solution.py:406
  101.3 0.6 reshape.62
  (7 shorter events, 0.1 us)
Async XLA Ops:
  0.6 0.7 copy-start.13
  1.4 5.7 %copy-start.9 = (s32[512]{0:T(512)S(1)}, s32[512]{0:T(512)}, u32[]{:S(2)}) copy-start(s32[512]{0:T(512)} %slot_ref.3) | copy-start | bytes 6148
  1.4 5.7 %copy-start.23 = (s32[512]{0:T(512)S(1)}, s32[512]{0:T(512)}, u32[]{:S(2)}) copy-start(s32[512]{0:T(512)} %param.25) | copy-start | bytes 6148
  1.4 5.9 %copy-start.22 = (f32[8,64]{1,0:T(8,128)S(1)}, f32[8,64]{1,0:T(8,128)}, u32[]{:S(2)}) copy-start(f32[8,64]{1,0:T(8,128)} %param.39) | copy-start | bytes 6148
  1.4 6.0 %copy-start.21 = (f32[8,16]{1,0:T(8,128)S(1)}, f32[8,16]{1,0:T(8,128)}, u32[]{:S(2)}) copy-start(f32[8,16]{1,0:T(8,128)} %param.40) | copy-start | bytes 1540
  2.0 9.5 %all-to-all-start = ((bf16[4,4,16,128]{3,2,1,0:T(8,128)(2,1)}), bf16[4,4,16,128]{3,2,1,0:T(8,128)(2,1)S(1)}, u32[]{:S(2)}, u32[]{:S(2)}) async-start(bf16[4,4,16,128]{3,2,1,0:T(8,128)(2,1)} %fan.1), calls=%async_computation | async-start | bytes 131072 | tf_op jit(solution)/shard_map/all_to_all | solution.py:331
  11.6 33.8 %copy-start = (bf16[3,512,512]{2,1,0:T(8,128)(2,1)S(1)}, bf16[3,512,512]{2,1,0:T(8,128)(2,1)}, u32[]{:S(2)}) copy-start(bf16[3,512,512]{2,1,0:T(8,128)(2,1)} %proj_ref.1) | copy-start | bytes 4718596
  11.6 33.8 %copy-start.2 = (bf16[512,512]{1,0:T(8,128)(2,1)S(1)}, bf16[512,512]{1,0:T(8,128)(2,1)}, u32[]{:S(2)}) copy-start(bf16[512,512]{1,0:T(8,128)(2,1)} %constant.31.clone.spread_ref) | copy-start | bytes 1572868
  11.6 33.8 %copy-start.3 = (bf16[512,96]{0,1:T(8,128)(2,1)S(1)}, bf16[512,96]{0,1:T(8,128)(2,1)}, u32[]{:S(2)}) copy-start(bf16[512,96]{0,1:T(8,128)(2,1)} %param.31) | copy-start | bytes 294916
  11.6 33.8 %copy-start.4 = (bf16[512,96]{0,1:T(8,128)(2,1)S(1)}, bf16[512,96]{0,1:T(8,128)(2,1)}, u32[]{:S(2)}) copy-start(bf16[512,96]{0,1:T(8,128)(2,1)} %param.34) | copy-start | bytes 294916
  11.6 33.8 %copy-start.6 = (f32[16,512]{1,0:T(8,128)S(1)}, f32[16,512]{1,0:T(8,128)}, u32[]{:S(2)}) copy-start(f32[16,512]{1,0:T(8,128)} %shift_ref.1) | copy-start | bytes 98308
  11.6 33.8 %copy-start.8 = (f32[5,512]{1,0:T(8,128)S(1)}, f32[5,512]{1,0:T(8,128)}, u32[]{:S(2)}) copy-start(f32[5,512]{1,0:T(8,128)} %blend_ref.1) | copy-start | bytes 30724
  45.5 15.3 %copy-start.10 = (f32[16,8,1024]{2,1,0:T(8,128)S(1)}, f32[16,8,1024]{2,1,0:T(8,128)}, u32[]{:S(2)}) copy-start(f32[16,8,1024]{2,1,0:T(8,128)} %param.27) | copy-start | bytes 1572868
  45.5 15.3 %copy-start.11 = (bf16[96,512]{1,0:T(8,128)(2,1)S(1)}, bf16[96,512]{1,0:T(8,128)(2,1)}, u32[]{:S(2)}) copy-start(bf16[96,512]{1,0:T(8,128)(2,1)} %decay_ref.1) | copy-start | bytes 294916
  45.5 15.3 %copy-start.12 = (bf16[96,512]{1,0:T(8,128)(2,1)S(1)}, bf16[96,512]{1,0:T(8,128)(2,1)}, u32[]{:S(2)}) copy-start(bf16[96,512]{1,0:T(8,128)(2,1)} %learn_ref.1) | copy-start | bytes 294916
  45.5 15.3 %copy-start.14 = (f32[512]{0:T(512)S(1)}, f32[512]{0:T(512)}, u32[]{:S(2)}) copy-start(f32[512]{0:T(512)} %param.33) | copy-start | bytes 6148
  45.5 15.3 %copy-start.15 = (f32[512]{0:T(512)S(1)}, f32[512]{0:T(512)}, u32[]{:S(2)}) copy-start(f32[512]{0:T(512)} %param.36) | copy-start | bytes 6148
  45.5 15.3 %copy-start.16 = (f32[512]{0:T(512)S(1)}, f32[512]{0:T(512)}, u32[]{:S(2)}) copy-start(f32[512]{0:T(512)} %param.37) | copy-start | bytes 6148
  45.5 15.3 %copy-start.17 = (f32[512]{0:T(512)S(1)}, f32[512]{0:T(512)}, u32[]{:S(2)}) copy-start(f32[512]{0:T(512)} %param.38) | copy-start | bytes 6148
  45.6 15.3 %copy-start.18 = (bf16[512,128]{1,0:T(8,128)(2,1)S(1)}, bf16[512,128]{1,0:T(8,128)(2,1)}, u32[]{:S(2)}) copy-start(bf16[512,128]{1,0:T(8,128)(2,1)} %constant.29.clone.head_to_lanes_ref) | copy-start | bytes 393220
  45.6 15.3 %copy-start.19 = (bf16[256,256]{1,0:T(8,128)(2,1)S(1)}, bf16[256,256]{1,0:T(8,128)(2,1)}, u32[]{:S(2)}) copy-start(bf16[256,256]{1,0:T(8,128)(2,1)} %constant.27.clone.halves_ref) | copy-start | bytes 393220
  45.6 15.3 %copy-start.20 = (bf16[128,128]{1,0:T(8,128)(2,1)S(1)}, bf16[128,128]{1,0:T(8,128)(2,1)}, u32[]{:S(2)}) copy-start(bf16[128,128]{1,0:T(8,128)(2,1)} %constant.28.clone.same_head_ref) | copy-start | bytes 98308
  60.8 9.5 %copy-start.5 = (bf16[128,256]{1,0:T(8,128)(2,1)S(1)}, bf16[128,256]{1,0:T(8,128)(2,1)}, u32[]{:S(2)}) copy-start(bf16[128,256]{1,0:T(8,128)(2,1)} %constant.32.clone.unpack_ref) | copy-start | bytes 196612
  60.8 9.5 %copy-start.7 = (bf16[128,128]{1,0:T(8,128)(2,1)S(1)}, bf16[128,128]{1,0:T(8,128)(2,1)}, u32[]{:S(2)}) copy-start(bf16[128,128]{1,0:T(8,128)(2,1)} %constant.30.clone.to_natural_ref) | copy-start | bytes 98308
  60.9 29.3 %copy-start.1 = (bf16[8,16,2048]{2,1,0:T(8,128)(2,1)S(1)}, bf16[8,16,2048]{2,1,0:T(8,128)(2,1)}, u32[]{:S(2)}) copy-start(bf16[8,16,2048]{2,1,0:T(8,128)(2,1)} %param.41) | copy-start | bytes 1572868

commit v6 on v5

--- a/solution.py
+++ b/solution.py
@@ -22,6 +22,7 @@
 WIDTH = LEARN_AT + LANES
 F32 = jnp.float32
 BF16 = jnp.bfloat16
+FIRST_A, FIRST_B, FIRST_C, FIRST_D, FIRST_E, FIRST_F = 2, 17, 2, 2, 17, 10
 VMEM = pl.BlockSpec(memory_space=pltpu.VMEM)
 SMEM = pl.BlockSpec(memory_space=pltpu.SMEM)
 ANY = pl.BlockSpec(memory_space=pl.ANY)
@@ -61,6 +62,11 @@
     return dot(high, b) + dot(low, b)
 
 
+def exchange(x, axes, first):
+    order = [[k ^ first for k in range(x.shape[0])]] if first else None
+    return lax.all_to_all(x, axes, 0, 0, tiled=True, axis_index_groups=order)
+
+
 def call(kernel, outs, in_specs, args, scratch=(), flops=0, name=None, out_spec=VMEM):
     size = sum(int(np.prod(a.shape)) * a.dtype.itemsize for a in args)
     size += sum(int(np.prod(o.shape)) * o.dtype.itemsize for o in outs)
@@ -87,7 +93,7 @@
 
 def pack_kernel(slot_ref, first_ref, x_ref, out_ref):
     for q in range(REQ_DEV):
-        out_ref[slot_ref[first_ref[0] + q] // REQ_DEV] = x_ref[q]
+        out_ref[(slot_ref[first_ref[0] + q] // REQ_DEV) ^ FIRST_B] = x_ref[q ^ (FIRST_A * 4)]
 
 
 def mix_kernel(
@@ -95,7 +101,7 @@
     out_ref, new_shift_ref, tokens,
 ):
     for page in range(REQ_DEV):
-        tile = got_ref[source_ref[page]].astype(F32)
+        tile = got_ref[source_ref[page] ^ FIRST_B].astype(F32)
         for part in range(4):
             tokens[part, pl.ds(page, TS, stride=REQ_DEV), :] = tile[part * TS:(part + 1) * TS]
     current = jnp.concatenate([tokens[part] for part in range(4)], axis=1)
@@ -119,7 +125,8 @@
     for part in range(4):
         out_ref[part, :, 0:FEATS] = recept
         out_ref[part, :, FEATS:2 * FEATS] = key
-        out_ref[part, :, 2 * FEATS:DECAY_AT] = value[:, part * VALS:(part + 1) * VALS]
+        row = part ^ FIRST_C
+        out_ref[part, :, 2 * FEATS:DECAY_AT] = value[:, row * VALS:(row + 1) * VALS]
         out_ref[part, :, DECAY_AT:LEARN_AT] = jnp.concatenate([decay, pad], axis=1)
         out_ref[part, :, LEARN_AT:WIDTH] = jnp.concatenate([learn, pad], axis=1)
     for page in range(REQ_DEV):
@@ -264,16 +271,18 @@
     normed = (reading_ref[...] - opened[:, 0:LANES]) * opened[:, LANES:256] * gain_ref[...] + bonus_ref[...]
     rows[...] = dot(normed.astype(BF16), to_natural_ref[...])
     for page in range(REQ_DEV):
-        out_ref[source_ref[page]] = rows[pl.ds(page, TS, stride=REQ_DEV), :].astype(BF16)
+        out_ref[source_ref[page] ^ FIRST_E] = rows[pl.ds(page, TS, stride=REQ_DEV), :].astype(BF16)
 
 
 def output_kernel(slot_ref, first_ref, got_ref, proj_ref, out_ref, rows):
     for q in range(REQ_DEV):
-        rows[q * TS:(q + 1) * TS, :] = got_ref[slot_ref[first_ref[0] + q] // REQ_DEV].astype(F32)
+        rows[q * TS:(q + 1) * TS, :] = got_ref[
+            (slot_ref[first_ref[0] + q] // REQ_DEV) ^ FIRST_E
+        ].astype(F32)
     terms = dot(rows[...].astype(BF16), proj_ref[...]).astype(BF16)
     for head in range(4):
         for part in range(4):
-            out_ref[head * 4 + part] = terms[
+            out_ref[(head * 4 + part) ^ FIRST_F] = terms[
                 head * REQ_DEV:(head + 1) * REQ_DEV, part * FEATS:(part + 1) * FEATS
             ]
 
@@ -328,7 +337,7 @@
         name="fan",
         out_spec=ANY,
     )
-    mine = lax.all_to_all(everywhere, "head", 0, 0, tiled=True).reshape(REQ_DEV, 16, LANES)
+    mine = exchange(everywhere, "head", FIRST_A).reshape(REQ_DEV, 16, LANES)
     mine, source, count, count_wide, gain, reward = lax.optimization_barrier(
         (mine, source, count, count_wide, gain, reward)
     )
@@ -340,7 +349,7 @@
         flops=6 * 10**9,
         name="pack",
     )
-    got = lax.all_to_all(packed, "req", 0, 0, tiled=True)
+    got = exchange(packed, "req", FIRST_B)
     partial, new_shift = call(
         mix_kernel,
         [shaped((4, TOK, WIDTH), BF16), shaped((REQ_DEV, FEATS), F32)],
@@ -355,7 +364,7 @@
     )
     sheets = memory_sheets.reshape(REQ_DEV, HEADS, 8, LANES).transpose(0, 2, 1, 3)
     sheets = sheets.reshape(REQ_DEV * HEADS * 8, LANES)
-    sums = lax.all_to_all(partial, "row", 0, 0, tiled=True)
+    sums = exchange(partial, "row", FIRST_C)
     new_state, reading, bonus, stat = call(
         state_kernel,
         [
@@ -384,7 +393,7 @@
         flops=2 * 3 * TS * 512 * 256 * 256,
         name="state",
     )
-    stats = lax.all_to_all(stat, "row", 0, 0, tiled=True)
+    stats = exchange(stat, "row", FIRST_D)
     leaving = call(
         norm_kernel,
         [shaped((groups, TS, LANES), BF16)],
@@ -393,7 +402,7 @@
         scratch=[pltpu.VMEM((TOK, LANES), F32)],
         name="norm",
     )
-    back = lax.all_to_all(leaving, "req", 0, 0, tiled=True)
+    back = exchange(leaving, "req", FIRST_E)
     terms = call(
         output_kernel,
         [shaped((16, 16, FEATS), BF16)],
@@ -403,7 +412,7 @@
         flops=2 * TOK * VALS * 4 * FEATS,
         name="output",
     )
-    arrived = lax.all_to_all(terms, ("head", "row"), 0, 0, tiled=True)
+    arrived = exchange(terms, ("head", "row"), FIRST_F)
     mixed = jnp.sum(arrived.astype(F32), axis=0).astype(BF16).reshape(4, TS, FEATS)
     new_state = new_state.reshape(REQ_DEV, 8, HEADS, LANES).transpose(0, 2, 1, 3)
     return (mixed, new_state.reshape(REQ_DEV, HEADS, 8 * LANES), new_shift)

time: 102 us -> 95.2 us (0.933)
  blocking collectives: 82.3 us -> 75.8 us
  waiting for transfers between devices: 3.93 us -> 1.16 us
  starting transfers between devices: 5.02 us -> 7.01 us
    all_to_all x5, blocking collectives: 82.3 us -> 75.8 us  [exchange(): return lax.all_to_all(x, axes, 0, 0, tiled=True, axis_index_groups=order)]
    all_to_all x1, waiting for transfers between devices: 3.93 us -> 1.16 us  [exchange(): return lax.all_to_all(x, axes, 0, 0, tiled=True, axis_index_groups=order)]
    all_to_all x1, starting transfers between devices: 5.02 us -> 7.01 us  [exchange(): return lax.all_to_all(x, axes, 0, 0, tiled=True, axis_index_groups=order)]
  transfers between devices with their start and end apart: 1 -> 1, of which waited for: 1 -> 1; matrix products, arithmetic and copies ran while one was open for 0% -> 1% of each run, Pallas kernels for 0% -> 0%
where the time goes in v6:
time: 95.2 us; the launch traced here: 94.7 us
  blocking collectives  75.8 us (80%)
  Pallas kernels  7.75 us (8%)
  starting transfers between devices  7.01 us (7%)
  local copies, waits for them, and re-layouts  1.83 us (2%)
  waiting for transfers between devices  1.16 us (1%)
    all_to_all x5, blocking collectives, exchange(): return lax.all_to_all(x, axes, 0, 0, tiled=True, axis_index_groups=order)  75.8 us
    pallas_call x6, Pallas kernels, call(): pl.pallas_call(kernel, out_shape=outs[0] if single else outs, in_specs=in...  7.75 us
    all_to_all x1, starting transfers between devices, exchange(): return lax.all_to_all(x, axes, 0, 0, tiled=True, axis_index_groups=order)  7.01 us
  transfers between devices with their start and end apart: 1, of which 1 were waited for; matrix products, arithmetic and copies ran while one was open for 1% of the time, Pallas kernels for 0%

profile of v6, /device:TPU:1, one launch (start us, length us, event | category | flops | bytes accessed | tf_op | source)
XLA Modules:
  0.0 94.7 jit_solution(12772894560076646402)
XLA Ops:
  0.6 0.0 copy-start.13
  0.6 0.7 copy-done.13
  1.4 0.0 copy-start.9
  1.4 0.0 copy-start.23
  1.4 0.0 copy-start.22
  1.4 0.0 copy-start.21
  1.4 0.7 fan.1
  2.0 7.0 %all-to-all-start = ((bf16[4,4,16,128]{3,2,1,0:T(8,128)(2,1)}), bf16[4,4,16,128]{3,2,1,0:T(8,128)(2,1)S(1)}, u32[]{:S(2)}, u32[]{:S(2)}) async-start(bf16[4,4,16,128]{3,2,1,0:T(8,128)(2,1)} %fan.1), calls=%async_computation | async-start | bytes 131072 | tf_op jit(solution)/shard_map/all_to_all | solution.py:67
  9.0 0.0 copy-done.9
  9.1 0.0 copy-done.23
  9.1 0.2 fusion.1
  9.2 0.0 copy-done.22
  9.3 0.1 reshape.58.reward_ref
  9.3 0.0 copy-done.21
  9.3 0.1 copy.31
  9.4 0.1 copy.32
  9.5 0.1 reshape.57.gain_ref
  9.6 1.2 %all-to-all-done = bf16[4,4,16,128]{3,2,1,0:T(8,128)(2,1)S(1)} async-done(((bf16[4,4,16,128]{3,2,1,0:T(8,128)(2,1)}), bf16[4,4,16,128]{3,2,1,0:T(8,128)(2,1)S(1)}, u32[]{:S(2)}, u32[]{:S(2)}) %all-to-all-start) | async-done | bytes 65568 | tf_op jit(solution)/shard_map/all_to_all | solution.py:67
  10.7 0.1 broadcast_in_dim.47.count_ref
  10.8 0.0 copy-start
  10.8 0.0 copy-start.2
  10.8 0.0 copy-start.6
  10.8 0.0 copy-start.8
  10.8 0.7 pack.1
  11.5 26.9 %all_to_all.30.got_ref = bf16[32,16,128]{2,1,0:T(8,128)(2,1)S(1)} all-to-all(bf16[32,16,128]{2,1,0:T(8,128)(2,1)S(1)} %pack.1), channel_id=1, replica_groups={{272,256,304,288,336,320,368,352,400,384,432,416,464,448,496,480,16,0,4..., dimensions={0} | all-to-all | bytes 262144 | tf_op jit(solution)/shard_map/all_to_all | solution.py:67
  38.4 0.0 copy-done
  38.4 0.0 copy-done.2
  38.4 0.0 copy-done.3
  38.4 0.0 copy-done.4
  38.5 0.0 copy-done.6
  38.5 0.0 copy-done.8
  38.5 0.0 copy-start.10
  38.5 0.0 copy-start.11
  38.5 0.0 copy-start.12
  38.5 0.0 copy-start.14
  38.5 0.0 copy-start.15
  38.5 0.0 copy-start.16
  38.5 0.0 copy-start.17
  38.6 0.0 copy-start.18
  38.6 0.0 copy-start.19
  38.6 0.0 copy-start.20
  38.6 1.8 %mix.1 = (bf16[4,64,1408]{2,1,0:T(8,128)(2,1)S(1)}, f32[16,512]{1,0:T(8,128)}) custom-call(s32[16]{0:T(128)S(1)} %get-tuple-element.15.source_ref, s32[16]{0:T(128)S(1)} %get-tuple-element.17.count_ref, bf16[32,16,128]{2,1,0:T(8,128)(2,1)S(1)} %all_to_all.30.got_ref, f32[16,512]{1,0:T(8,128)S(1)} %copy-done.6, f32[5,512]{1,0:T(8,128)S(1)} %copy-done.8, ...), custom_call_target="tpu_custom_call" | custom-call | flops 113246208 | bytes 3221632 | tf_op jit(solution)/shard_map/mix/pallas_call | solution.py:74
  40.3 13.8 %all_to_all.31.got_ref = bf16[4,64,1408]{2,1,0:T(8,128)(2,1)S(1)} all-to-all(bf16[4,64,1408]{2,1,0:T(8,128)(2,1)S(1)} %get-tuple-element.19), channel_id=1, replica_groups={{2,3,0,1},{6,7,4,5},{10,11,8,9},{14,15,12,13},{18,19,16,17},{22,23,20,2..., dimensions={0} | all-to-all | bytes 1441792 | tf_op jit(solution)/shard_map/all_to_all | solution.py:67
  54.2 0.0 copy-done.10
  54.2 0.0 copy-done.11
  54.2 0.0 copy-done.12
  54.2 0.0 copy-done.14
  54.2 0.0 copy-done.15
  54.2 0.0 copy-done.16
  54.2 0.0 copy-done.17
  54.2 0.0 copy-done.18
  54.2 0.0 copy-done.19
  54.2 0.0 copy-done.20
  54.2 0.0 copy-start.1
  54.3 2.9 %state.1 = (f32[1024,128]{1,0:T(8,128)}, f32[64,128]{1,0:T(8,128)S(1)}, f32[64,128]{1,0:T(8,128)S(1)}, f32[4,8,128]{2,1,0:T(8,128)S(1)}) custom-call(s32[16,128]{1,0:T(8,128)S(1)} %broadcast_in_dim.47.count_ref, bf16[4,64,1408]{2,1,0:T(8,128)(2,1)S(1)} %all_to_all.31.got_ref, f32[1024,128]{1,0:T(8,128)S(1)} %bitcast.31, bf16[96,512]{1,0:T(8,128)(2,1)S(1)} %copy-done.11, ...), custom_call_target="tpu_custom_call" | custom-call | flops 805306368 | bytes 2361344 | tf_op jit(solution)/shard_map/state/pallas_call | solution.py:74
  57.1 6.2 %all_to_all.32.stat_ref = f32[4,8,128]{2,1,0:T(8,128)S(1)} all-to-all(f32[4,8,128]{2,1,0:T(8,128)S(1)} %get-tuple-element.21), channel_id=1, replica_groups={{2,3,0,1},{6,7,4,5},{10,11,8,9},{14,15,12,13},{18,19,16,17},{22,23,20,2..., dimensions={0} | all-to-all | bytes 32768 | tf_op jit(solution)/shard_map/all_to_all | solution.py:67
  63.3 0.0 copy-done.5
  63.3 0.0 copy-done.7
  63.3 1.0 %norm.1 = bf16[32,4,128]{2,1,0:T(4,128)(2,1)S(1)} custom-call(s32[16]{0:T(128)S(1)} %get-tuple-element.15.source_ref, f32[4,8,128]{2,1,0:T(8,128)S(1)} %all_to_all.32.stat_ref, f32[64,128]{1,0:T(8,128)S(1)} %get-tuple-element.22.reading_ref, f32[64,128]{1,0:T(8,128)S(1)} %get-tuple-element.23.bonus_ref, f32[1,128]{1,0:T(1,128)S(1)} %reshape.57.gain_ref, ...), custom_call_target="tpu_custom_call" | custom-call | bytes 213568 | tf_op jit(solution)/shard_map/norm/pallas_call | solution.py:74
  64.3 17.0 %all_to_all.33.got_ref = bf16[32,4,128]{2,1,0:T(4,128)(2,1)S(1)} all-to-all(bf16[32,4,128]{2,1,0:T(4,128)(2,1)S(1)} %norm.1), channel_id=1, replica_groups={{272,256,304,288,336,320,368,352,400,384,432,416,464,448,496,480,16,0,4..., dimensions={0} | all-to-all | bytes 65536 | tf_op jit(solution)/shard_map/all_to_all | solution.py:67
  81.2 0.0 copy-done.1
  81.2 0.8 output.1
  82.1 12.0 %all_to_all.34 = bf16[16,16,512]{2,1,0:T(8,128)(2,1)S(1)} all-to-all(bf16[16,16,512]{2,1,0:T(8,128)(2,1)S(1)} %output.1), channel_id=1, replica_groups={{10,11,8,9,14,15,12,13,2,3,0,1,6,7,4,5},{26,27,24,25,30,31,28,29,18,19,..., dimensions={0} | all-to-all | bytes 524288 | tf_op jit(solution)/shard_map/all_to_all | solution.py:67
  94.1 0.6 reshape.62
  (7 shorter events, 0.1 us)
Async XLA Ops:
  0.6 0.7 copy-start.13
  1.4 7.7 %copy-start.9 = (s32[512]{0:T(512)S(1)}, s32[512]{0:T(512)}, u32[]{:S(2)}) copy-start(s32[512]{0:T(512)} %slot_ref.3) | copy-start | bytes 6148
  1.4 7.7 %copy-start.23 = (s32[512]{0:T(512)S(1)}, s32[512]{0:T(512)}, u32[]{:S(2)}) copy-start(s32[512]{0:T(512)} %param.25) | copy-start | bytes 6148
  1.4 7.9 %copy-start.22 = (f32[8,64]{1,0:T(8,128)S(1)}, f32[8,64]{1,0:T(8,128)}, u32[]{:S(2)}) copy-start(f32[8,64]{1,0:T(8,128)} %param.39) | copy-start | bytes 6148
  1.4 8.0 %copy-start.21 = (f32[8,16]{1,0:T(8,128)S(1)}, f32[8,16]{1,0:T(8,128)}, u32[]{:S(2)}) copy-start(f32[8,16]{1,0:T(8,128)} %param.40) | copy-start | bytes 1540
  2.0 8.7 %all-to-all-start = ((bf16[4,4,16,128]{3,2,1,0:T(8,128)(2,1)}), bf16[4,4,16,128]{3,2,1,0:T(8,128)(2,1)S(1)}, u32[]{:S(2)}, u32[]{:S(2)}) async-start(bf16[4,4,16,128]{3,2,1,0:T(8,128)(2,1)} %fan.1), calls=%async_computation | async-start | bytes 131072 | tf_op jit(solution)/shard_map/all_to_all | solution.py:67
  10.8 27.6 %copy-start = (bf16[3,512,512]{2,1,0:T(8,128)(2,1)S(1)}, bf16[3,512,512]{2,1,0:T(8,128)(2,1)}, u32[]{:S(2)}) copy-start(bf16[3,512,512]{2,1,0:T(8,128)(2,1)} %proj_ref.1) | copy-start | bytes 4718596
  10.8 27.6 %copy-start.2 = (bf16[512,512]{1,0:T(8,128)(2,1)S(1)}, bf16[512,512]{1,0:T(8,128)(2,1)}, u32[]{:S(2)}) copy-start(bf16[512,512]{1,0:T(8,128)(2,1)} %constant.31.clone.spread_ref) | copy-start | bytes 1572868
  10.8 27.6 %copy-start.3 = (bf16[512,96]{0,1:T(8,128)(2,1)S(1)}, bf16[512,96]{0,1:T(8,128)(2,1)}, u32[]{:S(2)}) copy-start(bf16[512,96]{0,1:T(8,128)(2,1)} %param.31) | copy-start | bytes 294916
  10.8 27.6 %copy-start.4 = (bf16[512,96]{0,1:T(8,128)(2,1)S(1)}, bf16[512,96]{0,1:T(8,128)(2,1)}, u32[]{:S(2)}) copy-start(bf16[512,96]{0,1:T(8,128)(2,1)} %param.34) | copy-start | bytes 294916
  10.8 27.6 %copy-start.6 = (f32[16,512]{1,0:T(8,128)S(1)}, f32[16,512]{1,0:T(8,128)}, u32[]{:S(2)}) copy-start(f32[16,512]{1,0:T(8,128)} %shift_ref.1) | copy-start | bytes 98308
  10.8 27.6 %copy-start.8 = (f32[5,512]{1,0:T(8,128)S(1)}, f32[5,512]{1,0:T(8,128)}, u32[]{:S(2)}) copy-start(f32[5,512]{1,0:T(8,128)} %blend_ref.1) | copy-start | bytes 30724
  38.5 15.7 %copy-start.10 = (f32[16,8,1024]{2,1,0:T(8,128)S(1)}, f32[16,8,1024]{2,1,0:T(8,128)}, u32[]{:S(2)}) copy-start(f32[16,8,1024]{2,1,0:T(8,128)} %param.27) | copy-start | bytes 1572868
  38.5 15.7 %copy-start.11 = (bf16[96,512]{1,0:T(8,128)(2,1)S(1)}, bf16[96,512]{1,0:T(8,128)(2,1)}, u32[]{:S(2)}) copy-start(bf16[96,512]{1,0:T(8,128)(2,1)} %decay_ref.1) | copy-start | bytes 294916
  38.5 15.7 %copy-start.12 = (bf16[96,512]{1,0:T(8,128)(2,1)S(1)}, bf16[96,512]{1,0:T(8,128)(2,1)}, u32[]{:S(2)}) copy-start(bf16[96,512]{1,0:T(8,128)(2,1)} %learn_ref.1) | copy-start | bytes 294916
  38.5 15.7 %copy-start.14 = (f32[512]{0:T(512)S(1)}, f32[512]{0:T(512)}, u32[]{:S(2)}) copy-start(f32[512]{0:T(512)} %param.33) | copy-start | bytes 6148
  38.5 15.7 %copy-start.15 = (f32[512]{0:T(512)S(1)}, f32[512]{0:T(512)}, u32[]{:S(2)}) copy-start(f32[512]{0:T(512)} %param.36) | copy-start | bytes 6148
  38.5 15.7 %copy-start.16 = (f32[512]{0:T(512)S(1)}, f32[512]{0:T(512)}, u32[]{:S(2)}) copy-start(f32[512]{0:T(512)} %param.37) | copy-start | bytes 6148
  38.5 15.7 %copy-start.17 = (f32[512]{0:T(512)S(1)}, f32[512]{0:T(512)}, u32[]{:S(2)}) copy-start(f32[512]{0:T(512)} %param.38) | copy-start | bytes 6148
  38.6 15.7 %copy-start.18 = (bf16[512,128]{1,0:T(8,128)(2,1)S(1)}, bf16[512,128]{1,0:T(8,128)(2,1)}, u32[]{:S(2)}) copy-start(bf16[512,128]{1,0:T(8,128)(2,1)} %constant.29.clone.head_to_lanes_ref) | copy-start | bytes 393220
  38.6 15.6 %copy-start.19 = (bf16[256,256]{1,0:T(8,128)(2,1)S(1)}, bf16[256,256]{1,0:T(8,128)(2,1)}, u32[]{:S(2)}) copy-start(bf16[256,256]{1,0:T(8,128)(2,1)} %constant.27.clone.halves_ref) | copy-start | bytes 393220
  38.6 15.6 %copy-start.20 = (bf16[128,128]{1,0:T(8,128)(2,1)S(1)}, bf16[128,128]{1,0:T(8,128)(2,1)}, u32[]{:S(2)}) copy-start(bf16[128,128]{1,0:T(8,128)(2,1)} %constant.28.clone.same_head_ref) | copy-start | bytes 98308
  54.1 9.1 %copy-start.5 = (bf16[128,256]{1,0:T(8,128)(2,1)S(1)}, bf16[128,256]{1,0:T(8,128)(2,1)}, u32[]{:S(2)}) copy-start(bf16[128,256]{1,0:T(8,128)(2,1)} %constant.32.clone.unpack_ref) | copy-start | bytes 196612
  54.1 9.1 %copy-start.7 = (bf16[128,128]{1,0:T(8,128)(2,1)S(1)}, bf16[128,128]{1,0:T(8,128)(2,1)}, u32[]{:S(2)}) copy-start(bf16[128,128]{1,0:T(8,128)(2,1)} %constant.30.clone.to_natural_ref) | copy-start | bytes 98308
  54.2 27.0 %copy-start.1 = (bf16[8,16,2048]{2,1,0:T(8,128)(2,1)S(1)}, bf16[8,16,2048]{2,1,0:T(8,128)(2,1)}, u32[]{:S(2)}) copy-start(bf16[8,16,2048]{2,1,0:T(8,128)(2,1)} %param.41) | copy-start | bytes 1572868

commit v7 on v6

--- a/solution.py
+++ b/solution.py
@@ -22,7 +22,7 @@
 WIDTH = LEARN_AT + LANES
 F32 = jnp.float32
 BF16 = jnp.bfloat16
-FIRST_A, FIRST_B, FIRST_C, FIRST_D, FIRST_E, FIRST_F = 2, 17, 2, 2, 17, 10
+FIRST_A, FIRST_B, FIRST_C, FIRST_D, FIRST_E, FIRST_F = 2, 19, 2, 2, 17, 10
 VMEM = pl.BlockSpec(memory_space=pltpu.VMEM)
 SMEM = pl.BlockSpec(memory_space=pltpu.SMEM)
 ANY = pl.BlockSpec(memory_space=pl.ANY)
@@ -97,7 +97,7 @@
 
 
 def mix_kernel(
-    source_ref, count_ref, got_ref, shift_ref, blend_ref, proj_ref, decay_ref, learn_ref, spread_ref,
+    source_ref, count_ref, got_ref, shift_ref, blend_ref, proj_ref, decay_ref, learn_ref, value_ref,
     out_ref, new_shift_ref, tokens,
 ):
     for page in range(REQ_DEV):
@@ -116,7 +116,7 @@
             rows, weight, (((1,), (1,)), ((), ())), preferred_element_type=F32
         ).astype(BF16)
 
-    value = dot(dot(mixed(3), proj_ref[2]).astype(BF16), spread_ref[...]).astype(BF16)
+    value = dot(mixed(3), value_ref[...]).astype(BF16)
     recept = dot(mixed(0), proj_ref[0]).astype(BF16)
     key = dot(mixed(2), proj_ref[1]).astype(BF16)
     decay = low_rank(mixed(1), decay_ref[...])
@@ -251,7 +251,7 @@
         stat_ref[part] = packed
 
 
-def norm_kernel(source_ref, stat_ref, reading_ref, bonus_ref, gain_ref, unpack_ref, to_natural_ref, out_ref, rows):
+def norm_kernel(source_ref, stat_ref, reading_ref, bonus_ref, gain_ref, unpack_ref, out_ref, rows):
     lane = lax.broadcasted_iota(jnp.int32, (8, LANES), 1)
     stats = [stat_ref[part] for part in range(4)]
     mean = (stats[0] + stats[1] + stats[2] + stats[3]) * (1.0 / CHANNEL_SPAN)
@@ -269,7 +269,7 @@
     opened = dot(jnp.concatenate([high, middle, low], axis=0), unpack_ref[...])
     opened = opened[0:TOK] + opened[TOK:2 * TOK] + opened[2 * TOK:3 * TOK]
     normed = (reading_ref[...] - opened[:, 0:LANES]) * opened[:, LANES:256] * gain_ref[...] + bonus_ref[...]
-    rows[...] = dot(normed.astype(BF16), to_natural_ref[...])
+    rows[...] = normed
     for page in range(REQ_DEV):
         out_ref[source_ref[page] ^ FIRST_E] = rows[pl.ds(page, TS, stride=REQ_DEV), :].astype(BF16)
 
@@ -338,8 +338,12 @@
         out_spec=ANY,
     )
     mine = exchange(everywhere, "head", FIRST_A).reshape(REQ_DEV, 16, LANES)
-    mine, source, count, count_wide, gain, reward = lax.optimization_barrier(
-        (mine, source, count, count_wide, gain, reward)
+    value_projector = dot(first_projectors[2], spread_values).astype(BF16)
+    output_projector = dot(to_natural, final_projector.reshape(VALS, 4 * FEATS)).astype(BF16)
+    mine, source, count, count_wide, gain, reward, value_projector, output_projector = (
+        lax.optimization_barrier(
+            (mine, source, count, count_wide, gain, reward, value_projector, output_projector)
+        )
     )
     packed = call(
         pack_kernel,
@@ -356,7 +360,7 @@
         [SMEM] * 2 + [VMEM] * 7,
         (
             source, count, got, prior_activation_sheets, blend_fractions, first_projectors,
-            fading_narrow_projector.T, context_step_narrowing.T, spread_values,
+            fading_narrow_projector.T, context_step_narrowing.T, value_projector,
         ),
         scratch=[pltpu.VMEM((4, TOK, LANES), F32)],
         flops=2 * TOK * FEATS * (3 * FEATS + 192),
@@ -397,8 +401,8 @@
     leaving = call(
         norm_kernel,
         [shaped((groups, TS, LANES), BF16)],
-        [SMEM] + [VMEM] * 6,
-        (source, stats, reading, bonus, gain, unpack, to_natural),
+        [SMEM] + [VMEM] * 5,
+        (source, stats, reading, bonus, gain, unpack),
         scratch=[pltpu.VMEM((TOK, LANES), F32)],
         name="norm",
     )
@@ -407,7 +411,7 @@
         output_kernel,
         [shaped((16, 16, FEATS), BF16)],
         [SMEM, SMEM, VMEM, VMEM],
-        (caller_sheet_slot, first, back, final_projector.reshape(VALS, 4 * FEATS)),
+        (caller_sheet_slot, first, back, output_projector),
         scratch=[pltpu.VMEM((TOK, LANES), F32)],
         flops=2 * TOK * VALS * 4 * FEATS,
         name="output",

time: 95.2 us -> 94.8 us (level)
  matrix products: 0 us -> 1.77 us
  waiting for transfers between devices: 1.16 us -> 0.01 us
    dot_general x0 -> x2, matrix products: none -> 1.77 us  [dot(): return jnp.dot(a, b, preferred_element_type=F32)]
    all_to_all x1, waiting for transfers between devices: 1.16 us -> 0.01 us  [exchange(): return lax.all_to_all(x, axes, 0, 0, tiled=True, axis_index_groups=order)]
    all_to_all x5, blocking collectives: 75.8 us -> 74.9 us  [exchange(): return lax.all_to_all(x, axes, 0, 0, tiled=True, axis_index_groups=order)]
  transfers between devices with their start and end apart: 1 -> 1, of which waited for: 1 -> 0; matrix products, arithmetic and copies ran while one was open for 1% -> 2% of each run, Pallas kernels for 0% -> 0%
where the time goes in v7:
time: 94.8 us; the launch traced here: 94.3 us
  blocking collectives  74.9 us (79%)
  Pallas kernels  7.47 us (8%)
  starting transfers between devices  7.14 us (8%)
  local copies, waits for them, and re-layouts  1.9 us (2%)
  matrix products  1.77 us (2%)
    all_to_all x5, blocking collectives, exchange(): return lax.all_to_all(x, axes, 0, 0, tiled=True, axis_index_groups=order)  74.9 us
    pallas_call x6, Pallas kernels, call(): pl.pallas_call(kernel, out_shape=outs[0] if single else outs, in_specs=in...  7.47 us
    all_to_all x1, starting transfers between devices, exchange(): return lax.all_to_all(x, axes, 0, 0, tiled=True, axis_index_groups=order)  7.14 us
  transfers between devices with their start and end apart: 1, of which 0 were waited for; matrix products, arithmetic and copies ran while one was open for 2% of the time, Pallas kernels for 0%

profile of v7, /device:TPU:1, one launch (start us, length us, event | category | flops | bytes accessed | tf_op | source)
XLA Modules:
  0.0 94.3 jit_solution(8445028881242315734)
XLA Ops:
  0.6 0.0 copy-start
  0.6 0.0 copy-start.11
  0.7 0.8 copy-done.11
  1.4 0.0 copy-start.19
  1.4 0.0 copy-start.1
  1.4 0.7 fan.1
  2.1 0.0 copy-start.7
  2.1 0.0 copy-start.22
  2.1 0.0 copy-start.21
  2.1 0.0 copy-start.20
  2.1 7.1 %all-to-all-start = ((bf16[4,4,16,128]{3,2,1,0:T(8,128)(2,1)}), bf16[4,4,16,128]{3,2,1,0:T(8,128)(2,1)S(1)}, u32[]{:S(2)}, u32[]{:S(2)}) async-start(bf16[4,4,16,128]{3,2,1,0:T(8,128)(2,1)} %fan.1), calls=%async_computation | async-start | bytes 131072 | tf_op jit(solution)/shard_map/all_to_all | solution.py:67
  9.3 0.0 copy-done
  9.3 0.0 copy-done.19
  9.3 0.3 convolution_convert_fusion.proj_ref
  9.6 0.0 copy-done.1
  9.6 1.5 %fusion.value_ref = bf16[512,512]{1,0:T(8,128)(2,1)S(1)} fusion(bf16[512,512]{1,0:T(8,128)(2,1)} %constant.31.clone, bf16[3,512,512]{2,1,0:T(8,128)(2,1)S(1)} %copy-done.1), kind=kOutput, calls=%fused_computation.2 | convolution fusion | flops 268697600 | bytes 1572864 | tf_op jit(solution)/shard_map/dot_general | solution.py:56
  11.1 0.0 copy-done.7
  11.1 0.0 copy-done.22
  11.1 0.2 fusion.4
  11.3 0.0 copy-done.21
  11.3 0.1 reshape.58.reward_ref
  11.4 0.0 copy-done.20
  11.4 0.1 copy.32
  11.5 0.1 copy.33
  11.5 0.1 reshape.57.gain_ref
  11.6 0.0 all-to-all-done
  11.6 0.1 broadcast_in_dim.47.count_ref
  11.7 0.0 copy-start.2
  11.7 0.7 pack.1
  12.4 25.6 %all_to_all.30.got_ref = bf16[32,16,128]{2,1,0:T(8,128)(2,1)S(1)} all-to-all(bf16[32,16,128]{2,1,0:T(8,128)(2,1)S(1)} %pack.1), channel_id=1, replica_groups={{304,288,272,256,368,352,336,320,432,416,400,384,496,480,464,448,48,32,..., dimensions={0} | all-to-all | bytes 262144 | tf_op jit(solution)/shard_map/all_to_all | solution.py:67
  38.0 0.0 copy-done.2
  38.0 0.0 copy-done.3
  38.0 0.0 copy-done.5
  38.0 0.0 copy-done.6
  38.0 0.0 copy-start.8
  38.0 0.0 copy-start.9
  38.0 0.0 copy-start.10
  38.0 0.0 copy-start.12
  38.0 0.0 copy-start.13
  38.1 0.0 copy-start.14
  38.1 0.0 copy-start.15
  38.1 0.0 copy-start.16
  38.1 0.0 copy-start.17
  38.1 0.0 copy-start.18
  38.1 1.6 %mix.1 = (bf16[4,64,1408]{2,1,0:T(8,128)(2,1)S(1)}, f32[16,512]{1,0:T(8,128)}) custom-call(s32[16]{0:T(128)S(1)} %get-tuple-element.17.source_ref, s32[16]{0:T(128)S(1)} %get-tuple-element.19.count_ref, bf16[32,16,128]{2,1,0:T(8,128)(2,1)S(1)} %all_to_all.30.got_ref, f32[16,512]{1,0:T(8,128)S(1)} %copy-done.5, f32[5,512]{1,0:T(8,128)S(1)} %copy-done.6, ...), custom_call_target="tpu_custom_call" | custom-call | flops 113246208 | bytes 3221632 | tf_op jit(solution)/shard_map/mix/pallas_call | solution.py:74
  39.7 13.0 %all_to_all.31.got_ref = bf16[4,64,1408]{2,1,0:T(8,128)(2,1)S(1)} all-to-all(bf16[4,64,1408]{2,1,0:T(8,128)(2,1)S(1)} %get-tuple-element.22), channel_id=1, replica_groups={{2,3,0,1},{6,7,4,5},{10,11,8,9},{14,15,12,13},{18,19,16,17},{22,23,20,2..., dimensions={0} | all-to-all | bytes 1441792 | tf_op jit(solution)/shard_map/all_to_all | solution.py:67
  52.7 0.0 copy-done.8
  52.7 0.0 copy-done.9
  52.7 0.0 copy-done.10
  52.7 0.0 copy-done.12
  52.7 0.0 copy-done.13
  52.8 0.0 copy-done.14
  52.8 0.0 copy-done.15
  52.8 0.0 copy-done.16
  52.8 0.0 copy-done.17
  52.8 0.0 copy-done.18
  52.8 2.9 %state.1 = (f32[1024,128]{1,0:T(8,128)}, f32[64,128]{1,0:T(8,128)S(1)}, f32[64,128]{1,0:T(8,128)S(1)}, f32[4,8,128]{2,1,0:T(8,128)S(1)}) custom-call(s32[16,128]{1,0:T(8,128)S(1)} %broadcast_in_dim.47.count_ref, bf16[4,64,1408]{2,1,0:T(8,128)(2,1)S(1)} %all_to_all.31.got_ref, f32[1024,128]{1,0:T(8,128)S(1)} %bitcast.39, bf16[96,512]{1,0:T(8,128)(2,1)S(1)} %copy-done.9, ...), custom_call_target="tpu_custom_call" | custom-call | flops 805306368 | bytes 2361344 | tf_op jit(solution)/shard_map/state/pallas_call | solution.py:74
  55.7 6.2 %all_to_all.32.stat_ref = f32[4,8,128]{2,1,0:T(8,128)S(1)} all-to-all(f32[4,8,128]{2,1,0:T(8,128)S(1)} %get-tuple-element.24), channel_id=1, replica_groups={{2,3,0,1},{6,7,4,5},{10,11,8,9},{14,15,12,13},{18,19,16,17},{22,23,20,2..., dimensions={0} | all-to-all | bytes 32768 | tf_op jit(solution)/shard_map/all_to_all | solution.py:67
  61.8 0.0 copy-done.4
  61.8 0.9 norm.1
  62.7 18.1 %all_to_all.33.got_ref = bf16[32,4,128]{2,1,0:T(4,128)(2,1)S(1)} all-to-all(bf16[32,4,128]{2,1,0:T(4,128)(2,1)S(1)} %norm.1), channel_id=1, replica_groups={{272,256,304,288,336,320,368,352,400,384,432,416,464,448,496,480,16,0,4..., dimensions={0} | all-to-all | bytes 65536 | tf_op jit(solution)/shard_map/all_to_all | solution.py:67
  80.8 0.8 output.1
  81.7 12.0 %all_to_all.34 = bf16[16,16,512]{2,1,0:T(8,128)(2,1)S(1)} all-to-all(bf16[16,16,512]{2,1,0:T(8,128)(2,1)S(1)} %output.1), channel_id=1, replica_groups={{10,11,8,9,14,15,12,13,2,3,0,1,6,7,4,5},{26,27,24,25,30,31,28,29,18,19,..., dimensions={0} | all-to-all | bytes 524288 | tf_op jit(solution)/shard_map/all_to_all | solution.py:67
  93.7 0.6 reshape.62
  (7 shorter events, 0.1 us)
Async XLA Ops:
  0.6 8.7 %copy-start = (bf16[8,16,2048]{2,1,0:T(8,128)(2,1)S(1)}, bf16[8,16,2048]{2,1,0:T(8,128)(2,1)}, u32[]{:S(2)}) copy-start(bf16[8,16,2048]{2,1,0:T(8,128)(2,1)} %param.41) | copy-start | bytes 1572868
  0.6 0.8 copy-start.11
  1.4 7.9 %copy-start.19 = (bf16[128,128]{1,0:T(8,128)(2,1)S(1)}, bf16[128,128]{1,0:T(8,128)(2,1)}, u32[]{:S(2)}) copy-start(bf16[128,128]{1,0:T(8,128)(2,1)} %constant.30.clone) | copy-start | bytes 98308
  1.4 8.2 %copy-start.1 = (bf16[3,512,512]{2,1,0:T(8,128)(2,1)S(1)}, bf16[3,512,512]{2,1,0:T(8,128)(2,1)}, u32[]{:S(2)}) copy-start(bf16[3,512,512]{2,1,0:T(8,128)(2,1)} %proj_ref.1) | copy-start | bytes 4718596
  2.1 9.0 %copy-start.7 = (s32[512]{0:T(512)S(1)}, s32[512]{0:T(512)}, u32[]{:S(2)}) copy-start(s32[512]{0:T(512)} %slot_ref.3) | copy-start | bytes 6148
  2.1 9.0 %copy-start.22 = (s32[512]{0:T(512)S(1)}, s32[512]{0:T(512)}, u32[]{:S(2)}) copy-start(s32[512]{0:T(512)} %param.25) | copy-start | bytes 6148
  2.1 9.2 %copy-start.21 = (f32[8,64]{1,0:T(8,128)S(1)}, f32[8,64]{1,0:T(8,128)}, u32[]{:S(2)}) copy-start(f32[8,64]{1,0:T(8,128)} %param.39) | copy-start | bytes 6148
  2.1 9.3 %copy-start.20 = (f32[8,16]{1,0:T(8,128)S(1)}, f32[8,16]{1,0:T(8,128)}, u32[]{:S(2)}) copy-start(f32[8,16]{1,0:T(8,128)} %param.40) | copy-start | bytes 1540
  2.1 9.5 %all-to-all-start = ((bf16[4,4,16,128]{3,2,1,0:T(8,128)(2,1)}), bf16[4,4,16,128]{3,2,1,0:T(8,128)(2,1)S(1)}, u32[]{:S(2)}, u32[]{:S(2)}) async-start(bf16[4,4,16,128]{3,2,1,0:T(8,128)(2,1)} %fan.1), calls=%async_computation | async-start | bytes 131072 | tf_op jit(solution)/shard_map/all_to_all | solution.py:67
  11.7 26.3 %copy-start.2 = (bf16[512,96]{0,1:T(8,128)(2,1)S(1)}, bf16[512,96]{0,1:T(8,128)(2,1)}, u32[]{:S(2)}) copy-start(bf16[512,96]{0,1:T(8,128)(2,1)} %param.31) | copy-start | bytes 294916
  11.7 26.3 %copy-start.3 = (bf16[512,96]{0,1:T(8,128)(2,1)S(1)}, bf16[512,96]{0,1:T(8,128)(2,1)}, u32[]{:S(2)}) copy-start(bf16[512,96]{0,1:T(8,128)(2,1)} %param.34) | copy-start | bytes 294916
  11.7 26.3 %copy-start.5 = (f32[16,512]{1,0:T(8,128)S(1)}, f32[16,512]{1,0:T(8,128)}, u32[]{:S(2)}) copy-start(f32[16,512]{1,0:T(8,128)} %shift_ref.1) | copy-start | bytes 98308
  11.7 26.3 %copy-start.6 = (f32[5,512]{1,0:T(8,128)S(1)}, f32[5,512]{1,0:T(8,128)}, u32[]{:S(2)}) copy-start(f32[5,512]{1,0:T(8,128)} %blend_ref.1) | copy-start | bytes 30724
  38.0 14.7 %copy-start.8 = (f32[16,8,1024]{2,1,0:T(8,128)S(1)}, f32[16,8,1024]{2,1,0:T(8,128)}, u32[]{:S(2)}) copy-start(f32[16,8,1024]{2,1,0:T(8,128)} %param.27) | copy-start | bytes 1572868
  38.0 14.7 %copy-start.9 = (bf16[96,512]{1,0:T(8,128)(2,1)S(1)}, bf16[96,512]{1,0:T(8,128)(2,1)}, u32[]{:S(2)}) copy-start(bf16[96,512]{1,0:T(8,128)(2,1)} %decay_ref.1) | copy-start | bytes 294916
  38.0 14.7 %copy-start.10 = (bf16[96,512]{1,0:T(8,128)(2,1)S(1)}, bf16[96,512]{1,0:T(8,128)(2,1)}, u32[]{:S(2)}) copy-start(bf16[96,512]{1,0:T(8,128)(2,1)} %learn_ref.1) | copy-start | bytes 294916
  38.0 14.7 %copy-start.12 = (f32[512]{0:T(512)S(1)}, f32[512]{0:T(512)}, u32[]{:S(2)}) copy-start(f32[512]{0:T(512)} %param.33) | copy-start | bytes 6148
  38.0 14.7 %copy-start.13 = (f32[512]{0:T(512)S(1)}, f32[512]{0:T(512)}, u32[]{:S(2)}) copy-start(f32[512]{0:T(512)} %param.36) | copy-start | bytes 6148
  38.1 14.7 %copy-start.14 = (f32[512]{0:T(512)S(1)}, f32[512]{0:T(512)}, u32[]{:S(2)}) copy-start(f32[512]{0:T(512)} %param.37) | copy-start | bytes 6148
  38.1 14.7 %copy-start.15 = (f32[512]{0:T(512)S(1)}, f32[512]{0:T(512)}, u32[]{:S(2)}) copy-start(f32[512]{0:T(512)} %param.38) | copy-start | bytes 6148
  38.1 14.7 %copy-start.16 = (bf16[512,128]{1,0:T(8,128)(2,1)S(1)}, bf16[512,128]{1,0:T(8,128)(2,1)}, u32[]{:S(2)}) copy-start(bf16[512,128]{1,0:T(8,128)(2,1)} %constant.29.clone.head_to_lanes_ref) | copy-start | bytes 393220
  38.1 14.7 %copy-start.17 = (bf16[256,256]{1,0:T(8,128)(2,1)S(1)}, bf16[256,256]{1,0:T(8,128)(2,1)}, u32[]{:S(2)}) copy-start(bf16[256,256]{1,0:T(8,128)(2,1)} %constant.27.clone.halves_ref) | copy-start | bytes 393220
  38.1 14.7 %copy-start.18 = (bf16[128,128]{1,0:T(8,128)(2,1)S(1)}, bf16[128,128]{1,0:T(8,128)(2,1)}, u32[]{:S(2)}) copy-start(bf16[128,128]{1,0:T(8,128)(2,1)} %constant.28.clone.same_head_ref) | copy-start | bytes 98308
  52.7 9.1 %copy-start.4 = (bf16[128,256]{1,0:T(8,128)(2,1)S(1)}, bf16[128,256]{1,0:T(8,128)(2,1)}, u32[]{:S(2)}) copy-start(bf16[128,256]{1,0:T(8,128)(2,1)} %constant.32.clone.unpack_ref) | copy-start | bytes 196612

commit v8 on v7

--- a/solution.py
+++ b/solution.py
@@ -135,13 +135,7 @@
             new_shift_ref[page:page + 1, part * LANES:(part + 1) * LANES] = tokens[part, pl.ds(row, 1), :]
 
 
-def state_kernel(
-    count_ref, got_ref, state_ref, decay_ref, decay_offset_ref, learn_ref, learn_offset_ref, gain_ref,
-    correction_ref, reward_ref, halves_ref, same_head_ref, head_to_lanes_ref,
-    new_state_ref, reading_ref, bonus_ref, stat_ref, spread, states, factors,
-):
-    lane = lax.broadcasted_iota(jnp.int32, (REQ_DEV, 256), 1)
-    lane_key = lane % 64 - lane // 128
+def order_kernel(state_ref, states):
     for head in range(HEADS):
         for quad in range(4):
             at = (head * 4 + quad) * REQ_DEV
@@ -151,6 +145,15 @@
                     states[at + group * 8:at + group * 8 + 8, half * LANES:(half + 1) * LANES] = (
                         state_ref[pl.ds(start, 8, stride=64), :]
                     )
+
+
+def state_kernel(
+    count_ref, got_ref, state_ref, decay_ref, decay_offset_ref, learn_ref, learn_offset_ref, gain_ref,
+    correction_ref, reward_ref, halves_ref, same_head_ref, head_to_lanes_ref,
+    new_state_ref, reading_ref, bonus_ref, stat_ref, spread, states, factors,
+):
+    lane = lax.broadcasted_iota(jnp.int32, (REQ_DEV, 256), 1)
+    lane_key = lane % 64 - lane // 128
     total = got_ref[0].astype(F32)
     for part in range(1, 4):
         total = total + got_ref[part].astype(F32)
@@ -196,7 +199,7 @@
     for t in range(TS + 1):
         for head in range(HEADS):
             place = slice(head * 64, (head + 1) * 64)
-            state = states[place, :]
+            state = states[place, :] if t > 0 else state_ref[place, :]
             if t > 0:
                 removed = product[head * 64:(head + 1) * 64]
                 added = product[512 + head * 64:512 + (head + 1) * 64]
@@ -218,6 +221,8 @@
                                 ]
                 query = (state * vector_at(4, head, t - 1)).astype(BF16)
                 factors[1024 + head * 64:1024 + (head + 1) * 64, :] = query
+            else:
+                states[place, :] = state
             if t < TS:
                 factors[place, :] = (state * vector_at(0, head, t)).astype(BF16)
                 now = value_pair[t * REQ_DEV:(t + 1) * REQ_DEV]
@@ -338,11 +343,14 @@
         out_spec=ANY,
     )
     mine = exchange(everywhere, "head", FIRST_A).reshape(REQ_DEV, 16, LANES)
+    sheets = memory_sheets.reshape(REQ_DEV, HEADS, 8, LANES).transpose(0, 2, 1, 3)
+    sheets = sheets.reshape(REQ_DEV * HEADS * 8, LANES)
+    sheets = call(order_kernel, [shaped((512, 256), F32)], [VMEM], (sheets,), name="order")
     value_projector = dot(first_projectors[2], spread_values).astype(BF16)
     output_projector = dot(to_natural, final_projector.reshape(VALS, 4 * FEATS)).astype(BF16)
-    mine, source, count, count_wide, gain, reward, value_projector, output_projector = (
+    mine, source, count, count_wide, gain, reward, value_projector, output_projector, sheets = (
         lax.optimization_barrier(
-            (mine, source, count, count_wide, gain, reward, value_projector, output_projector)
+            (mine, source, count, count_wide, gain, reward, value_projector, output_projector, sheets)
         )
     )
     packed = call(
@@ -366,8 +374,6 @@
         flops=2 * TOK * FEATS * (3 * FEATS + 192),
         name="mix",
     )
-    sheets = memory_sheets.reshape(REQ_DEV, HEADS, 8, LANES).transpose(0, 2, 1, 3)
-    sheets = sheets.reshape(REQ_DEV * HEADS * 8, LANES)
     sums = exchange(partial, "row", FIRST_C)
     new_state, reading, bonus, stat = call(
         state_kernel,

time: 94.8 us -> 95.5 us (level)
  blocking collectives: 74.9 us -> 73.8 us
    all_to_all x5, blocking collectives: 74.9 us -> 73.8 us  [exchange(): return lax.all_to_all(x, axes, 0, 0, tiled=True, axis_index_groups=order)]
    pallas_call x6 -> x7, Pallas kernels: 7.47 us -> 7.61 us  [call(): pl.pallas_call(kernel, out_shape=outs[0] if single else outs, in_specs=in...]
  transfers between devices with their start and end apart: 1 -> 1, of which waited for: 0 -> 0; matrix products, arithmetic and copies ran while one was open for 2% -> 3% of each run, Pallas kernels for 0% -> 0%
where the time goes in v8:
time: 95.5 us; the launch traced here: 95 us
  blocking collectives  73.8 us (77%)
  Pallas kernels  7.61 us (8%)
  starting transfers between devices  7.14 us (7%)
  local copies, waits for them, and re-layouts  2.71 us (3%)
  matrix products  2.56 us (3%)
  between operations  0.96 us (1%)
    all_to_all x5, blocking collectives, exchange(): return lax.all_to_all(x, axes, 0, 0, tiled=True, axis_index_groups=order)  73.8 us
    pallas_call x7, Pallas kernels, call(): pl.pallas_call(kernel, out_shape=outs[0] if single else outs, in_specs=in...  7.61 us
    all_to_all x1, starting transfers between devices, exchange(): return lax.all_to_all(x, axes, 0, 0, tiled=True, axis_index_groups=order)  7.14 us
    dot_general x2, matrix products, dot(): return jnp.dot(a, b, preferred_element_type=F32)  2.56 us
  transfers between devices with their start and end apart: 1, of which 0 were waited for; matrix products, arithmetic and copies ran while one was open for 3% of the time, Pallas kernels for 0%

profile of v8, /device:TPU:1, one launch (start us, length us, event | category | flops | bytes accessed | tf_op | source)
XLA Modules:
  0.0 95.0 jit_solution(1868659770755117113)
XLA Ops:
  0.6 0.0 copy-start
  0.6 0.0 copy-start.14
  0.7 0.8 copy-done.14
  1.4 0.7 fan.1
  2.1 0.0 copy-start.11
  2.1 0.0 copy-start.25
  2.1 0.0 copy-start.24
  2.1 0.0 copy-start.23
  2.1 0.0 copy-start.2
  2.2 7.1 %all-to-all-start = ((bf16[4,4,16,128]{3,2,1,0:T(8,128)(2,1)}), bf16[4,4,16,128]{3,2,1,0:T(8,128)(2,1)S(1)}, u32[]{:S(2)}, u32[]{:S(2)}) async-start(bf16[4,4,16,128]{3,2,1,0:T(8,128)(2,1)} %fan.1), calls=%async_computation | async-start | bytes 131072 | tf_op jit(solution)/shard_map/all_to_all | solution.py:67
  9.3 0.0 copy-done
  9.3 0.0 copy-done.22
  9.3 0.3 convolution_convert_fusion.proj_ref
  9.6 0.0 copy-done.1
  9.6 2.3 %fusion.value_ref = bf16[512,512]{1,0:T(8,128)(2,1)} fusion(bf16[512,512]{1,0:T(8,128)(2,1)} %constant.31.clone, bf16[3,512,512]{2,1,0:T(8,128)(2,1)S(1)} %copy-done.1), kind=kOutput, calls=%fused_computation.2 | convolution fusion | flops 268697600 | bytes 1572864 | tf_op jit(solution)/shard_map/dot_general | solution.py:56
  11.9 0.0 copy-done.11
  11.9 0.0 copy-done.25
  11.9 0.2 fusion.4
  12.1 0.0 copy-done.24
  12.1 0.1 reshape.58.reward_ref
  12.2 0.0 copy-done.23
  12.2 0.1 copy.32
  12.2 0.1 copy.33
  12.3 0.1 reshape.57.gain_ref
  12.4 0.0 copy-done.2
  12.4 0.3 order.1.state_ref
  12.7 0.0 copy-start.3
  12.8 0.8 copy-done.3
  13.5 0.0 all-to-all-done
  13.6 0.1 broadcast_in_dim.47.count_ref
  13.6 0.0 copy-start.10
  13.6 0.7 pack.1
  14.3 25.5 %all_to_all.30.got_ref = bf16[32,16,128]{2,1,0:T(8,128)(2,1)S(1)} all-to-all(bf16[32,16,128]{2,1,0:T(8,128)(2,1)S(1)} %pack.1), channel_id=1, replica_groups={{304,288,272,256,368,352,336,320,432,416,400,384,496,480,464,448,48,32,..., dimensions={0} | all-to-all | bytes 262144 | tf_op jit(solution)/shard_map/all_to_all | solution.py:67
  39.8 0.0 copy-done.5
  39.8 0.0 copy-done.6
  39.8 0.0 copy-done.7
  39.8 0.0 copy-done.9
  39.8 0.0 copy-done.10
  39.8 0.0 copy-start.12
  39.8 0.0 copy-start.13
  39.8 0.0 copy-start.15
  39.9 0.0 copy-start.16
  39.9 0.0 copy-start.17
  39.9 0.0 copy-start.18
  39.9 0.0 copy-start.19
  39.9 0.0 copy-start.20
  39.9 0.0 copy-start.21
  39.9 1.6 %mix.1 = (bf16[4,64,1408]{2,1,0:T(8,128)(2,1)S(1)}, f32[16,512]{1,0:T(8,128)}) custom-call(s32[16]{0:T(128)S(1)} %get-tuple-element.18.source_ref, s32[16]{0:T(128)S(1)} %get-tuple-element.20.count_ref, bf16[32,16,128]{2,1,0:T(8,128)(2,1)S(1)} %all_to_all.30.got_ref, f32[16,512]{1,0:T(8,128)S(1)} %copy-done.9, f32[5,512]{1,0:T(8,128)S(1)} %copy-done.10, ...), custom_call_target="tpu_custom_call" | custom-call | flops 113246208 | bytes 3221632 | tf_op jit(solution)/shard_map/mix/pallas_call | solution.py:74
  41.5 13.0 %all_to_all.31.got_ref = bf16[4,64,1408]{2,1,0:T(8,128)(2,1)S(1)} all-to-all(bf16[4,64,1408]{2,1,0:T(8,128)(2,1)S(1)} %get-tuple-element.23), channel_id=1, replica_groups={{2,3,0,1},{6,7,4,5},{10,11,8,9},{14,15,12,13},{18,19,16,17},{22,23,20,2..., dimensions={0} | all-to-all | bytes 1441792 | tf_op jit(solution)/shard_map/all_to_all | solution.py:67
  54.5 0.0 copy-done.12
  54.6 0.0 copy-done.15
  54.6 0.0 copy-done.16
  54.6 0.0 copy-done.17
  54.6 0.0 copy-done.18
  54.6 0.0 copy-done.19
  54.6 0.0 copy-done.20
  54.6 0.0 copy-done.21
  54.6 2.7 %state.1 = (f32[1024,128]{1,0:T(8,128)}, f32[64,128]{1,0:T(8,128)S(1)}, f32[64,128]{1,0:T(8,128)S(1)}, f32[4,8,128]{2,1,0:T(8,128)S(1)}) custom-call(s32[16,128]{1,0:T(8,128)S(1)} %broadcast_in_dim.47.count_ref, bf16[4,64,1408]{2,1,0:T(8,128)(2,1)S(1)} %all_to_all.31.got_ref, f32[512,256]{1,0:T(8,128)S(1)} %copy-done.4, bf16[96,512]{1,0:T(8,128)(2,1)S(1)} %copy-done.12, ...), custom_call_target="tpu_custom_call" | custom-call | flops 805306368 | bytes 2361344 | tf_op jit(solution)/shard_map/state/pallas_call | solution.py:74
  57.3 6.2 %all_to_all.32.stat_ref = f32[4,8,128]{2,1,0:T(8,128)S(1)} all-to-all(f32[4,8,128]{2,1,0:T(8,128)S(1)} %get-tuple-element.26), channel_id=1, replica_groups={{2,3,0,1},{6,7,4,5},{10,11,8,9},{14,15,12,13},{18,19,16,17},{22,23,20,2..., dimensions={0} | all-to-all | bytes 32768 | tf_op jit(solution)/shard_map/all_to_all | solution.py:67
  63.5 0.9 norm.1
  64.3 18.1 %all_to_all.33.got_ref = bf16[32,4,128]{2,1,0:T(4,128)(2,1)S(1)} all-to-all(bf16[32,4,128]{2,1,0:T(4,128)(2,1)S(1)} %norm.1), channel_id=1, replica_groups={{272,256,304,288,336,320,368,352,400,384,432,416,464,448,496,480,16,0,4..., dimensions={0} | all-to-all | bytes 65536 | tf_op jit(solution)/shard_map/all_to_all | solution.py:67
  82.4 0.8 output.1
  83.3 11.1 %all_to_all.34 = bf16[16,16,512]{2,1,0:T(8,128)(2,1)S(1)} all-to-all(bf16[16,16,512]{2,1,0:T(8,128)(2,1)S(1)} %output.1), channel_id=1, replica_groups={{10,11,8,9,14,15,12,13,2,3,0,1,6,7,4,5},{26,27,24,25,30,31,28,29,18,19,..., dimensions={0} | all-to-all | bytes 524288 | tf_op jit(solution)/shard_map/all_to_all | solution.py:67
  94.4 0.6 reshape.62
  (14 shorter events, 0.1 us)
Async XLA Ops:
  0.6 8.7 %copy-start = (bf16[8,16,2048]{2,1,0:T(8,128)(2,1)S(1)}, bf16[8,16,2048]{2,1,0:T(8,128)(2,1)}, u32[]{:S(2)}) copy-start(bf16[8,16,2048]{2,1,0:T(8,128)(2,1)} %param.41) | copy-start | bytes 1572868
  0.6 0.8 copy-start.14
  1.4 7.9 %copy-start.22 = (bf16[128,128]{1,0:T(8,128)(2,1)S(1)}, bf16[128,128]{1,0:T(8,128)(2,1)}, u32[]{:S(2)}) copy-start(bf16[128,128]{1,0:T(8,128)(2,1)} %constant.30.clone) | copy-start | bytes 98308
  1.4 8.2 %copy-start.1 = (bf16[3,512,512]{2,1,0:T(8,128)(2,1)S(1)}, bf16[3,512,512]{2,1,0:T(8,128)(2,1)}, u32[]{:S(2)}) copy-start(bf16[3,512,512]{2,1,0:T(8,128)(2,1)} %proj_ref.1) | copy-start | bytes 4718596
  2.1 9.8 %copy-start.11 = (s32[512]{0:T(512)S(1)}, s32[512]{0:T(512)}, u32[]{:S(2)}) copy-start(s32[512]{0:T(512)} %slot_ref.3) | copy-start | bytes 6148
  2.1 9.8 %copy-start.25 = (s32[512]{0:T(512)S(1)}, s32[512]{0:T(512)}, u32[]{:S(2)}) copy-start(s32[512]{0:T(512)} %param.25) | copy-start | bytes 6148
  2.1 10.0 %copy-start.24 = (f32[8,64]{1,0:T(8,128)S(1)}, f32[8,64]{1,0:T(8,128)}, u32[]{:S(2)}) copy-start(f32[8,64]{1,0:T(8,128)} %param.39) | copy-start | bytes 6148
  2.1 10.0 %copy-start.23 = (f32[8,16]{1,0:T(8,128)S(1)}, f32[8,16]{1,0:T(8,128)}, u32[]{:S(2)}) copy-start(f32[8,16]{1,0:T(8,128)} %param.40) | copy-start | bytes 1540
  2.1 10.3 %copy-start.2 = (f32[16,8,1024]{2,1,0:T(8,128)S(1)}, f32[16,8,1024]{2,1,0:T(8,128)}, u32[]{:S(2)}) copy-start(f32[16,8,1024]{2,1,0:T(8,128)} %param.27) | copy-start | bytes 1572868
  2.2 11.4 %all-to-all-start = ((bf16[4,4,16,128]{3,2,1,0:T(8,128)(2,1)}), bf16[4,4,16,128]{3,2,1,0:T(8,128)(2,1)S(1)}, u32[]{:S(2)}, u32[]{:S(2)}) async-start(bf16[4,4,16,128]{3,2,1,0:T(8,128)(2,1)} %fan.1), calls=%async_computation | async-start | bytes 131072 | tf_op jit(solution)/shard_map/all_to_all | solution.py:67
  12.7 0.8 copy-start.3
  13.6 26.2 %copy-start.5 = (bf16[512,512]{1,0:T(8,128)(2,1)S(1)}, bf16[512,512]{1,0:T(8,128)(2,1)}, u32[]{:S(2)}) copy-start(bf16[512,512]{1,0:T(8,128)(2,1)} %fusion.value_ref) | copy-start | bytes 1572868
  13.6 26.2 %copy-start.6 = (bf16[512,96]{0,1:T(8,128)(2,1)S(1)}, bf16[512,96]{0,1:T(8,128)(2,1)}, u32[]{:S(2)}) copy-start(bf16[512,96]{0,1:T(8,128)(2,1)} %param.31) | copy-start | bytes 294916
  13.6 26.2 %copy-start.7 = (bf16[512,96]{0,1:T(8,128)(2,1)S(1)}, bf16[512,96]{0,1:T(8,128)(2,1)}, u32[]{:S(2)}) copy-start(bf16[512,96]{0,1:T(8,128)(2,1)} %param.34) | copy-start | bytes 294916
  13.6 26.2 %copy-start.9 = (f32[16,512]{1,0:T(8,128)S(1)}, f32[16,512]{1,0:T(8,128)}, u32[]{:S(2)}) copy-start(f32[16,512]{1,0:T(8,128)} %shift_ref.1) | copy-start | bytes 98308
  13.6 26.2 %copy-start.10 = (f32[5,512]{1,0:T(8,128)S(1)}, f32[5,512]{1,0:T(8,128)}, u32[]{:S(2)}) copy-start(f32[5,512]{1,0:T(8,128)} %blend_ref.1) | copy-start | bytes 30724
  39.8 14.7 %copy-start.4 = (f32[512,256]{1,0:T(8,128)S(1)}, f32[512,256]{1,0:T(8,128)}, u32[]{:S(2)}) copy-start(f32[512,256]{1,0:T(8,128)} %copy-done.3) | copy-start | bytes 1572868
  39.8 14.7 %copy-start.12 = (bf16[96,512]{1,0:T(8,128)(2,1)S(1)}, bf16[96,512]{1,0:T(8,128)(2,1)}, u32[]{:S(2)}) copy-start(bf16[96,512]{1,0:T(8,128)(2,1)} %decay_ref.1) | copy-start | bytes 294916
  39.8 14.7 %copy-start.13 = (bf16[96,512]{1,0:T(8,128)(2,1)S(1)}, bf16[96,512]{1,0:T(8,128)(2,1)}, u32[]{:S(2)}) copy-start(bf16[96,512]{1,0:T(8,128)(2,1)} %learn_ref.1) | copy-start | bytes 294916
  39.8 14.7 %copy-start.15 = (f32[512]{0:T(512)S(1)}, f32[512]{0:T(512)}, u32[]{:S(2)}) copy-start(f32[512]{0:T(512)} %param.33) | copy-start | bytes 6148
  39.9 14.7 %copy-start.16 = (f32[512]{0:T(512)S(1)}, f32[512]{0:T(512)}, u32[]{:S(2)}) copy-start(f32[512]{0:T(512)} %param.36) | copy-start | bytes 6148
  39.9 14.7 %copy-start.17 = (f32[512]{0:T(512)S(1)}, f32[512]{0:T(512)}, u32[]{:S(2)}) copy-start(f32[512]{0:T(512)} %param.37) | copy-start | bytes 6148
  39.9 14.7 %copy-start.18 = (f32[512]{0:T(512)S(1)}, f32[512]{0:T(512)}, u32[]{:S(2)}) copy-start(f32[512]{0:T(512)} %param.38) | copy-start | bytes 6148
  39.9 14.7 %copy-start.19 = (bf16[512,128]{1,0:T(8,128)(2,1)S(1)}, bf16[512,128]{1,0:T(8,128)(2,1)}, u32[]{:S(2)}) copy-start(bf16[512,128]{1,0:T(8,128)(2,1)} %constant.29.clone.head_to_lanes_ref) | copy-start | bytes 393220
  39.9 14.7 %copy-start.20 = (bf16[256,256]{1,0:T(8,128)(2,1)S(1)}, bf16[256,256]{1,0:T(8,128)(2,1)}, u32[]{:S(2)}) copy-start(bf16[256,256]{1,0:T(8,128)(2,1)} %constant.27.clone.halves_ref) | copy-start | bytes 393220
  39.9 14.7 %copy-start.21 = (bf16[128,128]{1,0:T(8,128)(2,1)S(1)}, bf16[128,128]{1,0:T(8,128)(2,1)}, u32[]{:S(2)}) copy-start(bf16[128,128]{1,0:T(8,128)(2,1)} %constant.28.clone.same_head_ref) | copy-start | bytes 98308
  54.5 8.9 %copy-start.8 = (bf16[128,256]{1,0:T(8,128)(2,1)S(1)}, bf16[128,256]{1,0:T(8,128)(2,1)}, u32[]{:S(2)}) copy-start(bf16[128,256]{1,0:T(8,128)(2,1)} %constant.32.clone.unpack_ref) | copy-start | bytes 196612
